TPU v7x, 32 devices: a whole 2x2x4 slice. The times are simulated.
32 devices in a mesh: groups: 2 (over x), seq: 16 (over z, y, core).
Axes of the slice: x: 2, y: 2, z: 4, core: 2. Of those that a mesh axis runs over, the one named last changes fastest.
Arguments:
- queries: bfloat16 [128, 8192], P(('groups', 'seq')), parts along dimension 0, may hold values from -15 to 15
- draft_keys: bfloat16 [128, 1024], P(('groups', 'seq')), parts along dimension 0, may hold values from -16 to 16
- draft_values: bfloat16 [128, 1024], P(('groups', 'seq')), parts along dimension 0, may hold values from -6 to 6
- parents: int32 [128], P(('groups', 'seq')), parts along dimension 0, may hold values from -1 to 2, as said below
- private_keys: bfloat16 [32, 1024, 1024], P(('groups', 'seq')), parts along dimension 0, may hold values from -8 to 8
- private_values: bfloat16 [32, 1024, 1024], P(('groups', 'seq')), parts along dimension 0, may hold values from -6 to 6
- priv_lengths: int32 [32], P(('groups', 'seq')), parts along dimension 0, may hold values from 1 to 1024, as said below
- prefix_keys: bfloat16 [32, 16384, 128], P(('groups', 'seq')), parts along dimension 0, may hold values from -8 to 8
- prefix_values: bfloat16 [32, 16384, 128], P(('groups', 'seq')), parts along dimension 0, may hold values from -6 to 6
- out_weight: bfloat16 [8192, 8192], P(None, 'seq'), may hold values from -0.0625 to 0.0625
Outputs:
- output: float32 [128, 8192], P(('groups', 'seq')), parts along dimension 0
There are 2 independent parts, one for each index of `groups`. A program takes and returns all parts, laid end to end along the dimension named above; an argument that names none is the same for every part. Nothing has to cross between parts.
Inputs may be any that keep to these rules, and one draw needn't show every extreme that they name: parents[r * 4 + i] is the draft of request r that draft i extends, always smaller than i; -1 means draft i extends the cached context directly. Request r's live private slots are its first priv_lengths[r] slots; some request has all 1024.
All inputs are finite; a program needn't handle non-finite values.
Results may differ from a plain program's by a relative error of at most 0.0034.
Values may be sent and summed in bfloat16 or wider, within the bound.
No kernel may reach another device: no remote copies, remote signals or barrier semaphores. Data moves between devices by JAX's collectives and lax.ppermute only.
A program may use at most 192 MiB of HBM per device.

v0:
```python
import jax
import jax.numpy as jnp
from jax import lax
from jax.sharding import PartitionSpec as P

HEADS = 64
KVH = 8
HD = 128
DRAFT = 4
PRIV = 1024


def from_partner(array, axis, bit):
    return lax.ppermute(array, axis, [(i, i ^ 1 << bit) for i in range(lax.axis_size(axis))])


def tree_visible(parents):
    parent_rows = parents.reshape(-1, DRAFT)
    positions = jnp.arange(DRAFT, dtype=jnp.int32)
    visible = jnp.broadcast_to(
        positions[:, None] == positions[None, :], (parent_rows.shape[0], DRAFT, DRAFT)
    )
    ancestor = parent_rows
    for repeat_step in range(DRAFT - 1):
        matched = ancestor[:, :, None] == positions[None, None, :]
        visible = visible | matched
        lifted = jnp.sum(jnp.where(matched, parent_rows[:, None, :], 0), axis=2)
        ancestor = jnp.where(ancestor >= 0, lifted, -1)
    return visible


def merge_pair(first, second):
    first_max, first_sum, first_out = first
    second_max, second_sum, second_out = second
    peak_max = jnp.maximum(first_max, second_max)
    first_factor = jnp.exp(first_max - peak_max)
    second_factor = jnp.exp(second_max - peak_max)
    joined_sum = first_factor * first_sum + second_factor * second_sum
    joined_out = first_factor[..., None] * first_out + second_factor[..., None] * second_out
    return (peak_max, joined_sum, joined_out)


def shards(
    queries,
    draft_keys,
    draft_values,
    parents,
    private_keys,
    private_values,
    priv_lengths,
    prefix_keys,
    prefix_values,
    out_weight,
):
    group_heads = HEADS // KVH
    score_scale = HD ** (-0.5)
    own_rows = queries.shape[0]
    owned_reqs = own_rows // DRAFT
    seq_count = lax.axis_size("seq")
    local_heads = HEADS // seq_count
    blocks = seq_count // KVH
    level_count = blocks.bit_length() - 1
    device = lax.axis_index("seq")
    head_group = device // blocks
    block_rank = device % blocks
    every_query = lax.all_gather(queries, "seq", axis=0, tiled=True)
    group_query = lax.dynamic_slice_in_dim(
        every_query, head_group * (group_heads * HD), group_heads * HD, 1
    )
    total_rows = group_query.shape[0]
    query_block = group_query.reshape(total_rows * group_heads, HD)
    key_all = prefix_keys[0]
    value_all = prefix_values[0]
    span = key_all.shape[0] // KVH
    running = None
    for part_index in range(KVH):
        key_block = key_all[part_index * span : (part_index + 1) * span]
        value_block = value_all[part_index * span : (part_index + 1) * span]
        scores = (
            lax.dot_general(
                query_block, key_block, (((1,), (1,)), ((), ())), preferred_element_type=jnp.float32
            )
            * score_scale
        )
        row_max = jnp.max(scores, axis=1)
        weights = jnp.exp(scores - row_max[:, None])
        weight_sum = jnp.sum(weights, axis=1)
        mixture = jnp.dot(
            weights.astype(jnp.bfloat16), value_block, preferred_element_type=jnp.float32
        )
        block_part = (row_max, weight_sum, mixture)
        running = block_part if running is None else merge_pair(running, block_part)
    pre_max = running[0].reshape(total_rows, group_heads)
    pre_sum = running[1].reshape(total_rows, group_heads)
    pre_out = running[2].reshape(total_rows, group_heads, HD)
    visible = tree_visible(parents)
    live_slots = jnp.arange(PRIV, dtype=jnp.int32)[None, :] < priv_lengths[:, None]
    own_maxes, own_sums, own_outs = ([], [], [])
    for group in range(KVH):
        cols_lo = group * group_heads * HD
        own_query = queries[:, cols_lo : cols_lo + group_heads * HD].reshape(
            owned_reqs, DRAFT, group_heads, HD
        )
        priv_keys = private_keys[:, :, group * HD : (group + 1) * HD]
        priv_vals = private_values[:, :, group * HD : (group + 1) * HD]
        draft_key = draft_keys[:, group * HD : (group + 1) * HD].reshape(owned_reqs, DRAFT, HD)
        draft_val = draft_values[:, group * HD : (group + 1) * HD].reshape(owned_reqs, DRAFT, HD)
        priv_scores = (
            jnp.einsum("rihd,rkd->rihk", own_query, priv_keys, preferred_element_type=jnp.float32)
            * score_scale
        )
        priv_scores = jnp.where(live_slots[:, None, None, :], priv_scores, -1e30)
        tree_scores = (
            jnp.einsum("rihd,rjd->rihj", own_query, draft_key, preferred_element_type=jnp.float32)
            * score_scale
        )
        tree_scores = jnp.where(visible[:, :, None, :], tree_scores, -1e30)
        row_max = jnp.maximum(jnp.max(priv_scores, axis=-1), jnp.max(tree_scores, axis=-1))
        priv_w = jnp.exp(priv_scores - row_max[..., None])
        tree_w = jnp.exp(tree_scores - row_max[..., None])
        weight_sum = jnp.sum(priv_w, axis=-1) + jnp.sum(tree_w, axis=-1)
        mixture = jnp.einsum(
            "rihk,rkd->rihd",
            priv_w.astype(jnp.bfloat16),
            priv_vals,
            preferred_element_type=jnp.float32,
        )
        mixture = mixture + jnp.einsum(
            "rihj,rjd->rihd",
            tree_w.astype(jnp.bfloat16),
            draft_val,
            preferred_element_type=jnp.float32,
        )
        own_maxes.append(row_max.reshape(own_rows, group_heads))
        own_sums.append(weight_sum.reshape(own_rows, group_heads))
        own_outs.append(mixture.reshape(own_rows, group_heads, HD))
    own_max = jnp.concatenate(own_maxes, axis=1)
    own_sum = jnp.concatenate(own_sums, axis=1)
    own_out = jnp.concatenate(own_outs, axis=1)
    priv_max, priv_sum, priv_out = (
        lax.all_to_all(own_max, "seq", split_axis=1, concat_axis=0, tiled=True),
        lax.all_to_all(own_sum, "seq", split_axis=1, concat_axis=0, tiled=True),
        lax.all_to_all(own_out, "seq", split_axis=1, concat_axis=0, tiled=True),
    )
    merged_parts = (pre_max, pre_sum, pre_out)
    for level in range(level_count):
        partner = from_partner((merged_parts[0], merged_parts[1], merged_parts[2]), "seq", level)
        merged_parts = merge_pair(merged_parts, partner)
    start_head = block_rank * local_heads
    peak_part = lax.dynamic_slice_in_dim(merged_parts[0], start_head, local_heads, 1)
    sum_part = lax.dynamic_slice_in_dim(merged_parts[1], start_head, local_heads, 1)
    out_part = lax.dynamic_slice_in_dim(merged_parts[2], start_head, local_heads, 1)
    joint_max = jnp.maximum(peak_part, priv_max)
    prefix_scale = jnp.exp(peak_part - joint_max)
    private_scale = jnp.exp(priv_max - joint_max)
    denom = prefix_scale * sum_part + private_scale * priv_sum
    merged = (prefix_scale[..., None] * out_part + private_scale[..., None] * priv_out) / denom[
        ..., None
    ]
    attention = merged.astype(jnp.bfloat16).reshape(total_rows, local_heads * HD)
    columns = jnp.dot(
        lax.all_gather(attention, "seq", axis=1, tiled=True),
        out_weight,
        preferred_element_type=jnp.float32,
    )
    return lax.all_to_all(columns, "seq", split_axis=0, concat_axis=1, tiled=True)


def solution(mesh):
    in_specs = (
        P(("groups", "seq"), None),
        P(("groups", "seq"), None),
        P(("groups", "seq"), None),
        P(("groups", "seq")),
        P(("groups", "seq"), None, None),
        P(("groups", "seq"), None, None),
        P(("groups", "seq")),
        P(("groups", "seq"), None, None),
        P(("groups", "seq"), None, None),
        P(None, "seq"),
    )
    out_specs = P(("groups", "seq"), None)
    return jax.shard_map(shards, mesh=mesh, in_specs=in_specs, out_specs=out_specs, check_vma=False)
```

profile of v0, /device:TPU:0, one launch (start us, length us, event | category | flops | bytes accessed | tf_op | source)
XLA Modules:
  0.0 196.0 jit_solution(10677234079913019351)
XLA Ops:
  8.8 0.9 select_reduce_fusion.1
  12.8 0.8 fusion.382
  13.6 1.2 fusion.381
  14.8 1.2 fusion.369
  16.1 0.8 fusion.372
  16.9 1.2 fusion.371
  19.0 1.2 fusion.373
  20.2 0.8 fusion.376
  21.1 1.2 fusion.375
  22.3 0.8 fusion.378
  23.2 1.2 fusion.377
  24.4 0.8 fusion.380
  25.3 1.2 fusion.379
  26.5 0.8 fusion.384
  27.3 1.2 fusion.383
  30.0 7.4 %all-to-all-start = ((f32[4,16,4]{2,0,1:T(4,128)}), f32[4,16,4]{2,0,1:T(4,128)S(1)}, u32[]{:S(2)}, u32[]{:S(2)}) async-start(f32[4,16,4]{2,0,1:T(4,128)} %copy.64), calls=%async_computation | async-start | bytes 65536 | tf_op jit(solution)/shard_map/all_to_all | solution.py:141
  44.0 5.7 %all-to-all-start.2 = ((f32[4,16,4]{2,0,1:T(4,128)}), f32[4,16,4]{2,0,1:T(4,128)S(1)}, u32[]{:S(2)}, u32[]{:S(2)}) async-start(f32[4,16,4]{2,0,1:T(4,128)} %copy.88), calls=%async_computation.2 | async-start | bytes 65536 | tf_op jit(solution)/shard_map/all_to_all | solution.py:142
  50.7 5.7 %all-to-all-done.2 = f32[4,16,4]{2,0,1:T(4,128)S(1)} async-done(((f32[4,16,4]{2,0,1:T(4,128)}), f32[4,16,4]{2,0,1:T(4,128)S(1)}, u32[]{:S(2)}, u32[]{:S(2)}) %all-to-all-start.2) | async-done | bytes 1056 | tf_op jit(solution)/shard_map/all_to_all | solution.py:142
  56.4 3.5 %all-to-all-start.1 = ((f32[4,64,128]{2,0,1:T(4,128)}), f32[4,64,128]{2,0,1:T(4,128)S(1)}, u32[]{:S(2)}, u32[]{:S(2)}) async-start(f32[4,64,128]{2,0,1:T(4,128)} %copy.70), calls=%async_computation.1 | async-start | bytes 262144 | tf_op jit(solution)/shard_map/all_to_all | solution.py:143
  60.1 7.7 %all-to-all-done.1 = f32[4,64,128]{2,0,1:T(4,128)S(1)} async-done(((f32[4,64,128]{2,0,1:T(4,128)}), f32[4,64,128]{2,0,1:T(4,128)S(1)}, u32[]{:S(2)}, u32[]{:S(2)}) %all-to-all-start.1) | async-done | bytes 131104 | tf_op jit(solution)/shard_map/all_to_all | solution.py:143
  67.8 1.5 reshape.1126
  69.5 3.8 %multiply_reduce_fusion = (f32[512]{0:T(512)S(1)}, f32[512,2048]{1,0:T(8,128)}) fusion(bf16[512,128]{1,0:T(8,128)(2,1)S(1)} %reshape.1098, bf16[1,16384,128]{2,1,0:T(8,128)(2,1)} %param.17), kind=kOutput, calls=%fused_computation.8 | convolution fusion | flops 270532096 | bytes 4851712 | tf_op jit(solution)/shard_map/dot_general | solution.py:80
  73.3 2.7 %multiply_reduce_fusion.1 = (f32[512]{0:T(512)S(1)}, f32[512,2048]{1,0:T(8,128)}) fusion(bf16[512,128]{1,0:T(8,128)(2,1)S(1)} %reshape.1098, bf16[1,16384,128]{2,1,0:T(8,128)(2,1)S(1)} %copy-done.7), kind=kOutput, calls=%fused_computation.9 | convolution fusion | flops 270532096 | bytes 4851712 | tf_op jit(solution)/shard_map/dot_general | solution.py:80
  76.0 2.7 %multiply_reduce_fusion.2 = (f32[512]{0:T(512)S(1)}, f32[512,2048]{1,0:T(8,128)}) fusion(bf16[512,128]{1,0:T(8,128)(2,1)S(1)} %reshape.1098, bf16[1,16384,128]{2,1,0:T(8,128)(2,1)S(1)} %copy-done.7), kind=kOutput, calls=%fused_computation.10 | convolution fusion | flops 270532096 | bytes 4851712 | tf_op jit(solution)/shard_map/dot_general | solution.py:80
  78.7 2.7 %multiply_reduce_fusion.3 = (f32[512]{0:T(512)S(1)}, f32[512,2048]{1,0:T(8,128)}) fusion(bf16[512,128]{1,0:T(8,128)(2,1)S(1)} %reshape.1098, bf16[1,16384,128]{2,1,0:T(8,128)(2,1)S(1)} %copy-done.7), kind=kOutput, calls=%fused_computation.11 | convolution fusion | flops 270532096 | bytes 4851712 | tf_op jit(solution)/shard_map/dot_general | solution.py:80
  81.3 2.6 %multiply_reduce_fusion.4 = (f32[512]{0:T(512)S(1)}, f32[512,2048]{1,0:T(8,128)}) fusion(bf16[512,128]{1,0:T(8,128)(2,1)S(1)} %reshape.1098, bf16[1,16384,128]{2,1,0:T(8,128)(2,1)S(1)} %copy-done.7), kind=kOutput, calls=%fused_computation.12 | convolution fusion | flops 270532096 | bytes 4851712 | tf_op jit(solution)/shard_map/dot_general | solution.py:80
  84.0 2.7 %multiply_reduce_fusion.5 = (f32[512]{0:T(512)S(1)}, f32[512,2048]{1,0:T(8,128)}) fusion(bf16[512,128]{1,0:T(8,128)(2,1)S(1)} %reshape.1098, bf16[1,16384,128]{2,1,0:T(8,128)(2,1)S(1)} %copy-done.7), kind=kOutput, calls=%fused_computation.13 | convolution fusion | flops 270532096 | bytes 4851712 | tf_op jit(solution)/shard_map/dot_general | solution.py:80
  86.6 2.7 %multiply_reduce_fusion.6 = (f32[512]{0:T(512)S(1)}, f32[512,2048]{1,0:T(8,128)}) fusion(bf16[512,128]{1,0:T(8,128)(2,1)S(1)} %reshape.1098, bf16[1,16384,128]{2,1,0:T(8,128)(2,1)S(1)} %copy-done.7), kind=kOutput, calls=%fused_computation.14 | convolution fusion | flops 270532096 | bytes 4851712 | tf_op jit(solution)/shard_map/dot_general | solution.py:80
  89.3 2.7 %multiply_reduce_fusion.7 = (f32[512]{0:T(512)S(1)}, f32[512,2048]{1,0:T(8,128)}) fusion(bf16[512,128]{1,0:T(8,128)(2,1)S(1)} %reshape.1098, bf16[1,16384,128]{2,1,0:T(8,128)(2,1)S(1)} %copy-done.7), kind=kOutput, calls=%fused_computation.15 | convolution fusion | flops 270532096 | bytes 4851712 | tf_op jit(solution)/shard_map/dot_general | solution.py:80
  92.7 3.0 %fusion.14 = f32[512]{0:T(512)S(1)} fusion(f32[512,2048]{1,0:T(8,128)} %get-tuple-element.86, f32[512]{0:T(512)S(1)} %get-tuple-element.85), kind=kLoop, calls=%fused_computation.30 | loop fusion | flops 3145216 | bytes 4198400 | tf_op jit(solution)/shard_map/reduce_sum | solution.py:87
  95.9 3.0 %fusion.12 = f32[512]{0:T(512)S(1)} fusion(f32[512,2048]{1,0:T(8,128)} %get-tuple-element.88, f32[512]{0:T(512)S(1)} %get-tuple-element.87), kind=kLoop, calls=%fused_computation.28 | loop fusion | flops 3145216 | bytes 4198400 | tf_op jit(solution)/shard_map/reduce_sum | solution.py:87
  99.2 3.0 %fusion.10 = f32[512]{0:T(512)S(1)} fusion(f32[512,2048]{1,0:T(8,128)} %get-tuple-element.90, f32[512]{0:T(512)S(1)} %get-tuple-element.89), kind=kLoop, calls=%fused_computation.26 | loop fusion | flops 3145216 | bytes 4198400 | tf_op jit(solution)/shard_map/reduce_sum | solution.py:87
  102.4 3.0 %fusion.8 = f32[512]{0:T(512)S(1)} fusion(f32[512,2048]{1,0:T(8,128)} %get-tuple-element.92, f32[512]{0:T(512)S(1)} %get-tuple-element.91), kind=kLoop, calls=%fused_computation.24 | loop fusion | flops 3145216 | bytes 4198400 | tf_op jit(solution)/shard_map/reduce_sum | solution.py:87
  105.7 3.0 %fusion.6 = f32[512]{0:T(512)S(1)} fusion(f32[512,2048]{1,0:T(8,128)} %get-tuple-element.94, f32[512]{0:T(512)S(1)} %get-tuple-element.93), kind=kLoop, calls=%fused_computation.22 | loop fusion | flops 3145216 | bytes 4198400 | tf_op jit(solution)/shard_map/reduce_sum | solution.py:87
  108.9 3.0 %fusion.4 = f32[512]{0:T(512)S(1)} fusion(f32[512,2048]{1,0:T(8,128)} %get-tuple-element.96, f32[512]{0:T(512)S(1)} %get-tuple-element.95), kind=kLoop, calls=%fused_computation.20 | loop fusion | flops 3145216 | bytes 4198400 | tf_op jit(solution)/shard_map/reduce_sum | solution.py:87
  112.2 3.0 %fusion.2 = f32[512]{0:T(512)S(1)} fusion(f32[512,2048]{1,0:T(8,128)} %get-tuple-element.84, f32[512]{0:T(512)S(1)} %get-tuple-element.83), kind=kLoop, calls=%fused_computation.18 | loop fusion | flops 3145216 | bytes 4198400 | tf_op jit(solution)/shard_map/reduce_sum | solution.py:87
  115.4 3.2 %fusion = f32[512]{0:T(512)S(1)} fusion(f32[512,2048]{1,0:T(8,128)} %get-tuple-element.98, f32[512]{0:T(512)S(1)} %get-tuple-element.97), kind=kLoop, calls=%fused_computation.16 | loop fusion | flops 3145216 | bytes 4198400 | tf_op jit(solution)/shard_map/reduce_sum | solution.py:87
  119.6 3.5 %fusion.54 = f32[512,128]{1,0:T(8,128)S(1)} fusion(f32[512,2048]{1,0:T(8,128)} %get-tuple-element.84, f32[512]{0:T(512)S(1)} %get-tuple-element.83, bf16[1,16384,128]{2,1,0:T(8,128)(2,1)} %param.18, f32[512]{0:T(512)S(1)} %get-tuple-element.49), kind=kOutput, calls=%fused_computation.58 | convolution fusion | flops 271646720 | bytes 4984832 | tf_op jit(solution)/shard_map/dot_general | solution.py:88
  123.0 2.0 %fusion.111 = f32[512,128]{1,0:T(8,128)S(1)} fusion(f32[512,128]{1,0:T(8,128)S(1)} %fusion.54, f32[512,2048]{1,0:T(8,128)S(1)} %copy-done.6, f32[512]{0:T(512)S(1)} %get-tuple-element.97, bf16[1,16384,128]{2,1,0:T(8,128)(2,1)} %param.18, f32[512]{0:T(512)S(1)} %get-tuple-element.50, f32[512]{0:T(512)S(1)} %get-tuple-element.46), kind=kOutput, calls=%fused_computation.77 | convolution fusion | flops 271777792 | bytes 5249024 | tf_op jit(solution)/shard_map/dot_general | solution.py:88
  125.1 2.0 %fusion.108 = f32[512,128]{1,0:T(8,128)S(1)} fusion(f32[512,128]{1,0:T(8,128)S(1)} %fusion.111, f32[512,2048]{1,0:T(8,128)S(1)} %copy-done.5, f32[512]{0:T(512)S(1)} %get-tuple-element.95, bf16[1,16384,128]{2,1,0:T(8,128)(2,1)} %param.18, f32[512]{0:T(512)S(1)} %get-tuple-element.47, f32[512]{0:T(512)S(1)} %get-tuple-element.48), kind=kOutput, calls=%fused_computation.76 | convolution fusion | flops 271777792 | bytes 5249024 | tf_op jit(solution)/shard_map/dot_general | solution.py:88
  127.2 2.4 %fusion.105 = f32[512,128]{1,0:T(8,128)S(1)} fusion(f32[512,128]{1,0:T(8,128)S(1)} %fusion.108, f32[512,2048]{1,0:T(8,128)S(1)} %copy-done.4, f32[512]{0:T(512)S(1)} %get-tuple-element.93, bf16[1,16384,128]{2,1,0:T(8,128)(2,1)} %param.18, f32[512]{0:T(512)S(1)} %get-tuple-element.45, f32[512]{0:T(512)S(1)} %get-tuple-element.42), kind=kOutput, calls=%fused_computation.75 | convolution fusion | flops 271777792 | bytes 5249024 | tf_op jit(solution)/shard_map/dot_general | solution.py:88
  129.6 0.8 fusion.102
  130.4 0.8 fusion.99
  131.9 0.8 fusion.96
  134.6 0.9 collective-permute-done.1
  136.6 34.5 %all-gather.4.cloned.1.call-done = bf16[64,8192]{1,0:T(8,128)(2,1)} async-done(((bf16[64,512]{1,0:T(8,128)(2,1)}), bf16[64,8192]{1,0:T(8,128)(2,1)}) %all-gather.4.cloned.1.call-update) | async-done | bytes 1048592 | tf_op jit(solution)/shard_map/all_gather | solution.py:162
  171.1 5.3 %fusion.385 = f32[64,512]{1,0:T(8,128)S(1)} fusion(bf16[64,8192]{1,0:T(8,128)(2,1)} %all-gather.4.cloned.1.call-done, bf16[8192,512]{1,0:T(8,128)(2,1)} %param.19), kind=kOutput, calls=%fused_computation.421 | convolution fusion | flops 536870912 | bytes 9568256 | tf_op jit(solution)/shard_map/dot_general | solution.py:161
  176.5 12.0 %all_to_all.69 = f32[16,4,512]{2,1,0:T(4,128)S(1)} all-to-all(f32[16,4,512]{2,1,0:T(4,128)S(1)} %all_to_all.61), channel_id=1, replica_groups=mesh['groups'=2,'seq'=16] {'seq'}, dimensions={0} | all-to-all | bytes 262144 | tf_op jit(solution)/shard_map/all_to_all | solution.py:166
  (164 shorter events, 21.9 us)
Async XLA Ops:
  6.5 31.0 %copy-start.9 = (bf16[1,1024,1024]{2,1,0:T(8,128)(2,1)S(1)}, bf16[1,1024,1024]{2,1,0:T(8,128)(2,1)}, u32[]{:S(2)}) copy-start(bf16[1,1024,1024]{2,1,0:T(8,128)(2,1)} %param.15) | copy-start | bytes 6291460
  6.5 33.6 %copy-start.10 = (bf16[4,1024]{1,0:T(4,128)(2,1)S(1)}, bf16[4,1024]{1,0:T(4,128)(2,1)}, u32[]{:S(2)}) copy-start(bf16[4,1024]{1,0:T(4,128)(2,1)} %param.12) | copy-start | bytes 24580
  6.5 61.3 %all-gather.6.cloned.1.call-start = ((), (), s32[]{:S(2)}) async-start(), calls=%async_computation.5 | async-start | bytes 1114112 | tf_op jit(solution)/shard_map/all_gather | solution.py:66
  30.0 14.1 %all-to-all-start = ((f32[4,16,4]{2,0,1:T(4,128)}), f32[4,16,4]{2,0,1:T(4,128)S(1)}, u32[]{:S(2)}, u32[]{:S(2)}) async-start(f32[4,16,4]{2,0,1:T(4,128)} %copy.64), calls=%async_computation | async-start | bytes 65536 | tf_op jit(solution)/shard_map/all_to_all | solution.py:141
  44.0 12.3 %all-to-all-start.2 = ((f32[4,16,4]{2,0,1:T(4,128)}), f32[4,16,4]{2,0,1:T(4,128)S(1)}, u32[]{:S(2)}, u32[]{:S(2)}) async-start(f32[4,16,4]{2,0,1:T(4,128)} %copy.88), calls=%async_computation.2 | async-start | bytes 65536 | tf_op jit(solution)/shard_map/all_to_all | solution.py:142
  56.4 11.4 %all-to-all-start.1 = ((f32[4,64,128]{2,0,1:T(4,128)}), f32[4,64,128]{2,0,1:T(4,128)S(1)}, u32[]{:S(2)}, u32[]{:S(2)}) async-start(f32[4,64,128]{2,0,1:T(4,128)} %copy.70), calls=%async_computation.1 | async-start | bytes 262144 | tf_op jit(solution)/shard_map/all_to_all | solution.py:143
  59.9 111.3 %all-gather.4.cloned.1.call-start = ((), (), s32[]{:S(2)}) async-start(), calls=%async_computation.4 | async-start | bytes 1114112 | tf_op jit(solution)/shard_map/all_gather | solution.py:162
  69.4 3.8 %copy-start.7 = (bf16[1,16384,128]{2,1,0:T(8,128)(2,1)S(1)}, bf16[1,16384,128]{2,1,0:T(8,128)(2,1)}, u32[]{:S(2)}) copy-start(bf16[1,16384,128]{2,1,0:T(8,128)(2,1)} %param.17) | copy-start | bytes 12582916
  118.9 4.1 %copy-start.6 = (f32[512,2048]{1,0:T(8,128)S(1)}, f32[512,2048]{1,0:T(8,128)}, u32[]{:S(2)}) copy-start(f32[512,2048]{1,0:T(8,128)} %get-tuple-element.98) | copy-start | bytes 12582916
  119.0 15.1 %collective-permute-start.2 = (f32[64,8]{0,1:T(8,128)S(1)}, f32[64,8]{0,1:T(8,128)S(1)}, u32[]{:S(2)}, u32[]{:S(2)}) collective-permute-start(f32[64,8]{0,1:T(8,128)S(1)} %get-tuple-element.12), channel_id=1, source_target_pairs={{0,1},{1,0},{2,3},{3,2},{4,5},{5,4},{6,7},{7,6},{8,9},{9,8},{10,11... | collective-permute-start | bytes 6152 | tf_op jit(solution)/shard_map/ppermute | solution.py:14
  119.0 15.0 %collective-permute-start = (f32[64,8]{0,1:T(8,128)S(1)}, f32[64,8]{0,1:T(8,128)S(1)}, u32[]{:S(2)}, u32[]{:S(2)}) collective-permute-start(f32[64,8]{0,1:T(8,128)S(1)} %get-tuple-element.13), channel_id=1, source_target_pairs={{0,1},{1,0},{2,3},{3,2},{4,5},{5,4},{6,7},{7,6},{8,9},{9,8},{10,11... | collective-permute-start | bytes 6152 | tf_op jit(solution)/shard_map/ppermute | solution.py:14
  119.6 5.5 %copy-start.5 = (f32[512,2048]{1,0:T(8,128)S(1)}, f32[512,2048]{1,0:T(8,128)}, u32[]{:S(2)}) copy-start(f32[512,2048]{1,0:T(8,128)} %get-tuple-element.96) | copy-start | bytes 12582916
  123.0 4.1 %copy-start.4 = (f32[512,2048]{1,0:T(8,128)S(1)}, f32[512,2048]{1,0:T(8,128)}, u32[]{:S(2)}) copy-start(f32[512,2048]{1,0:T(8,128)} %get-tuple-element.94) | copy-start | bytes 12582916
  125.1 4.5 %copy-start.3 = (f32[512,2048]{1,0:T(8,128)S(1)}, f32[512,2048]{1,0:T(8,128)}, u32[]{:S(2)}) copy-start(f32[512,2048]{1,0:T(8,128)} %get-tuple-element.92) | copy-start | bytes 12582916
  125.1 4.5 %copy-start.8 = (bf16[1,16384,128]{2,1,0:T(8,128)(2,1)S(1)}, bf16[1,16384,128]{2,1,0:T(8,128)(2,1)}, u32[]{:S(2)}) copy-start(bf16[1,16384,128]{2,1,0:T(8,128)(2,1)} %param.18) | copy-start | bytes 12582916
  127.2 3.3 %copy-start.2 = (f32[512,2048]{1,0:T(8,128)S(1)}, f32[512,2048]{1,0:T(8,128)}, u32[]{:S(2)}) copy-start(f32[512,2048]{1,0:T(8,128)} %get-tuple-element.90) | copy-start | bytes 12582916
  129.6 2.4 %copy-start.1 = (f32[512,2048]{1,0:T(8,128)S(1)}, f32[512,2048]{1,0:T(8,128)}, u32[]{:S(2)}) copy-start(f32[512,2048]{1,0:T(8,128)} %get-tuple-element.88) | copy-start | bytes 12582916
  130.4 2.7 %copy-start = (f32[512,2048]{1,0:T(8,128)S(1)}, f32[512,2048]{1,0:T(8,128)}, u32[]{:S(2)}) copy-start(f32[512,2048]{1,0:T(8,128)} %get-tuple-element.86) | copy-start | bytes 12582916
  134.0 1.6 collective-permute-start.1
Sparse Core Ops, SparseCore 0:
  9.5 41.1 all-gather.5
  136.8 34.3 all-gather.3
where the time goes:
time: 197 us; the launch traced here: 196 us
  matrix products  61.1 us (31%)
  waiting for transfers between devices  49.8 us (25%)
  other arithmetic  29.8 us (15%)
  starting transfers between devices  17.3 us (9%)
  between operations  14.7 us (7%)
  blocking collectives  12 us (6%)
  local copies, waits for them, and re-layouts  11.3 us (6%)
    all_gather x1, waiting for transfers between devices, shards(): lax.all_gather(attention, 'seq', axis=1, tiled=True)  34.5 us
    reduce_sum x8, other arithmetic, shards(): weight_sum = jnp.sum(weights, axis=1)  24.4 us
    dot_general x8, matrix products, shards(): lax.dot_general(query_block, key_block, (((1,), (1,)), ((), ())), preferr...  22.5 us
    dot_general x8, matrix products, shards(): jnp.dot(weights.astype(jnp.bfloat16), value_block, preferred_element_type...  13.3 us
    all_to_all x1, blocking collectives, shards(): lax.all_to_all(columns, 'seq', split_axis=0, concat_axis=1, tiled=True)  12 us
    dot_general x8, matrix products, shards(): jnp.einsum('rihd,rkd->rihk', own_query, priv_keys, preferred_element_type...  9.86 us
    all_to_all x1, waiting for transfers between devices, shards(): lax.all_to_all(own_out, 'seq', split_axis=1, concat_axis=0, tiled=True)  7.65 us
    all_to_all x1, starting transfers between devices, shards(): lax.all_to_all(own_max, 'seq', split_axis=1, concat_axis=0, tiled=True)  7.42 us
  transfers between devices with their start and end apart: 8, of which 5 were waited for; matrix products, arithmetic and copies ran while one was open for 22% of the time, Pallas kernels for 0%

commit v1 on v0

v1 whole, which is shorter than its diff:
```python
import functools

import jax
import jax.numpy as jnp
from jax import lax
from jax.experimental import pallas as pl
from jax.experimental.pallas import tpu as pltpu
from jax.sharding import PartitionSpec as P

HEADS = 64
KVH = 8
HD = 128
GROUP = HEADS // KVH
SCALE = HD ** (-0.5)
LOG2E = 1.4426950408889634
LANES = 128
NEG = -1e30
NT = (((1,), (1,)), ((), ()))
F32 = jnp.float32
BF16 = jnp.bfloat16


def private_kernel(par_ref, len_ref, q_ref, dk_ref, dv_ref, k_ref, v_ref, out_ref, *, draft, blocks):
    heads = GROUP // blocks
    rows = GROUP * draft
    slots = k_ref.shape[1]
    q32 = q_ref[...].astype(F32)
    query = jnp.concatenate(
        [q32[:, h * HD : (h + 1) * HD] for h in range(GROUP)], axis=0
    ).astype(BF16)
    live = lax.broadcasted_iota(jnp.int32, (rows, slots), 1) < len_ref[0]
    scores = lax.dot_general(query, k_ref[0], NT, preferred_element_type=F32) * SCALE
    scores = jnp.where(live, scores, NEG)
    seen = []
    for i in range(draft):
        bits = jnp.int32(1 << i)
        for j in range(i):
            bits = bits | jnp.where(par_ref[i] == j, seen[j], 0)
        seen.append(bits)
    row = lax.broadcasted_iota(jnp.int32, (rows, LANES), 0) % draft
    lane = lax.broadcasted_iota(jnp.int32, (rows, LANES), 1)
    shown = lane < 0
    for i in range(draft):
        for j in range(i + 1):
            hit = (seen[i] >> j) & 1
            shown = shown | ((row == i) & (lane == j) & (hit == 1))
    fill = jnp.zeros((LANES - draft, HD), F32)
    dkey = jnp.concatenate([dk_ref[...].astype(F32), fill], axis=0).astype(BF16)
    dval = jnp.concatenate([dv_ref[...].astype(F32), fill], axis=0).astype(BF16)
    tree = lax.dot_general(query, dkey, NT, preferred_element_type=F32) * SCALE
    tree = jnp.where(shown, tree, NEG)
    peak = jnp.maximum(
        jnp.max(scores, axis=1, keepdims=True), jnp.max(tree, axis=1, keepdims=True)
    )
    weights = jnp.exp(scores - peak)
    tree_w = jnp.exp(tree - peak)
    denom = jnp.sum(weights, axis=1, keepdims=True) + jnp.sum(tree_w, axis=1, keepdims=True)
    mixture = jnp.dot(weights.astype(BF16), v_ref[0], preferred_element_type=F32)
    mixture = mixture + jnp.dot(tree_w.astype(BF16), dval, preferred_element_type=F32)
    mixture = mixture / denom
    lse = peak + jnp.log(denom)
    first = lse.astype(BF16).astype(F32)
    second = (lse - first).astype(BF16).astype(F32)
    third = lse - first - second
    stat_lane = lax.broadcasted_iota(jnp.int32, (draft, LANES), 1)
    for b in range(blocks):
        stats = jnp.zeros((draft, LANES), F32)
        for hh in range(heads):
            lo = (b * heads + hh) * draft
            out_ref[b, :, hh * HD : (hh + 1) * HD] = mixture[lo : lo + draft].astype(BF16)
            for t, term in enumerate((first, second, third)):
                stats = jnp.where(stat_lane == 3 * hh + t, term[lo : lo + draft], stats)
        out_ref[b, :, heads * HD :] = stats.astype(BF16)


def private_part(parents, lengths, queries, dkeys, dvals, pkeys, pvals, blocks):
    draft = queries.shape[0]
    slots = pkeys.shape[1]
    wide = (GROUP // blocks) * HD + LANES
    smem = pl.BlockSpec(memory_space=pltpu.SMEM)
    return pl.pallas_call(
        functools.partial(private_kernel, draft=draft, blocks=blocks),
        grid=(KVH,),
        in_specs=[
            smem,
            smem,
            pl.BlockSpec((draft, GROUP * HD), lambda g: (0, g)),
            pl.BlockSpec((draft, HD), lambda g: (0, g)),
            pl.BlockSpec((draft, HD), lambda g: (0, g)),
            pl.BlockSpec((1, slots, HD), lambda g: (0, 0, g)),
            pl.BlockSpec((1, slots, HD), lambda g: (0, 0, g)),
        ],
        out_specs=pl.BlockSpec((blocks, draft, wide), lambda g: (g, 0, 0)),
        out_shape=jax.ShapeDtypeStruct((KVH * blocks, draft, wide), BF16),
        name="private_part",
    )(parents, lengths, queries, dkeys, dvals, pkeys, pvals)


def prefix_kernel(rank_ref, q_ref, k_ref, v_ref, keep_ref, send_ref, q32, qs, peak, denom, acc):
    step = pl.program_id(0)
    owners, draft, _ = q_ref.shape
    rows = owners * draft

    @pl.when(step == 0)
    def _():
        for s in range(owners):
            q32[s * draft : (s + 1) * draft, :] = q_ref[s].astype(F32)
        for h in range(GROUP):
            qs[h * rows : (h + 1) * rows, :] = q32[:, h * HD : (h + 1) * HD].astype(BF16)
        peak[...] = jnp.full(peak.shape, NEG, F32)
        denom[...] = jnp.zeros(denom.shape, F32)
        acc[...] = jnp.zeros(acc.shape, F32)

    scores = lax.dot_general(qs[...], k_ref[0], NT, preferred_element_type=F32)
    tiles = scores.shape[1] // LANES
    top = scores[:, :LANES]
    for j in range(1, tiles):
        top = jnp.maximum(top, scores[:, j * LANES : (j + 1) * LANES])
    old = peak[...]
    new = jnp.maximum(old, jnp.max(top, axis=1, keepdims=True) * (SCALE * LOG2E))
    fade = jnp.exp2(old - new)
    peak[...] = new
    parts = [
        jnp.exp2(scores[:, j * LANES : (j + 1) * LANES] * (SCALE * LOG2E) - new)
        for j in range(tiles)
    ]
    total = parts[0]
    for part in parts[1:]:
        total = total + part
    denom[...] = denom[...] * fade + total
    weights = jnp.concatenate([part.astype(BF16) for part in parts], axis=1)
    acc[...] = acc[...] * fade + jnp.dot(weights, v_ref[0], preferred_element_type=F32)

    @pl.when(step == pl.num_programs(0) - 1)
    def _():
        total = jnp.sum(denom[...], axis=1, keepdims=True)
        acc[...] = acc[...] / total
        denom[...] = peak[...] * (1.0 / LOG2E) + jnp.log(total)
        half = keep_ref.shape[0]
        mine = pl.multiple_of(rank_ref[0] * half, half)
        other = pl.multiple_of((1 - rank_ref[0]) * half, half)
        keep_ref[:, :HD] = acc[pl.ds(mine, half), :]
        keep_ref[:, HD:] = denom[pl.ds(mine, half), :]
        send_ref[:, :HD] = acc[pl.ds(other, half), :]
        send_ref[:, HD:] = denom[pl.ds(other, half), :]


def prefix_part(side, queries, keys, values, span):
    owners, draft, _ = queries.shape
    rows = owners * draft * GROUP
    shape = jax.ShapeDtypeStruct((rows // 2, HD + LANES), F32)
    return pl.pallas_call(
        prefix_kernel,
        grid_spec=pltpu.PrefetchScalarGridSpec(
            num_scalar_prefetch=1,
            grid=(keys.shape[1] // span,),
            in_specs=[
                pl.BlockSpec(queries.shape, lambda i, r: (0, 0, 0)),
                pl.BlockSpec((1, span, HD), lambda i, r: (0, i, 0)),
                pl.BlockSpec((1, span, HD), lambda i, r: (0, i, 0)),
            ],
            out_specs=[
                pl.BlockSpec((rows // 2, HD + LANES), lambda i, r: (0, 0)),
                pl.BlockSpec((rows // 2, HD + LANES), lambda i, r: (0, 0)),
            ],
            scratch_shapes=[
                pltpu.VMEM((owners * draft, GROUP * HD), F32),
                pltpu.VMEM((rows, HD), BF16),
                pltpu.VMEM((rows, LANES), F32),
                pltpu.VMEM((rows, LANES), F32),
                pltpu.VMEM((rows, HD), F32),
            ],
        ),
        out_shape=[shape, shape],
        name="prefix_part",
    )(side, queries, keys, values)


def join(first, second):
    out_a, lse_a = first[:, :HD], first[:, HD:]
    out_b, lse_b = second[:, :HD], second[:, HD:]
    top = jnp.maximum(lse_a, lse_b)
    scale_a = jnp.exp(lse_a - top)
    scale_b = jnp.exp(lse_b - top)
    both = scale_a + scale_b
    return jnp.concatenate(
        [(scale_a * out_a + scale_b * out_b) / both, top + jnp.log(both)], axis=1
    )


def merge_kernel(mine_ref, other_ref, priv_ref, att_ref, p32):
    owners, draft, wide = priv_ref.shape
    rows = owners * draft
    heads = (wide - LANES) // HD
    for s in range(owners):
        p32[s * draft : (s + 1) * draft, :] = priv_ref[s].astype(F32)
    for h in range(heads):
        part = slice(h * rows, (h + 1) * rows)
        col = heads * HD + 3 * h
        lse_p = (p32[:, col : col + 1] + p32[:, col + 1 : col + 2]) + p32[:, col + 2 : col + 3]
        lse_a = mine_ref[part, HD:]
        lse_b = other_ref[part, HD:]
        top = jnp.maximum(jnp.maximum(lse_a, lse_b), lse_p)
        scale_a = jnp.exp(lse_a - top)
        scale_b = jnp.exp(lse_b - top)
        scale_p = jnp.exp(lse_p - top)
        mixed = (
            scale_a * mine_ref[part, :HD]
            + scale_b * other_ref[part, :HD]
            + scale_p * p32[:, h * HD : (h + 1) * HD]
        ) / (scale_a + scale_b + scale_p)
        mixed = mixed.astype(BF16)
        for copy in range(att_ref.shape[0]):
            att_ref[copy, :, h * HD : (h + 1) * HD] = mixed


def merge_part(mine, other, priv, copies):
    owners, draft, wide = priv.shape
    return pl.pallas_call(
        merge_kernel,
        out_shape=jax.ShapeDtypeStruct((copies, owners * draft, wide - LANES), BF16),
        scratch_shapes=[pltpu.VMEM((owners * draft, wide), F32)],
        name="merge_part",
    )(mine, other, priv)


def project_kernel(side_ref, own_ref, oth_ref, wo_ref, wp_ref, out_ref):
    step = pl.program_id(0)
    part = jnp.dot(own_ref[0], wo_ref[0, 0], preferred_element_type=F32)
    part = part + jnp.dot(oth_ref[0], wp_ref[0, 0], preferred_element_type=F32)

    @pl.when(step == 0)
    def _():
        out_ref[...] = part

    @pl.when(step > 0)
    def _():
        out_ref[...] = out_ref[...] + part


def project(side, own, oth, weight):
    chips, rows, deep = own.shape
    cols = weight.shape[1]
    split = weight.reshape(chips, 2, deep, cols)
    return pl.pallas_call(
        project_kernel,
        grid_spec=pltpu.PrefetchScalarGridSpec(
            num_scalar_prefetch=1,
            grid=(chips,),
            in_specs=[
                pl.BlockSpec((1, rows, deep), lambda i, r: (i, 0, 0)),
                pl.BlockSpec((1, rows, deep), lambda i, r: (i, 0, 0)),
                pl.BlockSpec((1, 1, deep, cols), lambda i, r: (i, r[0], 0, 0)),
                pl.BlockSpec((1, 1, deep, cols), lambda i, r: (i, 1 - r[0], 0, 0)),
            ],
            out_specs=pl.BlockSpec((rows, cols), lambda i, r: (0, 0)),
        ),
        out_shape=jax.ShapeDtypeStruct((rows, cols), F32),
        name="project",
    )(side, own, oth, split, split)


def shards(
    queries,
    draft_keys,
    draft_values,
    parents,
    private_keys,
    private_values,
    priv_lengths,
    prefix_keys,
    prefix_values,
    out_weight,
):
    own_rows = queries.shape[0]
    seq = lax.axis_size("seq")
    blocks = seq // KVH
    device = lax.axis_index("seq")
    rank = device % blocks
    top_bit = blocks.bit_length() - 2
    side = ((rank >> top_bit) & 1).astype(jnp.int32).reshape(1)
    parity = (device % 2).astype(jnp.int32).reshape(1)

    def from_partner(array, bit):
        return lax.ppermute(array, "seq", [(i, i ^ 1 << bit) for i in range(seq)])

    by_group = queries.reshape(own_rows, KVH, GROUP * HD).transpose(1, 0, 2)
    ask = jnp.broadcast_to(by_group[:, None], (KVH, blocks, own_rows, GROUP * HD))
    ask = ask.reshape(seq, own_rows, GROUP * HD)
    every_query = lax.all_to_all(ask, "seq", split_axis=0, concat_axis=0, tiled=True)

    told = private_part(
        parents, priv_lengths, queries, draft_keys, draft_values, private_keys, private_values, blocks
    )
    priv = lax.all_to_all(told, "seq", split_axis=0, concat_axis=0, tiled=True)

    span = min(1024, prefix_keys.shape[1])
    mine, gone = prefix_part(side, every_query, prefix_keys, prefix_values, span)
    other = from_partner(gone, top_bit)
    for level in range(top_bit - 1, -1, -1):
        held = join(mine, other)
        half = held.shape[0] // 2
        at = (rank >> level) & 1
        mine = lax.dynamic_slice_in_dim(held, at * half, half, 0)
        other = from_partner(lax.dynamic_slice_in_dim(held, (1 - at) * half, half, 0), level)

    members = [list(range(c, seq, 2)) for c in range(2)]
    copies = merge_part(mine, other, priv, seq // 2)
    same = lax.all_to_all(
        copies, "seq", split_axis=0, concat_axis=0, axis_index_groups=members, tiled=True
    )
    twin = from_partner(same, 0)
    columns = project(parity, same, twin, out_weight)
    pieces = columns.reshape(seq, own_rows, columns.shape[1])
    done = lax.all_to_all(pieces, "seq", split_axis=0, concat_axis=0, tiled=True)
    return done.transpose(1, 0, 2).reshape(own_rows, seq * columns.shape[1])


def solution(mesh):
    in_specs = (
        P(("groups", "seq"), None),
        P(("groups", "seq"), None),
        P(("groups", "seq"), None),
        P(("groups", "seq")),
        P(("groups", "seq"), None, None),
        P(("groups", "seq"), None, None),
        P(("groups", "seq")),
        P(("groups", "seq"), None, None),
        P(("groups", "seq"), None, None),
        P(None, "seq"),
    )
    out_specs = P(("groups", "seq"), None)
    return jax.shard_map(shards, mesh=mesh, in_specs=in_specs, out_specs=out_specs, check_vma=False)
```

time: 197 us -> 99.7 us (0.51)
  matrix products: 61.1 us -> 0 us
  waiting for transfers between devices: 49.8 us -> 9.8 us
  Pallas kernels: 0 us -> 34.9 us
  other arithmetic: 29.8 us -> 0 us
  blocking collectives: 12 us -> 40.5 us
  between operations: 14.7 us -> 0.7 us
  starting transfers between devices: 17.3 us -> 7.42 us
  local copies, waits for them, and re-layouts: 11.3 us -> 5.37 us
    dot_general x49 -> x0, matrix products: 61.1 us -> none  [the longest x8 22.5 us: shards(): lax.dot_general(query_block, key_block, (((1,), (1,)), ((), ())), preferr...]
    pallas_call x0 -> x4, Pallas kernels: none -> 34.9 us  [the longest x1 17.7 us: prefix_part(): pl.pallas_call(prefix_kernel, grid_spec=pltpu.PrefetchScalarGridSpec(num_...]
    all_gather x2 -> x0, waiting for transfers between devices: 34.5 us -> none  [the longest x1 34.5 us: shards(): lax.all_gather(attention, 'seq', axis=1, tiled=True)]
    all_to_all x1 -> x3, blocking collectives: 12 us -> 40.5 us  [the longest x1 17.9 us: shards(): lax.all_to_all(copies, 'seq', split_axis=0, concat_axis=0, axis_index_gro...]
    reduce_sum x26 -> x0, other arithmetic: 27.8 us -> none  [the longest x8 24.4 us: shards(): weight_sum = jnp.sum(weights, axis=1)]
    all_to_all x3 -> x1, starting transfers between devices: 16.6 us -> 7.41 us  [shards(): lax.all_to_all(ask, 'seq', split_axis=0, concat_axis=0, tiled=True)]
    all_to_all x3 -> x1, waiting for transfers between devices: 13.7 us -> 7.89 us  [shards(): lax.all_to_all(ask, 'seq', split_axis=0, concat_axis=0, tiled=True)]
    concatenate x5 -> x0, local copies, waits for them, and re-layouts: 2.1 us -> none  [the longest x1 0.75 us: shards(): own_out = jnp.concatenate(own_outs, axis=1)]
  transfers between devices with their start and end apart: 8 -> 3, of which waited for: 5 -> 2; matrix products, arithmetic and copies ran while one was open for 22% -> 0% of each run, Pallas kernels for 0% -> 8%
where the time goes in v1:
time: 99.7 us; the launch traced here: 98.7 us
  blocking collectives  40.5 us (41%)
  Pallas kernels  34.9 us (35%)
  waiting for transfers between devices  9.8 us (10%)
  starting transfers between devices  7.42 us (7%)
  local copies, waits for them, and re-layouts  5.37 us (5%)
    all_to_all x1, blocking collectives, shards(): lax.all_to_all(copies, 'seq', split_axis=0, concat_axis=0, axis_index_gro...  17.9 us
    pallas_call x1, Pallas kernels, prefix_part(): pl.pallas_call(prefix_kernel, grid_spec=pltpu.PrefetchScalarGridSpec(num_...  17.7 us
    all_to_all x1, blocking collectives, shards(): lax.all_to_all(pieces, 'seq', split_axis=0, concat_axis=0, tiled=True)  11.4 us
    all_to_all x1, blocking collectives, shards(): priv = lax.all_to_all(told, 'seq', split_axis=0, concat_axis=0, tiled=True)  11.3 us
    all_to_all x1, waiting for transfers between devices, shards(): lax.all_to_all(ask, 'seq', split_axis=0, concat_axis=0, tiled=True)  7.89 us
    pallas_call x1, Pallas kernels, project(): pl.pallas_call(project_kernel, grid_spec=pltpu.PrefetchScalarGridSpec(num...  7.54 us
    pallas_call x1, Pallas kernels, private_part(): pl.pallas_call(functools.partial(private_kernel, draft=draft, blocks=bloc...  7.53 us
    all_to_all x1, starting transfers between devices, shards(): lax.all_to_all(ask, 'seq', split_axis=0, concat_axis=0, tiled=True)  7.41 us
  transfers between devices with their start and end apart: 3, of which 2 were waited for; matrix products, arithmetic and copies ran while one was open for 0% of the time, Pallas kernels for 8%

profile of v1, /device:TPU:0, one launch (start us, length us, event | category | flops | bytes accessed | tf_op | source)
XLA Modules:
  0.0 98.7 jit_solution(13376102212797170155)
XLA Ops:
  0.0 0.9 copy.15
  0.9 0.1 copy.11
  0.9 0.7 broadcast_in_dim.2
  1.6 7.4 %all-to-all-start = ((bf16[16,4,1024]{2,1,0:T(4,128)(2,1)}), bf16[16,4,1024]{2,1,0:T(4,128)(2,1)S(1)}, u32[]{:S(2)}, u32[]{:S(2)}) async-start(bf16[16,4,1024]{2,1,0:T(4,128)(2,1)} %bitcast.3), calls=%async_computation | async-start | bytes 262144 | tf_op jit(solution)/shard_map/all_to_all | solution.py:290
  9.1 7.9 %all-to-all-done.q_ref = bf16[16,4,1024]{2,1,0:T(4,128)(2,1)S(1)} async-done(((bf16[16,4,1024]{2,1,0:T(4,128)(2,1)}), bf16[16,4,1024]{2,1,0:T(4,128)(2,1)S(1)}, u32[]{:S(2)}, u32[]{:S(2)}) %all-to-all-start) | async-done | bytes 131104 | tf_op jit(solution)/shard_map/all_to_all | solution.py:290
  16.9 0.0 copy-start.1
  16.9 0.7 copy-done.1
  17.6 17.7 %prefix_part.1 = (f32[256,256]{1,0:T(8,128)}, f32[256,256]{1,0:T(8,128)}) custom-call(s32[1]{0:T(128)} %bitcast.1.rank_ref, bf16[16,4,1024]{2,1,0:T(4,128)(2,1)} %copy-done.1, bf16[1,16384,128]{2,1,0:T(8,128)(2,1)} %k_ref.2, bf16[1,16384,128]{2,1,0:T(8,128)(2,1)} %v_ref.2), custom_call_target="tpu_custom_call" | custom-call | tf_op jit(solution)/shard_map/prefix_part/pallas_call | solution.py:152
  35.3 0.0 collective-permute-start
  36.0 7.5 %private_part.1 = bf16[16,4,640]{2,1,0:T(4,128)(2,1)} custom-call(s32[4]{0:T(128)} %par_ref.1, s32[1]{0:T(128)S(6)} %copy.17.len_ref, bf16[4,8192]{1,0:T(4,128)(2,1)} %q_ref.1, bf16[4,1024]{1,0:T(4,128)(2,1)} %dk_ref.1, bf16[4,1024]{1,0:T(4,128)(2,1)} %dv_ref.1, bf16[1,1024,1024]{2,1,0:T(8,128)(2,1)} %k_ref.3, bf16[1,1024,1024]{2,1,0:T(8,128)(2,1)} %v_ref.3), custom_call_target="tpu_custom_call" | custom-call | tf_op jit(solution)/shard_map/private_part/pallas_call | solution.py:81
  43.5 11.3 %all_to_all.20.priv_ref = bf16[16,4,640]{2,1,0:T(4,128)(2,1)} all-to-all(bf16[16,4,640]{2,1,0:T(4,128)(2,1)} %private_part.1), channel_id=1, replica_groups=mesh['groups'=2,'seq'=16] {'seq'}, dimensions={0} | all-to-all | bytes 163840 | tf_op jit(solution)/shard_map/all_to_all | solution.py:295
  54.8 0.0 collective-permute-done.other_ref
  54.8 0.0 copy-start.3
  54.8 0.7 copy-done.3
  55.5 2.1 %merge_part.1 = bf16[8,64,512]{2,1,0:T(8,128)(2,1)} custom-call(f32[256,256]{1,0:T(8,128)} %get-tuple-element.7.mine_ref, f32[256,256]{1,0:T(8,128)} %copy-done.3, bf16[16,4,640]{2,1,0:T(4,128)(2,1)} %all_to_all.20.priv_ref), custom_call_target="tpu_custom_call" | custom-call | tf_op jit(solution)/shard_map/merge_part/pallas_call | solution.py:219
  57.6 17.9 %all_to_all.21.own_ref = bf16[8,64,512]{2,1,0:T(8,128)(2,1)S(1)} all-to-all(bf16[8,64,512]{2,1,0:T(8,128)(2,1)} %merge_part.1), channel_id=1, replica_groups={{0,2,4,6,8,10,12,14},{1,3,5,7,9,11,13,15},{16,18,20,22,24,26,28,30},{17..., dimensions={0} | all-to-all | bytes 1048576 | tf_op jit(solution)/shard_map/all_to_all | solution.py:309
  75.5 0.0 copy-start
  75.5 0.0 collective-permute-start.1
  75.5 1.9 %collective-permute-done.1.oth_ref = bf16[8,64,512]{2,1,0:T(8,128)(2,1)S(1)} collective-permute-done((bf16[8,64,512]{2,1,0:T(8,128)(2,1)S(1)}, bf16[8,64,512]{2,1,0:T(8,128)(2,1)S(1)}, u32[]{:S(2)}, u32[]{:S(2)}) %collective-permute-start.1) | collective-permute-done | bytes 524320 | tf_op jit(solution)/shard_map/ppermute | solution.py:285
  77.4 0.0 copy-start.2
  77.4 0.0 copy-done
  77.4 0.8 copy-done.2
  78.2 7.5 %project.1 = f32[64,512]{1,0:T(8,128)} custom-call(s32[1]{0:T(128)} %bitcast.side_ref, bf16[8,64,512]{2,1,0:T(8,128)(2,1)} %copy-done, bf16[8,64,512]{2,1,0:T(8,128)(2,1)} %copy-done.2, bf16[8,2,512,512]{3,2,1,0:T(8,128)(2,1)} %bitcast.14, bf16[8,2,512,512]{3,2,1,0:T(8,128)(2,1)} %bitcast.15), custom_call_target="tpu_custom_call" | custom-call | tf_op jit(solution)/shard_map/project/pallas_call | solution.py:245
  85.7 0.9 reshape.27
  86.6 11.4 %all_to_all.22 = f32[16,4,512]{2,1,0:T(4,128)S(1)} all-to-all(f32[16,4,512]{2,1,0:T(4,128)S(1)} %reshape.27), channel_id=1, replica_groups=mesh['groups'=2,'seq'=16] {'seq'}, dimensions={0} | all-to-all | bytes 262144 | tf_op jit(solution)/shard_map/all_to_all | solution.py:315
  98.0 0.7 copy.18
Async XLA Ops:
  1.6 15.3 %all-to-all-start = ((bf16[16,4,1024]{2,1,0:T(4,128)(2,1)}), bf16[16,4,1024]{2,1,0:T(4,128)(2,1)S(1)}, u32[]{:S(2)}, u32[]{:S(2)}) async-start(bf16[16,4,1024]{2,1,0:T(4,128)(2,1)} %bitcast.3), calls=%async_computation | async-start | bytes 262144 | tf_op jit(solution)/shard_map/all_to_all | solution.py:290
  16.9 0.7 copy-start.1
  35.3 19.5 %collective-permute-start = (f32[256,256]{1,0:T(8,128)}, f32[256,256]{1,0:T(8,128)S(1)}, u32[]{:S(2)}, u32[]{:S(2)}) collective-permute-start(f32[256,256]{1,0:T(8,128)} %get-tuple-element.8), channel_id=1, source_target_pairs={{0,1},{1,0},{2,3},{3,2},{4,5},{5,4},{6,7},{7,6},{8,9},{9,8},{10,11... | collective-permute-start | bytes 786440 | tf_op jit(solution)/shard_map/ppermute | solution.py:285
  54.8 0.7 copy-start.3
  75.5 1.9 %copy-start = (bf16[8,64,512]{2,1,0:T(8,128)(2,1)}, bf16[8,64,512]{2,1,0:T(8,128)(2,1)S(1)}, u32[]{:S(2)}) copy-start(bf16[8,64,512]{2,1,0:T(8,128)(2,1)S(1)} %all_to_all.21.own_ref) | copy-start | bytes 1572868
  75.5 1.9 %collective-permute-start.1 = (bf16[8,64,512]{2,1,0:T(8,128)(2,1)S(1)}, bf16[8,64,512]{2,1,0:T(8,128)(2,1)S(1)}, u32[]{:S(2)}, u32[]{:S(2)}) collective-permute-start(bf16[8,64,512]{2,1,0:T(8,128)(2,1)S(1)} %all_to_all.21.own_ref), channel_id=1, source_target_pairs={{0,1},{1,0},{2,3},{3,2},{4,5},{5,4},{6,7},{7,6},{8,9},{9,8},{10,11... | collective-permute-start | bytes 1572872 | tf_op jit(solution)/shard_map/ppermute | solution.py:285
  77.4 0.8 copy-start.2

commit v2 on v1

--- a/solution.py
+++ b/solution.py
@@ -6,6 +6,7 @@
 from jax.experimental import pallas as pl
 from jax.experimental.pallas import tpu as pltpu
 from jax.sharding import PartitionSpec as P
+
 
 HEADS = 64
 KVH = 8
@@ -18,6 +19,45 @@
 NT = (((1,), (1,)), ((), ()))
 F32 = jnp.float32
 BF16 = jnp.bfloat16
+
+
+def in_hbm(array):
+    return pltpu.with_memory_space_constraint(array, pltpu.HBM)
+
+
+def on_chip(array):
+    return pltpu.with_memory_space_constraint(array, pltpu.VMEM)
+
+
+VMEM_SPEC = pl.BlockSpec(memory_space=pltpu.VMEM)
+SMEM_SPEC = pl.BlockSpec(memory_space=pltpu.SMEM)
+
+
+def spread_kernel(q_ref, out_ref, sems, *, blocks):
+    width = out_ref.shape[2]
+    moves = [
+        pltpu.make_async_copy(
+            q_ref.at[:, pl.ds((d // blocks) * width, width)], out_ref.at[d], sems.at[d]
+        )
+        for d in range(out_ref.shape[0])
+    ]
+    for move in moves:
+        move.start()
+    for move in moves:
+        move.wait()
+
+
+def spread(queries, seq, blocks):
+    rows = queries.shape[0]
+    return pl.pallas_call(
+        functools.partial(spread_kernel, blocks=blocks),
+        in_specs=[pl.BlockSpec(memory_space=pl.ANY)],
+        out_specs=pl.BlockSpec(memory_space=pl.ANY),
+        out_shape=jax.ShapeDtypeStruct((seq, rows, GROUP * HD), queries.dtype),
+        scratch_shapes=[pltpu.SemaphoreType.DMA((seq,))],
+        compiler_params=pltpu.CompilerParams(vmem_limit_bytes=4 << 20),
+        name="spread",
+    )(in_hbm(queries))
 
 
 def private_kernel(par_ref, len_ref, q_ref, dk_ref, dv_ref, k_ref, v_ref, out_ref, *, draft, blocks):
@@ -59,18 +99,14 @@
     mixture = mixture + jnp.dot(tree_w.astype(BF16), dval, preferred_element_type=F32)
     mixture = mixture / denom
     lse = peak + jnp.log(denom)
-    first = lse.astype(BF16).astype(F32)
-    second = (lse - first).astype(BF16).astype(F32)
-    third = lse - first - second
     stat_lane = lax.broadcasted_iota(jnp.int32, (draft, LANES), 1)
     for b in range(blocks):
         stats = jnp.zeros((draft, LANES), F32)
         for hh in range(heads):
             lo = (b * heads + hh) * draft
-            out_ref[b, :, hh * HD : (hh + 1) * HD] = mixture[lo : lo + draft].astype(BF16)
-            for t, term in enumerate((first, second, third)):
-                stats = jnp.where(stat_lane == 3 * hh + t, term[lo : lo + draft], stats)
-        out_ref[b, :, heads * HD :] = stats.astype(BF16)
+            out_ref[b, :, hh * HD : (hh + 1) * HD] = mixture[lo : lo + draft]
+            stats = jnp.where(stat_lane == hh, lse[lo : lo + draft], stats)
+        out_ref[b, :, heads * HD :] = stats
 
 
 def private_part(parents, lengths, queries, dkeys, dvals, pkeys, pvals, blocks):
@@ -91,12 +127,19 @@
             pl.BlockSpec((1, slots, HD), lambda g: (0, 0, g)),
         ],
         out_specs=pl.BlockSpec((blocks, draft, wide), lambda g: (g, 0, 0)),
-        out_shape=jax.ShapeDtypeStruct((KVH * blocks, draft, wide), BF16),
+        out_shape=jax.ShapeDtypeStruct((KVH * blocks, draft, wide), F32),
+        cost_estimate=pl.CostEstimate(
+            flops=4 * draft * HEADS * slots * HD,
+            transcendentals=draft * HEADS * slots,
+            bytes_accessed=4 * slots * KVH * HD,
+        ),
         name="private_part",
     )(parents, lengths, queries, dkeys, dvals, pkeys, pvals)
 
 
-def prefix_kernel(rank_ref, q_ref, k_ref, v_ref, keep_ref, send_ref, q32, qs, peak, denom, acc):
+def prefix_kernel(
+    rank_ref, q_ref, k_ref, v_ref, keep_ref, send_ref, q32, qs, peak, denom, acc, *, sub
+):
     step = pl.program_id(0)
     owners, draft, _ = q_ref.shape
     rows = owners * draft
@@ -111,25 +154,28 @@
         denom[...] = jnp.zeros(denom.shape, F32)
         acc[...] = jnp.zeros(acc.shape, F32)
 
-    scores = lax.dot_general(qs[...], k_ref[0], NT, preferred_element_type=F32)
-    tiles = scores.shape[1] // LANES
-    top = scores[:, :LANES]
-    for j in range(1, tiles):
-        top = jnp.maximum(top, scores[:, j * LANES : (j + 1) * LANES])
-    old = peak[...]
-    new = jnp.maximum(old, jnp.max(top, axis=1, keepdims=True) * (SCALE * LOG2E))
-    fade = jnp.exp2(old - new)
-    peak[...] = new
-    parts = [
-        jnp.exp2(scores[:, j * LANES : (j + 1) * LANES] * (SCALE * LOG2E) - new)
-        for j in range(tiles)
-    ]
-    total = parts[0]
-    for part in parts[1:]:
-        total = total + part
-    denom[...] = denom[...] * fade + total
-    weights = jnp.concatenate([part.astype(BF16) for part in parts], axis=1)
-    acc[...] = acc[...] * fade + jnp.dot(weights, v_ref[0], preferred_element_type=F32)
+    span = k_ref.shape[1]
+    count = span // sub
+
+    def score(b):
+        block = k_ref[0, b * sub : (b + 1) * sub, :]
+        return lax.dot_general(qs[...], block, NT, preferred_element_type=F32)
+
+    top, total, mixed = peak[...], denom[...], acc[...]
+    scores = score(0)
+    for b in range(count):
+        ahead = score(b + 1) if b + 1 < count else None
+        tiles = [scores[:, j : j + LANES] for j in range(0, sub, LANES)]
+        block_top = functools.reduce(jnp.maximum, tiles)
+        new = jnp.maximum(top, jnp.max(block_top, axis=1, keepdims=True) * (SCALE * LOG2E))
+        fade = jnp.exp2(top - new)
+        parts = [jnp.exp2(tile * (SCALE * LOG2E) - new) for tile in tiles]
+        total = total * fade + functools.reduce(jnp.add, parts)
+        weights = jnp.concatenate([part.astype(BF16) for part in parts], axis=1)
+        block = v_ref[0, b * sub : (b + 1) * sub, :]
+        mixed = mixed * fade + jnp.dot(weights, block, preferred_element_type=F32)
+        top, scores = new, ahead
+    peak[...], denom[...], acc[...] = top, total, mixed
 
     @pl.when(step == pl.num_programs(0) - 1)
     def _():
@@ -145,12 +191,12 @@
         send_ref[:, HD:] = denom[pl.ds(other, half), :]
 
 
-def prefix_part(side, queries, keys, values, span):
+def prefix_part(side, queries, keys, values, span, sub):
     owners, draft, _ = queries.shape
     rows = owners * draft * GROUP
     shape = jax.ShapeDtypeStruct((rows // 2, HD + LANES), F32)
     return pl.pallas_call(
-        prefix_kernel,
+        functools.partial(prefix_kernel, sub=sub),
         grid_spec=pltpu.PrefetchScalarGridSpec(
             num_scalar_prefetch=1,
             grid=(keys.shape[1] // span,),
@@ -172,8 +218,14 @@
             ],
         ),
         out_shape=[shape, shape],
+        compiler_params=pltpu.CompilerParams(vmem_limit_bytes=32 << 20),
+        cost_estimate=pl.CostEstimate(
+            flops=4 * rows * keys.shape[1] * HD,
+            transcendentals=rows * keys.shape[1],
+            bytes_accessed=4 * keys.shape[1] * HD,
+        ),
         name="prefix_part",
-    )(side, queries, keys, values)
+    )(side, queries, in_hbm(keys), in_hbm(values))
 
 
 def join(first, second):
@@ -188,16 +240,17 @@
     )
 
 
-def merge_kernel(mine_ref, other_ref, priv_ref, att_ref, p32):
+def merge_kernel(side_ref, mine_ref, other_ref, priv_ref, w_ref, att_ref, wide_ref, p32, sem):
+    fetch = pltpu.make_async_copy(w_ref.at[:, side_ref[0]], wide_ref, sem)
+    fetch.start()
     owners, draft, wide = priv_ref.shape
     rows = owners * draft
     heads = (wide - LANES) // HD
     for s in range(owners):
-        p32[s * draft : (s + 1) * draft, :] = priv_ref[s].astype(F32)
+        p32[s * draft : (s + 1) * draft, :] = priv_ref[s]
     for h in range(heads):
         part = slice(h * rows, (h + 1) * rows)
-        col = heads * HD + 3 * h
-        lse_p = (p32[:, col : col + 1] + p32[:, col + 1 : col + 2]) + p32[:, col + 2 : col + 3]
+        lse_p = p32[:, heads * HD + h : heads * HD + h + 1]
         lse_a = mine_ref[part, HD:]
         lse_b = other_ref[part, HD:]
         top = jnp.maximum(jnp.maximum(lse_a, lse_b), lse_p)
@@ -212,52 +265,86 @@
         mixed = mixed.astype(BF16)
         for copy in range(att_ref.shape[0]):
             att_ref[copy, :, h * HD : (h + 1) * HD] = mixed
-
-
-def merge_part(mine, other, priv, copies):
+    fetch.wait()
+
+
+def merge_part(side, mine, other, priv, weight):
     owners, draft, wide = priv.shape
+    chips, _, deep, cols = weight.shape
     return pl.pallas_call(
         merge_kernel,
-        out_shape=jax.ShapeDtypeStruct((copies, owners * draft, wide - LANES), BF16),
-        scratch_shapes=[pltpu.VMEM((owners * draft, wide), F32)],
+        in_specs=[SMEM_SPEC, VMEM_SPEC, VMEM_SPEC, VMEM_SPEC, pl.BlockSpec(memory_space=pl.ANY)],
+        out_specs=[VMEM_SPEC, VMEM_SPEC],
+        out_shape=[
+            pltpu.VMEM((chips, owners * draft, wide - LANES), BF16),
+            pltpu.VMEM((chips, deep, cols), BF16),
+        ],
+        scratch_shapes=[pltpu.VMEM((owners * draft, wide), F32), pltpu.SemaphoreType.DMA],
+        compiler_params=pltpu.CompilerParams(vmem_limit_bytes=8 << 20),
+        cost_estimate=pl.CostEstimate(
+            flops=8 * mine.size, transcendentals=mine.size, bytes_accessed=2 * chips * deep * cols
+        ),
         name="merge_part",
-    )(mine, other, priv)
-
-
-def project_kernel(side_ref, own_ref, oth_ref, wo_ref, wp_ref, out_ref):
-    step = pl.program_id(0)
-    part = jnp.dot(own_ref[0], wo_ref[0, 0], preferred_element_type=F32)
-    part = part + jnp.dot(oth_ref[0], wp_ref[0, 0], preferred_element_type=F32)
-
-    @pl.when(step == 0)
-    def _():
-        out_ref[...] = part
-
-    @pl.when(step > 0)
-    def _():
-        out_ref[...] = out_ref[...] + part
-
-
-def project(side, own, oth, weight):
-    chips, rows, deep = own.shape
-    cols = weight.shape[1]
-    split = weight.reshape(chips, 2, deep, cols)
-    return pl.pallas_call(
-        project_kernel,
-        grid_spec=pltpu.PrefetchScalarGridSpec(
-            num_scalar_prefetch=1,
-            grid=(chips,),
-            in_specs=[
-                pl.BlockSpec((1, rows, deep), lambda i, r: (i, 0, 0)),
-                pl.BlockSpec((1, rows, deep), lambda i, r: (i, 0, 0)),
-                pl.BlockSpec((1, 1, deep, cols), lambda i, r: (i, r[0], 0, 0)),
-                pl.BlockSpec((1, 1, deep, cols), lambda i, r: (i, 1 - r[0], 0, 0)),
-            ],
-            out_specs=pl.BlockSpec((rows, cols), lambda i, r: (0, 0)),
-        ),
-        out_shape=jax.ShapeDtypeStruct((rows, cols), F32),
-        name="project",
-    )(side, own, oth, split, split)
+    )(side, on_chip(mine), on_chip(other), on_chip(priv), in_hbm(weight))
+
+
+def matmuls(att_ref, wide_ref):
+    return functools.reduce(
+        jnp.add,
+        [
+            jnp.dot(att_ref[i], wide_ref[i], preferred_element_type=F32)
+            for i in range(att_ref.shape[0])
+        ],
+    )
+
+
+def first_kernel(side_ref, att_ref, wide_ref, w_ref, out_ref, next_ref, sem):
+    fetch = pltpu.make_async_copy(w_ref.at[:, 1 - side_ref[0]], next_ref, sem)
+    fetch.start()
+    out_ref[...] = matmuls(att_ref, wide_ref)
+    fetch.wait()
+
+
+def second_kernel(part_ref, att_ref, wide_ref, out_ref):
+    total = part_ref[...] + matmuls(att_ref, wide_ref)
+    owners, draft, _ = out_ref.shape
+    for s in range(owners):
+        out_ref[s] = total[s * draft : (s + 1) * draft].astype(BF16)
+
+
+def project_own(side, att, wide, weight):
+    chips, rows, deep = att.shape
+    cols = weight.shape[3]
+    return pl.pallas_call(
+        first_kernel,
+        in_specs=[SMEM_SPEC, VMEM_SPEC, VMEM_SPEC, pl.BlockSpec(memory_space=pl.ANY)],
+        out_specs=[VMEM_SPEC, VMEM_SPEC],
+        out_shape=[pltpu.VMEM((rows, cols), F32), pltpu.VMEM((chips, deep, cols), BF16)],
+        scratch_shapes=[pltpu.SemaphoreType.DMA],
+        compiler_params=pltpu.CompilerParams(vmem_limit_bytes=8 << 20),
+        cost_estimate=pl.CostEstimate(
+            flops=2 * rows * deep * chips * cols,
+            transcendentals=0,
+            bytes_accessed=2 * deep * chips * cols,
+        ),
+        name="project_own",
+    )(side, on_chip(att), on_chip(wide), in_hbm(weight))
+
+
+def project_twin(part, att, wide, owners):
+    chips, rows, deep = att.shape
+    cols = wide.shape[2]
+    return pl.pallas_call(
+        second_kernel,
+        in_specs=[VMEM_SPEC, VMEM_SPEC, VMEM_SPEC],
+        out_specs=VMEM_SPEC,
+        out_shape=pltpu.VMEM((owners, rows // owners, cols), BF16),
+        compiler_params=pltpu.CompilerParams(vmem_limit_bytes=8 << 20),
+        cost_estimate=pl.CostEstimate(
+            flops=2 * rows * deep * chips * cols, transcendentals=0, bytes_accessed=0
+        ),
+        name="project_twin",
+    )(on_chip(part), on_chip(att), on_chip(wide))
 
 
 def shards(
@@ -284,9 +371,7 @@
     def from_partner(array, bit):
         return lax.ppermute(array, "seq", [(i, i ^ 1 << bit) for i in range(seq)])
 
-    by_group = queries.reshape(own_rows, KVH, GROUP * HD).transpose(1, 0, 2)
-    ask = jnp.broadcast_to(by_group[:, None], (KVH, blocks, own_rows, GROUP * HD))
-    ask = ask.reshape(seq, own_rows, GROUP * HD)
+    ask = spread(queries, seq, blocks)
     every_query = lax.all_to_all(ask, "seq", split_axis=0, concat_axis=0, tiled=True)
 
     told = private_part(
@@ -294,8 +379,10 @@
     )
     priv = lax.all_to_all(told, "seq", split_axis=0, concat_axis=0, tiled=True)
 
-    span = min(1024, prefix_keys.shape[1])
-    mine, gone = prefix_part(side, every_query, prefix_keys, prefix_values, span)
+    span = min(4096, prefix_keys.shape[1])
+    mine, gone = prefix_part(
+        side, every_query, prefix_keys, prefix_values, span, span // 4
+    )
     other = from_partner(gone, top_bit)
     for level in range(top_bit - 1, -1, -1):
         held = join(mine, other)
@@ -305,15 +392,16 @@
         other = from_partner(lax.dynamic_slice_in_dim(held, (1 - at) * half, half, 0), level)
 
     members = [list(range(c, seq, 2)) for c in range(2)]
-    copies = merge_part(mine, other, priv, seq // 2)
+    weight = out_weight.reshape(seq // 2, 2, -1, out_weight.shape[1])
+    copies, wide = merge_part(parity, mine, other, priv, weight)
     same = lax.all_to_all(
         copies, "seq", split_axis=0, concat_axis=0, axis_index_groups=members, tiled=True
     )
     twin = from_partner(same, 0)
-    columns = project(parity, same, twin, out_weight)
-    pieces = columns.reshape(seq, own_rows, columns.shape[1])
+    part, wide = project_own(parity, same, wide, weight)
+    pieces = project_twin(part, twin, wide, seq)
     done = lax.all_to_all(pieces, "seq", split_axis=0, concat_axis=0, tiled=True)
-    return done.transpose(1, 0, 2).reshape(own_rows, seq * columns.shape[1])
+    return done.transpose(1, 0, 2).reshape(own_rows, -1).astype(F32)
 
 
 def solution(mesh):
@@ -330,4 +418,5 @@
         P(None, "seq"),
     )
     out_specs = P(("groups", "seq"), None)
+
     return jax.shard_map(shards, mesh=mesh, in_specs=in_specs, out_specs=out_specs, check_vma=False)

time: 99.7 us -> 78.9 us (0.79)
  blocking collectives: 40.5 us -> 31 us
  waiting for transfers between devices: 9.8 us -> 1.17 us
  starting transfers between devices: 7.42 us -> 13.9 us
  local copies, waits for them, and re-layouts: 5.37 us -> 0 us
  Pallas kernels: 34.9 us -> 30.9 us
    all_to_all x1 -> x0, blocking collectives: 11.3 us -> none  [shards(): priv = lax.all_to_all(told, 'seq', split_axis=0, concat_axis=0, tiled=True)]
    all_to_all x1, waiting for transfers between devices: 7.89 us -> 0.01 us  [shards(): lax.all_to_all(ask, 'seq', split_axis=0, concat_axis=0, tiled=True)]
    all_to_all x0 -> x1, starting transfers between devices: none -> 6 us  [shards(): priv = lax.all_to_all(told, 'seq', split_axis=0, concat_axis=0, tiled=True)]
    pallas_call x3 -> x5, Pallas kernels: 27.4 us -> 23.4 us  [the longest x1 12.9 us: prefix_part(): pl.pallas_call(functools.partial(prefix_kernel, sub=sub), grid_spec=pltpu...]
    unnamed x10 -> x0, local copies, waits for them, and re-layouts: 3.67 us -> none
    all_to_all x1, blocking collectives: 17.9 us -> 20.5 us  [shards(): lax.all_to_all(copies, 'seq', split_axis=0, concat_axis=0, axis_index_gro...]
  transfers between devices with their start and end apart: 3 -> 4, of which waited for: 2 -> 1; matrix products, arithmetic and copies ran while one was open for 0% -> 0% of each run, Pallas kernels for 8% -> 29%
where the time goes in v2:
time: 78.9 us; the launch traced here: 78.4 us
  blocking collectives  31 us (39%)
  Pallas kernels  30.9 us (39%)
  starting transfers between devices  13.9 us (18%)
  waiting for transfers between devices  1.17 us (1%)
    all_to_all x1, blocking collectives, shards(): lax.all_to_all(copies, 'seq', split_axis=0, concat_axis=0, axis_index_gro...  20.5 us
    pallas_call x1, Pallas kernels, prefix_part(): pl.pallas_call(functools.partial(prefix_kernel, sub=sub), grid_spec=pltpu...  12.9 us
    all_to_all x1, blocking collectives, shards(): lax.all_to_all(pieces, 'seq', split_axis=0, concat_axis=0, tiled=True)  10.5 us
    pallas_call x1, Pallas kernels, private_part(): pl.pallas_call(functools.partial(private_kernel, draft=draft, blocks=bloc...  7.54 us
    all_to_all x1, starting transfers between devices, shards(): lax.all_to_all(ask, 'seq', split_axis=0, concat_axis=0, tiled=True)  7.43 us
    all_to_all x1, starting transfers between devices, shards(): priv = lax.all_to_all(told, 'seq', split_axis=0, concat_axis=0, tiled=True)  6 us
    pallas_call x1, Pallas kernels, spread(): pl.pallas_call(functools.partial(spread_kernel, blocks=blocks), in_specs=...  5.22 us
    pallas_call x1, Pallas kernels, merge_part(): pl.pallas_call(merge_kernel, in_specs=[SMEM_SPEC, VMEM_SPEC, VMEM_SPEC, V...  2.22 us
  transfers between devices with their start and end apart: 4, of which 1 were waited for; matrix products, arithmetic and copies ran while one was open for 0% of the time, Pallas kernels for 29%

profile of v2, /device:TPU:0, one launch (start us, length us, event | category | flops | bytes accessed | tf_op | source)
XLA Modules:
  0.0 78.4 jit_solution(12663622123598577461)
XLA Ops:
  0.0 5.2 %spread.1 = bf16[16,4,1024]{2,1,0:T(4,128)(2,1)} custom-call(bf16[4,8192]{1,0:T(4,128)(2,1)} %q_ref.3), custom_call_target="tpu_custom_call" | custom-call | tf_op jit(solution)/shard_map/spread/pallas_call | solution.py:52
  5.2 7.4 %all-to-all-start = ((bf16[16,4,1024]{2,1,0:T(4,128)(2,1)}), bf16[16,4,1024]{2,1,0:T(4,128)(2,1)S(1)}, u32[]{:S(2)}, u32[]{:S(2)}) async-start(bf16[16,4,1024]{2,1,0:T(4,128)(2,1)} %spread.1), calls=%async_computation | async-start | bytes 262144 | tf_op jit(solution)/shard_map/all_to_all | solution.py:375
  13.3 7.5 %private_part.1 = f32[16,4,640]{2,1,0:T(4,128)} custom-call(s32[4]{0:T(128)} %par_ref.1, s32[1]{0:T(128)S(6)} %copy.11.len_ref, bf16[4,8192]{1,0:T(4,128)(2,1)} %q_ref.3, bf16[4,1024]{1,0:T(4,128)(2,1)} %dk_ref.1, bf16[4,1024]{1,0:T(4,128)(2,1)} %dv_ref.1, bf16[1,1024,1024]{2,1,0:T(8,128)(2,1)} %k_ref.3, bf16[1,1024,1024]{2,1,0:T(8,128)(2,1)} %v_ref.3), custom_call_target="tpu_custom_call" | custom-call | flops 134217728 | bytes 4194304 | tf_op jit(solution)/shard_map/private_part/pallas_call | solution.py:117
  20.9 0.0 all-to-all-done.q_ref
  20.9 6.0 %all-to-all-start.1 = ((f32[16,4,640]{2,1,0:T(4,128)}), f32[16,4,640]{2,1,0:T(4,128)S(1)}, u32[]{:S(2)}, u32[]{:S(2)}) async-start(f32[16,4,640]{2,1,0:T(4,128)} %private_part.1), calls=%async_computation.1 | async-start | bytes 327680 | tf_op jit(solution)/shard_map/all_to_all | solution.py:380
  26.9 12.9 %prefix_part.1 = (f32[256,256]{1,0:T(8,128)S(1)}, f32[256,256]{1,0:T(8,128)S(1)}) custom-call(s32[1]{0:T(128)} %bitcast.1.rank_ref, bf16[16,4,1024]{2,1,0:T(4,128)(2,1)S(1)} %all-to-all-done.q_ref, bf16[1,16384,128]{2,1,0:T(8,128)(2,1)} %k_ref.2, bf16[1,16384,128]{2,1,0:T(8,128)(2,1)} %v_ref.2), custom_call_target="tpu_custom_call" | custom-call | flops 4294967296 | bytes 8388608 | tf_op jit(solution)/shard_map/prefix_part/pallas_call | solution.py:198
  39.7 0.5 collective-permute-start
  40.2 0.0 all-to-all-done.1.priv_ref
  40.2 1.2 %collective-permute-done.other_ref = f32[256,256]{1,0:T(8,128)S(1)} collective-permute-done((f32[256,256]{1,0:T(8,128)S(1)}, f32[256,256]{1,0:T(8,128)S(1)}, u32[]{:S(2)}, u32[]{:S(2)}) %collective-permute-start) | collective-permute-done | bytes 262176 | tf_op jit(solution)/shard_map/ppermute | solution.py:372
  41.4 2.2 %merge_part.1 = (bf16[8,64,512]{2,1,0:T(8,128)(2,1)S(1)}, bf16[8,512,512]{2,1,0:T(8,128)(2,1)S(1)}) custom-call(s32[1]{0:T(128)} %bitcast.side_ref, f32[256,256]{1,0:T(8,128)S(1)} %get-tuple-element.11.mine_ref, f32[256,256]{1,0:T(8,128)S(1)} %collective-permute-done.other_ref, f32[16,4,640]{2,1,0:T(4,128)S(1)} %all-to-all-done.1.priv_ref, ...), custom_call_target="tpu_custom_call" | custom-call | flops 524288 | bytes 4194304 | tf_op jit(solution)/shard_map/merge_part/pallas_call | solution.py:274
  43.6 20.5 %all_to_all.20.att_ref = bf16[8,64,512]{2,1,0:T(8,128)(2,1)S(1)} all-to-all(bf16[8,64,512]{2,1,0:T(8,128)(2,1)S(1)} %get-tuple-element.13), channel_id=1, replica_groups={{0,2,4,6,8,10,12,14},{1,3,5,7,9,11,13,15},{16,18,20,22,24,26,28,30},{17..., dimensions={0} | all-to-all | bytes 1048576 | tf_op jit(solution)/shard_map/all_to_all | solution.py:397
  64.1 0.0 collective-permute-start.1
  64.1 2.2 %project_own.1 = (f32[64,512]{1,0:T(8,128)S(1)}, bf16[8,512,512]{2,1,0:T(8,128)(2,1)S(1)}) custom-call(s32[1]{0:T(128)} %bitcast.side_ref, bf16[8,64,512]{2,1,0:T(8,128)(2,1)S(1)} %all_to_all.20.att_ref, bf16[8,512,512]{2,1,0:T(8,128)(2,1)S(1)} %get-tuple-element.14.wide_ref, bf16[8,2,512,512]{3,2,1,0:T(8,128)(2,1)} %bitcast.7), custom_call_target="tpu_custom_call" | custom-call | flops 268435456 | bytes 4194304 | tf_op jit(solution)/shard_map/project_own/pallas_call | solution.py:318
  66.3 0.0 collective-permute-done.1.att_ref
  66.3 0.8 %project_twin.1 = bf16[16,4,512]{2,1,0:T(4,128)(2,1)S(1)} custom-call(f32[64,512]{1,0:T(8,128)S(1)} %get-tuple-element.15.part_ref, bf16[8,64,512]{2,1,0:T(8,128)(2,1)S(1)} %collective-permute-done.1.att_ref, bf16[8,512,512]{2,1,0:T(8,128)(2,1)S(1)} %get-tuple-element.16.wide_ref), custom_call_target="tpu_custom_call" | custom-call | flops 268435456 | tf_op jit(solution)/shard_map/project_twin/pallas_call | solution.py:337
  67.1 10.5 %all_to_all.21 = bf16[16,4,512]{2,1,0:T(4,128)(2,1)S(1)} all-to-all(bf16[16,4,512]{2,1,0:T(4,128)(2,1)S(1)} %project_twin.1), channel_id=1, replica_groups=mesh['groups'=2,'seq'=16] {'seq'}, dimensions={0} | all-to-all | bytes 131072 | tf_op jit(solution)/shard_map/all_to_all | solution.py:403
  77.7 0.7 convert_element_type.13
Async XLA Ops:
  5.2 15.6 %all-to-all-start = ((bf16[16,4,1024]{2,1,0:T(4,128)(2,1)}), bf16[16,4,1024]{2,1,0:T(4,128)(2,1)S(1)}, u32[]{:S(2)}, u32[]{:S(2)}) async-start(bf16[16,4,1024]{2,1,0:T(4,128)(2,1)} %spread.1), calls=%async_computation | async-start | bytes 262144 | tf_op jit(solution)/shard_map/all_to_all | solution.py:375
  20.9 19.4 %all-to-all-start.1 = ((f32[16,4,640]{2,1,0:T(4,128)}), f32[16,4,640]{2,1,0:T(4,128)S(1)}, u32[]{:S(2)}, u32[]{:S(2)}) async-start(f32[16,4,640]{2,1,0:T(4,128)} %private_part.1), calls=%async_computation.1 | async-start | bytes 327680 | tf_op jit(solution)/shard_map/all_to_all | solution.py:380
  39.7 1.6 %collective-permute-start = (f32[256,256]{1,0:T(8,128)S(1)}, f32[256,256]{1,0:T(8,128)S(1)}, u32[]{:S(2)}, u32[]{:S(2)}) collective-permute-start(f32[256,256]{1,0:T(8,128)S(1)} %get-tuple-element.12), channel_id=1, source_target_pairs={{0,1},{1,0},{2,3},{3,2},{4,5},{5,4},{6,7},{7,6},{8,9},{9,8},{10,11... | collective-permute-start | bytes 786440 | tf_op jit(solution)/shard_map/ppermute | solution.py:372
  64.1 2.2 %collective-permute-start.1 = (bf16[8,64,512]{2,1,0:T(8,128)(2,1)S(1)}, bf16[8,64,512]{2,1,0:T(8,128)(2,1)S(1)}, u32[]{:S(2)}, u32[]{:S(2)}) collective-permute-start(bf16[8,64,512]{2,1,0:T(8,128)(2,1)S(1)} %all_to_all.20.att_ref), channel_id=1, source_target_pairs={{0,1},{1,0},{2,3},{3,2},{4,5},{5,4},{6,7},{7,6},{8,9},{9,8},{10,11... | collective-permute-start | bytes 1572872 | tf_op jit(solution)/shard_map/ppermute | solution.py:372

commit v3 on v2

--- a/solution.py
+++ b/solution.py
@@ -33,44 +33,12 @@
 SMEM_SPEC = pl.BlockSpec(memory_space=pltpu.SMEM)
 
 
-def spread_kernel(q_ref, out_ref, sems, *, blocks):
-    width = out_ref.shape[2]
-    moves = [
-        pltpu.make_async_copy(
-            q_ref.at[:, pl.ds((d // blocks) * width, width)], out_ref.at[d], sems.at[d]
-        )
-        for d in range(out_ref.shape[0])
-    ]
-    for move in moves:
-        move.start()
-    for move in moves:
-        move.wait()
-
-
-def spread(queries, seq, blocks):
-    rows = queries.shape[0]
-    return pl.pallas_call(
-        functools.partial(spread_kernel, blocks=blocks),
-        in_specs=[pl.BlockSpec(memory_space=pl.ANY)],
-        out_specs=pl.BlockSpec(memory_space=pl.ANY),
-        out_shape=jax.ShapeDtypeStruct((seq, rows, GROUP * HD), queries.dtype),
-        scratch_shapes=[pltpu.SemaphoreType.DMA((seq,))],
-        compiler_params=pltpu.CompilerParams(vmem_limit_bytes=4 << 20),
-        name="spread",
-    )(in_hbm(queries))
-
-
-def private_kernel(par_ref, len_ref, q_ref, dk_ref, dv_ref, k_ref, v_ref, out_ref, *, draft, blocks):
+def private_kernel(
+    par_ref, len_ref, q_ref, dk_ref, dv_ref, k_ref, v_ref, out_ref, ask_ref, *, draft, blocks, batch
+):
     heads = GROUP // blocks
     rows = GROUP * draft
     slots = k_ref.shape[1]
-    q32 = q_ref[...].astype(F32)
-    query = jnp.concatenate(
-        [q32[:, h * HD : (h + 1) * HD] for h in range(GROUP)], axis=0
-    ).astype(BF16)
-    live = lax.broadcasted_iota(jnp.int32, (rows, slots), 1) < len_ref[0]
-    scores = lax.dot_general(query, k_ref[0], NT, preferred_element_type=F32) * SCALE
-    scores = jnp.where(live, scores, NEG)
     seen = []
     for i in range(draft):
         bits = jnp.int32(1 << i)
@@ -79,55 +47,78 @@
         seen.append(bits)
     row = lax.broadcasted_iota(jnp.int32, (rows, LANES), 0) % draft
     lane = lax.broadcasted_iota(jnp.int32, (rows, LANES), 1)
-    shown = lane < 0
+    mask = jnp.zeros((rows, LANES), jnp.int32)
     for i in range(draft):
-        for j in range(i + 1):
-            hit = (seen[i] >> j) & 1
-            shown = shown | ((row == i) & (lane == j) & (hit == 1))
+        mask = jnp.where(row == i, seen[i], mask)
+    shown = (lane < draft) & ((lax.shift_right_logical(mask, jnp.minimum(lane, 31)) & 1) == 1)
+    live = lax.broadcasted_iota(jnp.int32, (rows, slots), 1) < len_ref[0]
     fill = jnp.zeros((LANES - draft, HD), F32)
-    dkey = jnp.concatenate([dk_ref[...].astype(F32), fill], axis=0).astype(BF16)
-    dval = jnp.concatenate([dv_ref[...].astype(F32), fill], axis=0).astype(BF16)
-    tree = lax.dot_general(query, dkey, NT, preferred_element_type=F32) * SCALE
-    tree = jnp.where(shown, tree, NEG)
-    peak = jnp.maximum(
-        jnp.max(scores, axis=1, keepdims=True), jnp.max(tree, axis=1, keepdims=True)
-    )
-    weights = jnp.exp(scores - peak)
-    tree_w = jnp.exp(tree - peak)
-    denom = jnp.sum(weights, axis=1, keepdims=True) + jnp.sum(tree_w, axis=1, keepdims=True)
-    mixture = jnp.dot(weights.astype(BF16), v_ref[0], preferred_element_type=F32)
-    mixture = mixture + jnp.dot(tree_w.astype(BF16), dval, preferred_element_type=F32)
-    mixture = mixture / denom
-    lse = peak + jnp.log(denom)
     stat_lane = lax.broadcasted_iota(jnp.int32, (draft, LANES), 1)
-    for b in range(blocks):
-        stats = jnp.zeros((draft, LANES), F32)
-        for hh in range(heads):
-            lo = (b * heads + hh) * draft
-            out_ref[b, :, hh * HD : (hh + 1) * HD] = mixture[lo : lo + draft]
-            stats = jnp.where(stat_lane == hh, lse[lo : lo + draft], stats)
-        out_ref[b, :, heads * HD :] = stats
-
-
-def private_part(parents, lengths, queries, dkeys, dvals, pkeys, pvals, blocks):
+    groups = range(batch)
+    wide = GROUP * HD
+    queries = []
+    for g in groups:
+        q = q_ref[:, g * wide : (g + 1) * wide]
+        for b in range(blocks):
+            ask_ref[g * blocks + b] = q
+        q32 = q.astype(F32)
+        queries.append(
+            jnp.concatenate([q32[:, h * HD : (h + 1) * HD] for h in range(GROUP)], axis=0).astype(BF16)
+        )
+    cols = [slice(g * HD, (g + 1) * HD) for g in groups]
+    scores = [
+        lax.dot_general(queries[g], k_ref[0, :, cols[g]], NT, preferred_element_type=F32) for g in groups
+    ]
+    trees = []
+    for g in groups:
+        dkey = jnp.concatenate([dk_ref[:, cols[g]].astype(F32), fill], axis=0).astype(BF16)
+        trees.append(lax.dot_general(queries[g], dkey, NT, preferred_element_type=F32))
+    for g in groups:
+        score = jnp.where(live, scores[g] * SCALE, NEG)
+        tree = jnp.where(shown, trees[g] * SCALE, NEG)
+        tiles = [score[:, j : j + LANES] for j in range(0, slots, LANES)] + [tree]
+        peak = jnp.max(functools.reduce(jnp.maximum, tiles), axis=1, keepdims=True)
+        tiles = [jnp.exp(tile - peak) for tile in tiles]
+        denom = jnp.sum(functools.reduce(jnp.add, tiles), axis=1, keepdims=True)
+        weights = jnp.concatenate([tile.astype(BF16) for tile in tiles[:-1]], axis=1)
+        dval = jnp.concatenate([dv_ref[:, cols[g]].astype(F32), fill], axis=0).astype(BF16)
+        mixture = jnp.dot(weights, v_ref[0, :, cols[g]], preferred_element_type=F32)
+        mixture = mixture + jnp.dot(tiles[-1].astype(BF16), dval, preferred_element_type=F32)
+        mixture = mixture / denom
+        lse = peak + jnp.log(denom)
+        for b in range(blocks):
+            stats = jnp.zeros((draft, LANES), F32)
+            for hh in range(heads):
+                lo = (b * heads + hh) * draft
+                out_ref[g * blocks + b, :, hh * HD : (hh + 1) * HD] = mixture[lo : lo + draft]
+                stats = jnp.where(stat_lane == hh, lse[lo : lo + draft], stats)
+            out_ref[g * blocks + b, :, heads * HD :] = stats
+
+
+def private_part(parents, lengths, queries, dkeys, dvals, pkeys, pvals, blocks, batch):
     draft = queries.shape[0]
     slots = pkeys.shape[1]
     wide = (GROUP // blocks) * HD + LANES
-    smem = pl.BlockSpec(memory_space=pltpu.SMEM)
     return pl.pallas_call(
-        functools.partial(private_kernel, draft=draft, blocks=blocks),
-        grid=(KVH,),
+        functools.partial(private_kernel, draft=draft, blocks=blocks, batch=batch),
+        grid=(KVH // batch,),
         in_specs=[
-            smem,
-            smem,
-            pl.BlockSpec((draft, GROUP * HD), lambda g: (0, g)),
-            pl.BlockSpec((draft, HD), lambda g: (0, g)),
-            pl.BlockSpec((draft, HD), lambda g: (0, g)),
-            pl.BlockSpec((1, slots, HD), lambda g: (0, 0, g)),
-            pl.BlockSpec((1, slots, HD), lambda g: (0, 0, g)),
+            SMEM_SPEC,
+            SMEM_SPEC,
+            pl.BlockSpec((draft, batch * GROUP * HD), lambda g: (0, g)),
+            pl.BlockSpec((draft, batch * HD), lambda g: (0, g)),
+            pl.BlockSpec((draft, batch * HD), lambda g: (0, g)),
+            pl.BlockSpec((1, slots, batch * HD), lambda g: (0, 0, g)),
+            pl.BlockSpec((1, slots, batch * HD), lambda g: (0, 0, g)),
         ],
-        out_specs=pl.BlockSpec((blocks, draft, wide), lambda g: (g, 0, 0)),
-        out_shape=jax.ShapeDtypeStruct((KVH * blocks, draft, wide), F32),
+        out_specs=[
+            pl.BlockSpec((batch * blocks, draft, wide), lambda g: (g, 0, 0)),
+            pl.BlockSpec((batch * blocks, draft, GROUP * HD), lambda g: (g, 0, 0)),
+        ],
+        out_shape=[
+            jax.ShapeDtypeStruct((KVH * blocks, draft, wide), F32),
+            jax.ShapeDtypeStruct((KVH * blocks, draft, GROUP * HD), BF16),
+        ],
         cost_estimate=pl.CostEstimate(
             flops=4 * draft * HEADS * slots * HD,
             transcendentals=draft * HEADS * slots,
@@ -371,12 +362,18 @@
     def from_partner(array, bit):
         return lax.ppermute(array, "seq", [(i, i ^ 1 << bit) for i in range(seq)])
 
-    ask = spread(queries, seq, blocks)
+    told, ask = private_part(
+        parents,
+        priv_lengths,
+        queries,
+        draft_keys,
+        draft_values,
+        in_hbm(private_keys),
+        in_hbm(private_values),
+        blocks,
+        KVH // 2,
+    )
     every_query = lax.all_to_all(ask, "seq", split_axis=0, concat_axis=0, tiled=True)
-
-    told = private_part(
-        parents, priv_lengths, queries, draft_keys, draft_values, private_keys, private_values, blocks
-    )
     priv = lax.all_to_all(told, "seq", split_axis=0, concat_axis=0, tiled=True)
 
     span = min(4096, prefix_keys.shape[1])

time: 78.9 us -> 75.4 us (0.956)
  Pallas kernels: 30.9 us -> 22.1 us
  waiting for transfers between devices: 1.17 us -> 9.15 us
  starting transfers between devices: 13.9 us -> 11.3 us
    all_to_all x1, waiting for transfers between devices: 0.01 us -> 7.89 us  [shards(): lax.all_to_all(ask, 'seq', split_axis=0, concat_axis=0, tiled=True)]
    pallas_call x1 -> x0, Pallas kernels: 5.22 us -> none  [spread(): pl.pallas_call(functools.partial(spread_kernel, blocks=blocks), in_specs=...]
    pallas_call x1, Pallas kernels: 7.54 us -> 4 us  [private_part(): pl.pallas_call(functools.partial(private_kernel, draft=draft, blocks=bloc...]
    all_to_all x1, starting transfers between devices: 6 us -> 3.52 us  [shards(): priv = lax.all_to_all(told, 'seq', split_axis=0, concat_axis=0, tiled=True)]
  transfers between devices with their start and end apart: 4 -> 4, of which waited for: 1 -> 2; matrix products, arithmetic and copies ran while one was open for 0% -> 0% of each run, Pallas kernels for 29% -> 20%
where the time goes in v3:
time: 75.4 us; the launch traced here: 75 us
  blocking collectives  31 us (41%)
  Pallas kernels  22.1 us (29%)
  starting transfers between devices  11.3 us (15%)
  waiting for transfers between devices  9.15 us (12%)
    all_to_all x1, blocking collectives, shards(): lax.all_to_all(copies, 'seq', split_axis=0, concat_axis=0, axis_index_gro...  20.4 us
    pallas_call x1, Pallas kernels, prefix_part(): pl.pallas_call(functools.partial(prefix_kernel, sub=sub), grid_spec=pltpu...  12.9 us
    all_to_all x1, blocking collectives, shards(): lax.all_to_all(pieces, 'seq', split_axis=0, concat_axis=0, tiled=True)  10.6 us
    all_to_all x1, waiting for transfers between devices, shards(): lax.all_to_all(ask, 'seq', split_axis=0, concat_axis=0, tiled=True)  7.89 us
    all_to_all x1, starting transfers between devices, shards(): lax.all_to_all(ask, 'seq', split_axis=0, concat_axis=0, tiled=True)  7.41 us
    pallas_call x1, Pallas kernels, private_part(): pl.pallas_call(functools.partial(private_kernel, draft=draft, blocks=bloc...  4 us
    all_to_all x1, starting transfers between devices, shards(): priv = lax.all_to_all(told, 'seq', split_axis=0, concat_axis=0, tiled=True)  3.52 us
    pallas_call x1, Pallas kernels, merge_part(): pl.pallas_call(merge_kernel, in_specs=[SMEM_SPEC, VMEM_SPEC, VMEM_SPEC, V...  2.22 us
  transfers between devices with their start and end apart: 4, of which 2 were waited for; matrix products, arithmetic and copies ran while one was open for 0% of the time, Pallas kernels for 20%

profile of v3, /device:TPU:0, one launch (start us, length us, event | category | flops | bytes accessed | tf_op | source)
XLA Modules:
  0.0 75.0 jit_solution(11275070189550671472)
XLA Ops:
  0.7 4.0 %private_part.1 = (f32[16,4,640]{2,1,0:T(4,128)}, bf16[16,4,1024]{2,1,0:T(4,128)(2,1)}) custom-call(s32[4]{0:T(128)} %par_ref.1, s32[1]{0:T(128)S(6)} %copy.11.len_ref, bf16[4,8192]{1,0:T(4,128)(2,1)} %q_ref.1, bf16[4,1024]{1,0:T(4,128)(2,1)} %dk_ref.1, bf16[4,1024]{1,0:T(4,128)(2,1)} %dv_ref.1, bf16[1,1024,1024]{2,1,0:T(8,128)(2,1)} %k_ref.2, ...), custom_call_target="tpu_custom_call" | custom-call | flops 134217728 | bytes 4194304 | tf_op jit(solution)/shard_map/private_part/pallas_call | solution.py:102
  4.7 7.4 %all-to-all-start = ((bf16[16,4,1024]{2,1,0:T(4,128)(2,1)}), bf16[16,4,1024]{2,1,0:T(4,128)(2,1)S(1)}, u32[]{:S(2)}, u32[]{:S(2)}) async-start(bf16[16,4,1024]{2,1,0:T(4,128)(2,1)} %get-tuple-element.13), calls=%async_computation | async-start | bytes 262144 | tf_op jit(solution)/shard_map/all_to_all | solution.py:376
  12.1 7.9 %all-to-all-done.q_ref = bf16[16,4,1024]{2,1,0:T(4,128)(2,1)S(1)} async-done(((bf16[16,4,1024]{2,1,0:T(4,128)(2,1)}), bf16[16,4,1024]{2,1,0:T(4,128)(2,1)S(1)}, u32[]{:S(2)}, u32[]{:S(2)}) %all-to-all-start) | async-done | bytes 131104 | tf_op jit(solution)/shard_map/all_to_all | solution.py:376
  20.0 3.5 %all-to-all-start.1 = ((f32[16,4,640]{2,1,0:T(4,128)}), f32[16,4,640]{2,1,0:T(4,128)S(1)}, u32[]{:S(2)}, u32[]{:S(2)}) async-start(f32[16,4,640]{2,1,0:T(4,128)} %get-tuple-element.16), calls=%async_computation.1 | async-start | bytes 327680 | tf_op jit(solution)/shard_map/all_to_all | solution.py:377
  23.5 12.9 %prefix_part.1 = (f32[256,256]{1,0:T(8,128)S(1)}, f32[256,256]{1,0:T(8,128)S(1)}) custom-call(s32[1]{0:T(128)} %bitcast.1.rank_ref, bf16[16,4,1024]{2,1,0:T(4,128)(2,1)S(1)} %all-to-all-done.q_ref, bf16[1,16384,128]{2,1,0:T(8,128)(2,1)} %k_ref.3, bf16[1,16384,128]{2,1,0:T(8,128)(2,1)} %v_ref.3), custom_call_target="tpu_custom_call" | custom-call | flops 4294967296 | bytes 8388608 | tf_op jit(solution)/shard_map/prefix_part/pallas_call | solution.py:189
  36.4 0.3 collective-permute-start
  36.7 0.0 all-to-all-done.1.priv_ref
  36.7 1.3 %collective-permute-done.other_ref = f32[256,256]{1,0:T(8,128)S(1)} collective-permute-done((f32[256,256]{1,0:T(8,128)S(1)}, f32[256,256]{1,0:T(8,128)S(1)}, u32[]{:S(2)}, u32[]{:S(2)}) %collective-permute-start) | collective-permute-done | bytes 262176 | tf_op jit(solution)/shard_map/ppermute | solution.py:363
  38.0 2.2 %merge_part.1 = (bf16[8,64,512]{2,1,0:T(8,128)(2,1)S(1)}, bf16[8,512,512]{2,1,0:T(8,128)(2,1)S(1)}) custom-call(s32[1]{0:T(128)} %bitcast.side_ref, f32[256,256]{1,0:T(8,128)S(1)} %get-tuple-element.14.mine_ref, f32[256,256]{1,0:T(8,128)S(1)} %collective-permute-done.other_ref, f32[16,4,640]{2,1,0:T(4,128)S(1)} %all-to-all-done.1.priv_ref, ...), custom_call_target="tpu_custom_call" | custom-call | flops 524288 | bytes 4194304 | tf_op jit(solution)/shard_map/merge_part/pallas_call | solution.py:265
  40.2 20.4 %all_to_all.20.att_ref = bf16[8,64,512]{2,1,0:T(8,128)(2,1)S(1)} all-to-all(bf16[8,64,512]{2,1,0:T(8,128)(2,1)S(1)} %get-tuple-element.17), channel_id=1, replica_groups={{0,2,4,6,8,10,12,14},{1,3,5,7,9,11,13,15},{16,18,20,22,24,26,28,30},{17..., dimensions={0} | all-to-all | bytes 1048576 | tf_op jit(solution)/shard_map/all_to_all | solution.py:394
  60.7 0.0 collective-permute-start.1
  60.7 2.2 %project_own.1 = (f32[64,512]{1,0:T(8,128)S(1)}, bf16[8,512,512]{2,1,0:T(8,128)(2,1)S(1)}) custom-call(s32[1]{0:T(128)} %bitcast.side_ref, bf16[8,64,512]{2,1,0:T(8,128)(2,1)S(1)} %all_to_all.20.att_ref, bf16[8,512,512]{2,1,0:T(8,128)(2,1)S(1)} %get-tuple-element.18.wide_ref, bf16[8,2,512,512]{3,2,1,0:T(8,128)(2,1)} %bitcast.7), custom_call_target="tpu_custom_call" | custom-call | flops 268435456 | bytes 4194304 | tf_op jit(solution)/shard_map/project_own/pallas_call | solution.py:309
  62.9 0.0 collective-permute-done.1.att_ref
  62.9 0.8 %project_twin.1 = bf16[16,4,512]{2,1,0:T(4,128)(2,1)S(1)} custom-call(f32[64,512]{1,0:T(8,128)S(1)} %get-tuple-element.19.part_ref, bf16[8,64,512]{2,1,0:T(8,128)(2,1)S(1)} %collective-permute-done.1.att_ref, bf16[8,512,512]{2,1,0:T(8,128)(2,1)S(1)} %get-tuple-element.20.wide_ref), custom_call_target="tpu_custom_call" | custom-call | flops 268435456 | tf_op jit(solution)/shard_map/project_twin/pallas_call | solution.py:328
  63.7 10.6 %all_to_all.21 = bf16[16,4,512]{2,1,0:T(4,128)(2,1)S(1)} all-to-all(bf16[16,4,512]{2,1,0:T(4,128)(2,1)S(1)} %project_twin.1), channel_id=1, replica_groups=mesh['groups'=2,'seq'=16] {'seq'}, dimensions={0} | all-to-all | bytes 131072 | tf_op jit(solution)/shard_map/all_to_all | solution.py:400
  74.3 0.7 convert_element_type.13
Async XLA Ops:
  4.7 15.3 %all-to-all-start = ((bf16[16,4,1024]{2,1,0:T(4,128)(2,1)}), bf16[16,4,1024]{2,1,0:T(4,128)(2,1)S(1)}, u32[]{:S(2)}, u32[]{:S(2)}) async-start(bf16[16,4,1024]{2,1,0:T(4,128)(2,1)} %get-tuple-element.13), calls=%async_computation | async-start | bytes 262144 | tf_op jit(solution)/shard_map/all_to_all | solution.py:376
  20.0 16.7 %all-to-all-start.1 = ((f32[16,4,640]{2,1,0:T(4,128)}), f32[16,4,640]{2,1,0:T(4,128)S(1)}, u32[]{:S(2)}, u32[]{:S(2)}) async-start(f32[16,4,640]{2,1,0:T(4,128)} %get-tuple-element.16), calls=%async_computation.1 | async-start | bytes 327680 | tf_op jit(solution)/shard_map/all_to_all | solution.py:377
  36.4 1.6 %collective-permute-start = (f32[256,256]{1,0:T(8,128)S(1)}, f32[256,256]{1,0:T(8,128)S(1)}, u32[]{:S(2)}, u32[]{:S(2)}) collective-permute-start(f32[256,256]{1,0:T(8,128)S(1)} %get-tuple-element.15), channel_id=1, source_target_pairs={{0,1},{1,0},{2,3},{3,2},{4,5},{5,4},{6,7},{7,6},{8,9},{9,8},{10,11... | collective-permute-start | bytes 786440 | tf_op jit(solution)/shard_map/ppermute | solution.py:363
  60.7 2.2 %collective-permute-start.1 = (bf16[8,64,512]{2,1,0:T(8,128)(2,1)S(1)}, bf16[8,64,512]{2,1,0:T(8,128)(2,1)S(1)}, u32[]{:S(2)}, u32[]{:S(2)}) collective-permute-start(bf16[8,64,512]{2,1,0:T(8,128)(2,1)S(1)} %all_to_all.20.att_ref), channel_id=1, source_target_pairs={{0,1},{1,0},{2,3},{3,2},{4,5},{5,4},{6,7},{7,6},{8,9},{9,8},{10,11... | collective-permute-start | bytes 1572872 | tf_op jit(solution)/shard_map/ppermute | solution.py:363

commit v4 on v3

v4 whole, which is shorter than its diff:
```python
import functools

import jax
import jax.numpy as jnp
from jax import lax
from jax.experimental import pallas as pl
from jax.experimental.pallas import tpu as pltpu
from jax.sharding import PartitionSpec as P


HEADS = 64
KVH = 8
HD = 128
GROUP = HEADS // KVH
SCALE = HD ** (-0.5)
LOG2E = 1.4426950408889634
LANES = 128
NEG = -1e30
LIMIT = 2.0**100
WIDE = GROUP * HD
MESSAGE = 3 * WIDE + LANES
NT = (((1,), (1,)), ((), ()))
TN = (((0,), (0,)), ((), ()))
F32 = jnp.float32
BF16 = jnp.bfloat16


def in_hbm(array):
    return pltpu.with_memory_space_constraint(array, pltpu.HBM)


def on_chip(array):
    return pltpu.with_memory_space_constraint(array, pltpu.VMEM)


VMEM_SPEC = pl.BlockSpec(memory_space=pltpu.VMEM)
SMEM_SPEC = pl.BlockSpec(memory_space=pltpu.SMEM)


def private_kernel(
    par_ref, len_ref, q_ref, dk_ref, dv_ref, k_ref, v_ref, out_ref, *, draft, copies, batch
):
    rows = GROUP * draft
    slots = k_ref.shape[1]
    seen = []
    for i in range(draft):
        bits = jnp.int32(1 << i)
        for j in range(i):
            bits = bits | jnp.where(par_ref[i] == j, seen[j], 0)
        seen.append(bits)
    row = lax.broadcasted_iota(jnp.int32, (rows, LANES), 0) % draft
    lane = lax.broadcasted_iota(jnp.int32, (rows, LANES), 1)
    mask = jnp.zeros((rows, LANES), jnp.int32)
    for i in range(draft):
        mask = jnp.where(row == i, seen[i], mask)
    shown = (lane < draft) & ((lax.shift_right_logical(mask, jnp.minimum(lane, 31)) & 1) == 1)
    live = lax.broadcasted_iota(jnp.int32, (rows, slots), 1) < len_ref[0]
    fill = jnp.zeros((LANES - draft, HD), F32)
    stat_lane = lax.broadcasted_iota(jnp.int32, (draft, LANES), 1)
    groups = range(batch)
    queries = []
    for g in groups:
        q = q_ref[:, g * WIDE : (g + 1) * WIDE]
        for copy in range(copies):
            out_ref[g * copies + copy, :, :WIDE] = q
        q32 = q.astype(F32)
        queries.append(
            jnp.concatenate([q32[:, h * HD : (h + 1) * HD] for h in range(GROUP)], axis=0).astype(BF16)
        )
    cols = [slice(g * HD, (g + 1) * HD) for g in groups]
    scores = [
        lax.dot_general(queries[g], k_ref[0, :, cols[g]], NT, preferred_element_type=F32) for g in groups
    ]
    trees = []
    for g in groups:
        dkey = jnp.concatenate([dk_ref[:, cols[g]].astype(F32), fill], axis=0).astype(BF16)
        trees.append(lax.dot_general(queries[g], dkey, NT, preferred_element_type=F32))
    for g in groups:
        score = jnp.where(live, scores[g] * SCALE, NEG)
        tree = jnp.where(shown, trees[g] * SCALE, NEG)
        tiles = [score[:, j : j + LANES] for j in range(0, slots, LANES)] + [tree]
        peak = jnp.max(functools.reduce(jnp.maximum, tiles), axis=1, keepdims=True)
        tiles = [jnp.exp(tile - peak) for tile in tiles]
        denom = jnp.sum(functools.reduce(jnp.add, tiles), axis=1, keepdims=True)
        weights = jnp.concatenate([tile.astype(BF16) for tile in tiles[:-1]], axis=1)
        dval = jnp.concatenate([dv_ref[:, cols[g]].astype(F32), fill], axis=0).astype(BF16)
        mixture = jnp.dot(weights, v_ref[0, :, cols[g]], preferred_element_type=F32)
        mixture = mixture + jnp.dot(tiles[-1].astype(BF16), dval, preferred_element_type=F32)
        mixture = mixture / denom
        coarse = mixture.astype(BF16).astype(F32)
        fine = mixture - coarse
        lse = peak + jnp.log(denom)
        first = lse.astype(BF16).astype(F32)
        second = (lse - first).astype(BF16).astype(F32)
        third = lse - first - second
        stats = jnp.zeros((draft, LANES), F32)
        for copy in range(copies):
            at = g * copies + copy
            for h in range(GROUP):
                part = slice(h * draft, (h + 1) * draft)
                out_ref[at, :, WIDE + h * HD : WIDE + (h + 1) * HD] = coarse[part].astype(BF16)
                out_ref[at, :, 2 * WIDE + h * HD : 2 * WIDE + (h + 1) * HD] = fine[part].astype(BF16)
                if copy == 0:
                    for t, term in enumerate((first, second, third)):
                        stats = jnp.where(stat_lane == 3 * h + t, term[part], stats)
            out_ref[at, :, 3 * WIDE :] = stats.astype(BF16)


def private_part(parents, lengths, queries, dkeys, dvals, pkeys, pvals, copies, batch):
    draft = queries.shape[0]
    slots = pkeys.shape[1]
    return pl.pallas_call(
        functools.partial(private_kernel, draft=draft, copies=copies, batch=batch),
        grid=(KVH // batch,),
        in_specs=[
            SMEM_SPEC,
            SMEM_SPEC,
            pl.BlockSpec((draft, batch * WIDE), lambda g: (0, g)),
            pl.BlockSpec((draft, batch * HD), lambda g: (0, g)),
            pl.BlockSpec((draft, batch * HD), lambda g: (0, g)),
            pl.BlockSpec((1, slots, batch * HD), lambda g: (0, 0, g)),
            pl.BlockSpec((1, slots, batch * HD), lambda g: (0, 0, g)),
        ],
        out_specs=pl.BlockSpec((batch * copies, draft, MESSAGE), lambda g: (g, 0, 0)),
        out_shape=jax.ShapeDtypeStruct((KVH * copies, draft, MESSAGE), BF16),
        cost_estimate=pl.CostEstimate(
            flops=4 * draft * HEADS * slots * HD,
            transcendentals=draft * HEADS * slots,
            bytes_accessed=4 * slots * KVH * HD,
        ),
        name="private_part",
    )(parents, lengths, queries, dkeys, dvals, pkeys, pvals)


def by_parity(parity, own, twin):
    return (jnp.where(parity == 0, own, twin), jnp.where(parity == 0, twin, own))


def prefix_kernel(
    place_ref, own_ref, twin_ref, k_ref, v_ref, keep_ref, send_ref, own32, twin32, qs, peak, denom, acc
):
    step = pl.program_id(0)
    chips, draft, _ = own_ref.shape
    half = chips * draft
    rows = 2 * half * GROUP
    span = k_ref.shape[1]

    @pl.when(step == 0)
    def _():
        for j in range(chips):
            own32[j * draft : (j + 1) * draft, :] = own_ref[j, :, :WIDE].astype(F32)
            twin32[j * draft : (j + 1) * draft, :] = twin_ref[j, :, :WIDE].astype(F32)
        halves = by_parity(place_ref[1], own32[...], twin32[...])
        for h in range(GROUP):
            for p in range(2):
                at = (2 * h + p) * half
                qs[at : at + half, :] = halves[p][:, h * HD : (h + 1) * HD].astype(BF16)
        head = lax.dot_general(k_ref[0, :HD, :], qs[...], NT, preferred_element_type=F32)
        peak[...] = jnp.max(head, axis=0, keepdims=True) * (SCALE * LOG2E)
        denom[...] = jnp.zeros(denom.shape, F32)
        acc[...] = jnp.zeros(acc.shape, F32)

    scores = lax.dot_general(k_ref[0], qs[...], NT, preferred_element_type=F32)
    weights = jnp.exp2(scores * (SCALE * LOG2E) - peak[...])
    total = denom[...] + jnp.sum(weights.reshape(span // 8, 8, rows), axis=0)
    mixed = acc[...] + lax.dot_general(v_ref[0], weights.astype(BF16), TN, preferred_element_type=F32)
    fits = jnp.max(total) < LIMIT

    @pl.when(fits)
    def _():
        denom[...] = total
        acc[...] = mixed

    @pl.when(jnp.logical_not(fits))
    def _():
        part = 4 * HD

        @pl.loop(0, span // part)
        def _(b):
            block = pl.ds(pl.multiple_of(b * part, part), part)
            scores = lax.dot_general(k_ref[0, block, :], qs[...], NT, preferred_element_type=F32)
            scores = scores * (SCALE * LOG2E)
            old = peak[...]
            new = jnp.maximum(old, jnp.max(scores, axis=0, keepdims=True))
            fade = jnp.exp2(old - new)
            weights = jnp.exp2(scores - new)
            peak[...] = new
            denom[...] = denom[...] * fade + jnp.sum(weights.reshape(part // 8, 8, rows), axis=0)
            acc[...] = acc[...] * fade + lax.dot_general(
                v_ref[0, block, :], weights.astype(BF16), TN, preferred_element_type=F32
            )

    @pl.when(step == pl.num_programs(0) - 1)
    def _():
        total = jnp.sum(denom[...], axis=0, keepdims=True)
        lse = peak[...] * (1.0 / LOG2E) + jnp.log(total)
        mixed = (acc[...] / total).T
        lse = jnp.broadcast_to(lse, (LANES, rows)).T
        lower = place_ref[0] == 0
        split = rows // 2
        keep_ref[:, :HD] = jnp.where(lower, mixed[:split], mixed[split:])
        keep_ref[:, HD:] = jnp.where(lower, lse[:split], lse[split:])
        send_ref[:, :HD] = jnp.where(lower, mixed[split:], mixed[:split])
        send_ref[:, HD:] = jnp.where(lower, lse[split:], lse[:split])


def prefix_part(place, own, twin, keys, values, span):
    chips, draft, _ = own.shape
    half = chips * draft
    rows = 2 * half * GROUP
    shape = jax.ShapeDtypeStruct((rows // 2, HD + LANES), F32)
    whole = pl.BlockSpec(own.shape, lambda i: (0, 0, 0))
    return pl.pallas_call(
        prefix_kernel,
        grid=(keys.shape[1] // span,),
        in_specs=[
            SMEM_SPEC,
            whole,
            whole,
            pl.BlockSpec((1, span, HD), lambda i: (0, i, 0)),
            pl.BlockSpec((1, span, HD), lambda i: (0, i, 0)),
        ],
        out_specs=[pl.BlockSpec((rows // 2, HD + LANES), lambda i: (0, 0))] * 2,
        out_shape=[shape, shape],
        scratch_shapes=[
            pltpu.VMEM((half, WIDE), F32),
            pltpu.VMEM((half, WIDE), F32),
            pltpu.VMEM((rows, HD), BF16),
            pltpu.VMEM((1, rows), F32),
            pltpu.VMEM((8, rows), F32),
            pltpu.VMEM((HD, rows), F32),
        ],
        compiler_params=pltpu.CompilerParams(vmem_limit_bytes=40 << 20),
        cost_estimate=pl.CostEstimate(
            flops=4 * rows * keys.shape[1] * HD,
            transcendentals=rows * keys.shape[1],
            bytes_accessed=4 * keys.shape[1] * HD,
        ),
        name="prefix_part",
    )(place, on_chip(own), on_chip(twin), in_hbm(keys), in_hbm(values))


def join(first, second):
    out_a, lse_a = first[:, :HD], first[:, HD:]
    out_b, lse_b = second[:, :HD], second[:, HD:]
    top = jnp.maximum(lse_a, lse_b)
    scale_a = jnp.exp(lse_a - top)
    scale_b = jnp.exp(lse_b - top)
    both = scale_a + scale_b
    return jnp.concatenate(
        [(scale_a * out_a + scale_b * out_b) / both, top + jnp.log(both)], axis=1
    )


def merge_kernel(
    place_ref, mine_ref, other_ref, own_ref, twin_ref, w_ref, att_ref, wide_ref, own32, twin32, sem
):
    fetch = pltpu.make_async_copy(w_ref.at[:, place_ref[1]], wide_ref, sem)
    fetch.start()
    chips, draft, _ = own_ref.shape
    half = chips * draft
    wide = att_ref.shape[2]
    heads = wide // HD
    first_head = place_ref[2] * heads
    col = pl.multiple_of(first_head * HD, wide)
    for given, held in ((own_ref, own32), (twin_ref, twin32)):
        for j in range(chips):
            part = slice(j * draft, (j + 1) * draft)
            held[part, :wide] = given[j, :, pl.ds(WIDE + col, wide)].astype(F32) + given[
                j, :, pl.ds(2 * WIDE + col, wide)
            ].astype(F32)
            held[part, wide:] = given[j, :, 3 * WIDE :].astype(F32)
    told = by_parity(place_ref[1], own32[...], twin32[...])
    lane = lax.broadcasted_iota(jnp.int32, (half, LANES), 1)
    for h in range(heads):
        at = 3 * (first_head + h)
        mark = (lane >= at) & (lane < at + 3)
        for p in range(2):
            out_p = told[p][:, h * HD : (h + 1) * HD]
            lse_p = jnp.sum(jnp.where(mark, told[p][:, wide:], 0.0), axis=1, keepdims=True)
            part = slice((2 * h + p) * half, (2 * h + p + 1) * half)
            lse_a = mine_ref[part, HD:]
            lse_b = other_ref[part, HD:]
            top = jnp.maximum(jnp.maximum(lse_a, lse_b), lse_p)
            scale_a = jnp.exp(lse_a - top)
            scale_b = jnp.exp(lse_b - top)
            scale_p = jnp.exp(lse_p - top)
            mixed = scale_a * mine_ref[part, :HD] + scale_b * other_ref[part, :HD] + scale_p * out_p
            mixed = (mixed / (scale_a + scale_b + scale_p)).astype(BF16)
            for copy in range(att_ref.shape[0]):
                att_ref[copy, p * half : (p + 1) * half, h * HD : (h + 1) * HD] = mixed
    fetch.wait()


def merge_part(place, mine, other, own, twin, weight):
    chips, draft, _ = own.shape
    half = chips * draft
    _, _, deep, cols = weight.shape
    return pl.pallas_call(
        merge_kernel,
        in_specs=[SMEM_SPEC] + [VMEM_SPEC] * 4 + [pl.BlockSpec(memory_space=pl.ANY)],
        out_specs=[VMEM_SPEC, VMEM_SPEC],
        out_shape=[
            pltpu.VMEM((chips, 2 * half, deep), BF16),
            pltpu.VMEM((chips, deep, cols), BF16),
        ],
        scratch_shapes=[
            pltpu.VMEM((half, deep + LANES), F32),
            pltpu.VMEM((half, deep + LANES), F32),
            pltpu.SemaphoreType.DMA,
        ],
        compiler_params=pltpu.CompilerParams(vmem_limit_bytes=8 << 20),
        cost_estimate=pl.CostEstimate(
            flops=8 * mine.size, transcendentals=mine.size, bytes_accessed=2 * chips * deep * cols
        ),
        name="merge_part",
    )(place, on_chip(mine), on_chip(other), on_chip(own), on_chip(twin), in_hbm(weight))


def matmuls(att_ref, wide_ref):
    return functools.reduce(
        jnp.add,
        [
            jnp.dot(att_ref[i], wide_ref[i], preferred_element_type=F32)
            for i in range(att_ref.shape[0])
        ],
    )


def first_kernel(place_ref, att_ref, wide_ref, w_ref, out_ref, next_ref, sem):
    fetch = pltpu.make_async_copy(w_ref.at[:, 1 - place_ref[1]], next_ref, sem)
    fetch.start()
    out_ref[...] = matmuls(att_ref, wide_ref)
    fetch.wait()


def second_kernel(part_ref, att_ref, wide_ref, out_ref):
    total = part_ref[...] + matmuls(att_ref, wide_ref)
    owners, draft, _ = out_ref.shape
    for s in range(owners):
        at = ((s % 2) * (owners // 2) + s // 2) * draft
        out_ref[s] = total[at : at + draft].astype(BF16)


def project_own(place, att, wide, weight):
    chips, rows, deep = att.shape
    cols = weight.shape[3]
    return pl.pallas_call(
        first_kernel,
        in_specs=[SMEM_SPEC, VMEM_SPEC, VMEM_SPEC, pl.BlockSpec(memory_space=pl.ANY)],
        out_specs=[VMEM_SPEC, VMEM_SPEC],
        out_shape=[pltpu.VMEM((rows, cols), F32), pltpu.VMEM((chips, deep, cols), BF16)],
        scratch_shapes=[pltpu.SemaphoreType.DMA],
        compiler_params=pltpu.CompilerParams(vmem_limit_bytes=8 << 20),
        cost_estimate=pl.CostEstimate(
            flops=2 * rows * deep * chips * cols,
            transcendentals=0,
            bytes_accessed=2 * deep * chips * cols,
        ),
        name="project_own",
    )(place, on_chip(att), on_chip(wide), in_hbm(weight))


def project_twin(part, att, wide, owners):
    chips, rows, deep = att.shape
    cols = wide.shape[2]
    return pl.pallas_call(
        second_kernel,
        in_specs=[VMEM_SPEC, VMEM_SPEC, VMEM_SPEC],
        out_specs=VMEM_SPEC,
        out_shape=pltpu.VMEM((owners, rows // owners, cols), BF16),
        compiler_params=pltpu.CompilerParams(vmem_limit_bytes=8 << 20),
        cost_estimate=pl.CostEstimate(
            flops=2 * rows * deep * chips * cols, transcendentals=0, bytes_accessed=0
        ),
        name="project_twin",
    )(on_chip(part), on_chip(att), on_chip(wide))


def shards(
    queries,
    draft_keys,
    draft_values,
    parents,
    private_keys,
    private_values,
    priv_lengths,
    prefix_keys,
    prefix_values,
    out_weight,
):
    own_rows = queries.shape[0]
    seq = lax.axis_size("seq")
    chips = seq // 2
    blocks = seq // KVH
    device = lax.axis_index("seq")
    rank = device % blocks
    top_bit = blocks.bit_length() - 2
    place = jnp.stack([(rank >> top_bit) & 1, device % 2, rank]).astype(jnp.int32)
    members = [list(range(c, seq, 2)) for c in range(2)]

    def from_partner(array, bit):
        return lax.ppermute(array, "seq", [(i, i ^ 1 << bit) for i in range(seq)])

    def among_members(array):
        return lax.all_to_all(
            array, "seq", split_axis=0, concat_axis=0, axis_index_groups=members, tiled=True
        )

    message = private_part(
        parents,
        priv_lengths,
        queries,
        draft_keys,
        draft_values,
        in_hbm(private_keys),
        in_hbm(private_values),
        blocks // 2,
        KVH // 2,
    )
    own = among_members(message)
    twin = from_partner(own, 0)

    span = min(4096, prefix_keys.shape[1])
    mine, gone = prefix_part(place, own, twin, prefix_keys, prefix_values, span)
    other = from_partner(gone, top_bit)
    for level in range(top_bit - 1, -1, -1):
        held = join(mine, other)
        half = held.shape[0] // 2
        at = (rank >> level) & 1
        mine = lax.dynamic_slice_in_dim(held, at * half, half, 0)
        other = from_partner(lax.dynamic_slice_in_dim(held, (1 - at) * half, half, 0), level)

    weight = out_weight.reshape(chips, 2, -1, out_weight.shape[1])
    copies, wide = merge_part(place, mine, other, own, twin, weight)
    same = among_members(copies)
    twin = from_partner(same, 0)
    part, wide = project_own(place, same, wide, weight)
    pieces = project_twin(part, twin, wide, seq)
    done = lax.all_to_all(pieces, "seq", split_axis=0, concat_axis=0, tiled=True)
    return done.transpose(1, 0, 2).reshape(own_rows, -1).astype(F32)


def solution(mesh):
    in_specs = (
        P(("groups", "seq"), None),
        P(("groups", "seq"), None),
        P(("groups", "seq"), None),
        P(("groups", "seq")),
        P(("groups", "seq"), None, None),
        P(("groups", "seq"), None, None),
        P(("groups", "seq")),
        P(("groups", "seq"), None, None),
        P(("groups", "seq"), None, None),
        P(None, "seq"),
    )
    out_specs = P(("groups", "seq"), None)

    return jax.shard_map(shards, mesh=mesh, in_specs=in_specs, out_specs=out_specs, check_vma=False)
```

time: 75.4 us -> 77.4 us (1.027)
  the two profiles are of different devices: /device:TPU:0 before, /device:TPU:2 now
where the time goes in v4:
time: 77.4 us; the launch traced here: 77 us
  blocking collectives  52.1 us (67%)
  Pallas kernels  20.5 us (26%)
  waiting for transfers between devices  2.78 us (4%)
    all_to_all x2, blocking collectives, among_members(): lax.all_to_all(array, 'seq', split_axis=0, concat_axis=0, axis_index_grou...  41.6 us
    all_to_all x1, blocking collectives, shards(): lax.all_to_all(pieces, 'seq', split_axis=0, concat_axis=0, tiled=True)  10.6 us
    pallas_call x1, Pallas kernels, prefix_part(): pl.pallas_call(prefix_kernel, grid=(keys.shape[1] // span,), in_specs=[SM...  10.1 us
    pallas_call x1, Pallas kernels, private_part(): pl.pallas_call(functools.partial(private_kernel, draft=draft, copies=copi...  4.02 us
    ppermute x3, waiting for transfers between devices, from_partner(): return lax.ppermute(array, 'seq', [(i, i ^ 1 << bit) for i in range(seq)])  2.78 us
    pallas_call x1, Pallas kernels, merge_part(): pl.pallas_call(merge_kernel, in_specs=[SMEM_SPEC] + [VMEM_SPEC] * 4 + [pl...  2.77 us
    pallas_call x1, Pallas kernels, project_own(): pl.pallas_call(first_kernel, in_specs=[SMEM_SPEC, VMEM_SPEC, VMEM_SPEC, p...  2.76 us
  transfers between devices with their start and end apart: 3, of which 2 were waited for; matrix products, arithmetic and copies ran while one was open for 0% of the time, Pallas kernels for 4%

profile of v4, /device:TPU:2, one launch (start us, length us, event | category | flops | bytes accessed | tf_op | source)
XLA Modules:
  0.0 77.0 jit_solution(13862595490738444741)
XLA Ops:
  0.7 4.0 %private_part.1 = bf16[8,4,3200]{2,1,0:T(4,128)(2,1)} custom-call(s32[4]{0:T(128)} %par_ref.1, s32[1]{0:T(128)S(6)} %copy.11.len_ref, bf16[4,8192]{1,0:T(4,128)(2,1)} %q_ref.1, bf16[4,1024]{1,0:T(4,128)(2,1)} %dk_ref.1, bf16[4,1024]{1,0:T(4,128)(2,1)} %dv_ref.1, bf16[1,1024,1024]{2,1,0:T(8,128)(2,1)} %k_ref.2, bf16[1,1024,1024]{2,1,0:T(8,128)(2,1)} %v_ref.2), custom_call_target="tpu_custom_call" | custom-call | flops 134217728 | bytes 4194304 | tf_op jit(solution)/shard_map/private_part/pallas_call | solution.py:112
  4.7 13.9 %all_to_all.15.own_ref = bf16[8,4,3200]{2,1,0:T(4,128)(2,1)S(1)} all-to-all(bf16[8,4,3200]{2,1,0:T(4,128)(2,1)} %private_part.1), channel_id=1, replica_groups={{0,2,4,6,8,10,12,14},{1,3,5,7,9,11,13,15},{16,18,20,22,24,26,28,30},{17..., dimensions={0} | all-to-all | bytes 409600 | tf_op jit(solution)/shard_map/all_to_all | solution.py:406
  18.6 0.0 collective-permute-start
  18.6 0.1 pad_add_fusion.place_ref
  18.7 1.4 %collective-permute-done.twin_ref = bf16[8,4,3200]{2,1,0:T(4,128)(2,1)S(1)} collective-permute-done((bf16[8,4,3200]{2,1,0:T(4,128)(2,1)S(1)}, bf16[8,4,3200]{2,1,0:T(4,128)(2,1)S(1)}, u32[]{:S(2)}, u32[]{:S(2)}) %collective-permute-start) | collective-permute-done | bytes 204832 | tf_op jit(solution)/shard_map/ppermute | solution.py:403
  20.0 10.1 %prefix_part.1 = (f32[256,256]{1,0:T(8,128)S(1)}, f32[256,256]{1,0:T(8,128)S(1)}) custom-call(s32[3]{0:T(128)S(1)} %pad_add_fusion.place_ref, bf16[8,4,3200]{2,1,0:T(4,128)(2,1)S(1)} %all_to_all.15.own_ref, bf16[8,4,3200]{2,1,0:T(4,128)(2,1)S(1)} %collective-permute-done.twin_ref, bf16[1,16384,128]{2,1,0:T(8,128)(2,1)} %k_ref.3, bf16[1,16384,128]{2,1,0:T(8,128)(2,1)} %v_ref.3), custom_call_target="tpu_custom_call" | custom-call | flops 4294967296 | bytes 8388608 | tf_op jit(solution)/shard_map/prefix_part/pallas_call | solution.py:213
  30.1 0.2 collective-permute-start.1
  30.3 1.4 %collective-permute-done.1.other_ref = f32[256,256]{1,0:T(8,128)S(1)} collective-permute-done((f32[256,256]{1,0:T(8,128)S(1)}, f32[256,256]{1,0:T(8,128)S(1)}, u32[]{:S(2)}, u32[]{:S(2)}) %collective-permute-start.1) | collective-permute-done | bytes 262176 | tf_op jit(solution)/shard_map/ppermute | solution.py:403
  31.7 2.8 %merge_part.1 = (bf16[8,64,512]{2,1,0:T(8,128)(2,1)S(1)}, bf16[8,512,512]{2,1,0:T(8,128)(2,1)S(1)}) custom-call(s32[3]{0:T(128)S(1)} %pad_add_fusion.place_ref, f32[256,256]{1,0:T(8,128)S(1)} %get-tuple-element.11.mine_ref, f32[256,256]{1,0:T(8,128)S(1)} %collective-permute-done.1.other_ref, bf16[8,4,3200]{2,1,0:T(4,128)(2,1)S(1)} %all_to_all.15.own_ref, ...), custom_call_target="tpu_custom_call" | custom-call | flops 524288 | bytes 4194304 | tf_op jit(solution)/shard_map/merge_part/pallas_call | solution.py:299
  34.5 27.7 %all_to_all.16.att_ref = bf16[8,64,512]{2,1,0:T(8,128)(2,1)S(1)} all-to-all(bf16[8,64,512]{2,1,0:T(8,128)(2,1)S(1)} %get-tuple-element.13), channel_id=1, replica_groups={{0,2,4,6,8,10,12,14},{1,3,5,7,9,11,13,15},{16,18,20,22,24,26,28,30},{17..., dimensions={0} | all-to-all | bytes 1048576 | tf_op jit(solution)/shard_map/all_to_all | solution.py:406
  62.2 0.0 collective-permute-start.2
  62.2 2.8 %project_own.1 = (f32[64,512]{1,0:T(8,128)S(1)}, bf16[8,512,512]{2,1,0:T(8,128)(2,1)S(1)}) custom-call(s32[3]{0:T(128)S(1)} %pad_add_fusion.place_ref, bf16[8,64,512]{2,1,0:T(8,128)(2,1)S(1)} %all_to_all.16.att_ref, bf16[8,512,512]{2,1,0:T(8,128)(2,1)S(1)} %get-tuple-element.14.wide_ref, bf16[8,2,512,512]{3,2,1,0:T(8,128)(2,1)} %bitcast.7), custom_call_target="tpu_custom_call" | custom-call | flops 268435456 | bytes 4194304 | tf_op jit(solution)/shard_map/project_own/pallas_call | solution.py:348
  64.9 0.0 collective-permute-done.2.att_ref
  65.0 0.8 %project_twin.1 = bf16[16,4,512]{2,1,0:T(4,128)(2,1)S(1)} custom-call(f32[64,512]{1,0:T(8,128)S(1)} %get-tuple-element.15.part_ref, bf16[8,64,512]{2,1,0:T(8,128)(2,1)S(1)} %collective-permute-done.2.att_ref, bf16[8,512,512]{2,1,0:T(8,128)(2,1)S(1)} %get-tuple-element.16.wide_ref), custom_call_target="tpu_custom_call" | custom-call | flops 268435456 | tf_op jit(solution)/shard_map/project_twin/pallas_call | solution.py:367
  65.8 10.6 %all_to_all.17 = bf16[16,4,512]{2,1,0:T(4,128)(2,1)S(1)} all-to-all(bf16[16,4,512]{2,1,0:T(4,128)(2,1)S(1)} %project_twin.1), channel_id=1, replica_groups=mesh['groups'=2,'seq'=16] {'seq'}, dimensions={0} | all-to-all | bytes 131072 | tf_op jit(solution)/shard_map/all_to_all | solution.py:440
  76.4 0.7 convert_element_type.13
Async XLA Ops:
  18.6 1.5 %collective-permute-start = (bf16[8,4,3200]{2,1,0:T(4,128)(2,1)S(1)}, bf16[8,4,3200]{2,1,0:T(4,128)(2,1)S(1)}, u32[]{:S(2)}, u32[]{:S(2)}) collective-permute-start(bf16[8,4,3200]{2,1,0:T(4,128)(2,1)S(1)} %all_to_all.15.own_ref), channel_id=1, source_target_pairs={{0,1},{1,0},{2,3},{3,2},{4,5},{5,4},{6,7},{7,6},{8,9},{9,8},{10,11... | collective-permute-start | bytes 614408 | tf_op jit(solution)/shard_map/ppermute | solution.py:403
  30.1 1.6 %collective-permute-start.1 = (f32[256,256]{1,0:T(8,128)S(1)}, f32[256,256]{1,0:T(8,128)S(1)}, u32[]{:S(2)}, u32[]{:S(2)}) collective-permute-start(f32[256,256]{1,0:T(8,128)S(1)} %get-tuple-element.12), channel_id=1, source_target_pairs={{0,1},{1,0},{2,3},{3,2},{4,5},{5,4},{6,7},{7,6},{8,9},{9,8},{10,11... | collective-permute-start | bytes 786440 | tf_op jit(solution)/shard_map/ppermute | solution.py:403
  62.2 2.8 %collective-permute-start.2 = (bf16[8,64,512]{2,1,0:T(8,128)(2,1)S(1)}, bf16[8,64,512]{2,1,0:T(8,128)(2,1)S(1)}, u32[]{:S(2)}, u32[]{:S(2)}) collective-permute-start(bf16[8,64,512]{2,1,0:T(8,128)(2,1)S(1)} %all_to_all.16.att_ref), channel_id=1, source_target_pairs={{0,1},{1,0},{2,3},{3,2},{4,5},{5,4},{6,7},{7,6},{8,9},{9,8},{10,11... | collective-permute-start | bytes 1572872 | tf_op jit(solution)/shard_map/ppermute | solution.py:403

commit v5 on v4

--- a/solution.py
+++ b/solution.py
@@ -137,16 +137,33 @@
 
 
 def prefix_kernel(
-    place_ref, own_ref, twin_ref, k_ref, v_ref, keep_ref, send_ref, own32, twin32, qs, peak, denom, acc
+    place_ref,
+    own_ref,
+    twin_ref,
+    k_ref,
+    v_ref,
+    w_ref,
+    keep_ref,
+    send_ref,
+    wide_ref,
+    own32,
+    twin32,
+    qs,
+    peak,
+    denom,
+    acc,
+    sem,
 ):
     step = pl.program_id(0)
     chips, draft, _ = own_ref.shape
     half = chips * draft
     rows = 2 * half * GROUP
     span = k_ref.shape[1]
+    fetch = pltpu.make_async_copy(w_ref, wide_ref, sem)
 
     @pl.when(step == 0)
     def _():
+        fetch.start()
         for j in range(chips):
             own32[j * draft : (j + 1) * draft, :] = own_ref[j, :, :WIDE].astype(F32)
             twin32[j * draft : (j + 1) * draft, :] = twin_ref[j, :, :WIDE].astype(F32)
@@ -202,9 +219,10 @@
         keep_ref[:, HD:] = jnp.where(lower, lse[:split], lse[split:])
         send_ref[:, :HD] = jnp.where(lower, mixed[split:], mixed[:split])
         send_ref[:, HD:] = jnp.where(lower, lse[split:], lse[:split])
-
-
-def prefix_part(place, own, twin, keys, values, span):
+        fetch.wait()
+
+
+def prefix_part(place, own, twin, keys, values, weight, span):
     chips, draft, _ = own.shape
     half = chips * draft
     rows = 2 * half * GROUP
@@ -219,9 +237,10 @@
             whole,
             pl.BlockSpec((1, span, HD), lambda i: (0, i, 0)),
             pl.BlockSpec((1, span, HD), lambda i: (0, i, 0)),
+            pl.BlockSpec(memory_space=pl.ANY),
         ],
-        out_specs=[pl.BlockSpec((rows // 2, HD + LANES), lambda i: (0, 0))] * 2,
-        out_shape=[shape, shape],
+        out_specs=[pl.BlockSpec((rows // 2, HD + LANES), lambda i: (0, 0))] * 2 + [VMEM_SPEC],
+        out_shape=[shape, shape, pltpu.VMEM(weight.shape, BF16)],
         scratch_shapes=[
             pltpu.VMEM((half, WIDE), F32),
             pltpu.VMEM((half, WIDE), F32),
@@ -229,6 +248,7 @@
             pltpu.VMEM((1, rows), F32),
             pltpu.VMEM((8, rows), F32),
             pltpu.VMEM((HD, rows), F32),
+            pltpu.SemaphoreType.DMA,
         ],
         compiler_params=pltpu.CompilerParams(vmem_limit_bytes=40 << 20),
         cost_estimate=pl.CostEstimate(
@@ -237,7 +257,7 @@
             bytes_accessed=4 * keys.shape[1] * HD,
         ),
         name="prefix_part",
-    )(place, on_chip(own), on_chip(twin), in_hbm(keys), in_hbm(values))
+    )(place, on_chip(own), on_chip(twin), in_hbm(keys), in_hbm(values), in_hbm(weight))
 
 
 def join(first, second):
@@ -253,10 +273,8 @@
 
 
 def merge_kernel(
-    place_ref, mine_ref, other_ref, own_ref, twin_ref, w_ref, att_ref, wide_ref, own32, twin32, sem
+    place_ref, mine_ref, other_ref, own_ref, twin_ref, att_ref, own32, twin32
 ):
-    fetch = pltpu.make_async_copy(w_ref.at[:, place_ref[1]], wide_ref, sem)
-    fetch.start()
     chips, draft, _ = own_ref.shape
     half = chips * draft
     wide = att_ref.shape[2]
@@ -289,84 +307,72 @@
             mixed = (mixed / (scale_a + scale_b + scale_p)).astype(BF16)
             for copy in range(att_ref.shape[0]):
                 att_ref[copy, p * half : (p + 1) * half, h * HD : (h + 1) * HD] = mixed
-    fetch.wait()
-
-
-def merge_part(place, mine, other, own, twin, weight):
+
+
+def merge_part(place, mine, other, own, twin, deep):
     chips, draft, _ = own.shape
     half = chips * draft
-    _, _, deep, cols = weight.shape
     return pl.pallas_call(
         merge_kernel,
-        in_specs=[SMEM_SPEC] + [VMEM_SPEC] * 4 + [pl.BlockSpec(memory_space=pl.ANY)],
-        out_specs=[VMEM_SPEC, VMEM_SPEC],
-        out_shape=[
-            pltpu.VMEM((chips, 2 * half, deep), BF16),
-            pltpu.VMEM((chips, deep, cols), BF16),
-        ],
+        in_specs=[SMEM_SPEC] + [VMEM_SPEC] * 4,
+        out_specs=VMEM_SPEC,
+        out_shape=pltpu.VMEM((chips, 2 * half, deep), BF16),
         scratch_shapes=[
             pltpu.VMEM((half, deep + LANES), F32),
             pltpu.VMEM((half, deep + LANES), F32),
-            pltpu.SemaphoreType.DMA,
         ],
         compiler_params=pltpu.CompilerParams(vmem_limit_bytes=8 << 20),
         cost_estimate=pl.CostEstimate(
-            flops=8 * mine.size, transcendentals=mine.size, bytes_accessed=2 * chips * deep * cols
+            flops=8 * mine.size, transcendentals=mine.size, bytes_accessed=0
         ),
         name="merge_part",
-    )(place, on_chip(mine), on_chip(other), on_chip(own), on_chip(twin), in_hbm(weight))
-
-
-def matmuls(att_ref, wide_ref):
+    )(place, on_chip(mine), on_chip(other), on_chip(own), on_chip(twin))
+
+
+def matmuls(att_ref, wide_ref, parity):
     return functools.reduce(
         jnp.add,
         [
-            jnp.dot(att_ref[i], wide_ref[i], preferred_element_type=F32)
+            jnp.dot(att_ref[i], wide_ref[i, parity], preferred_element_type=F32)
             for i in range(att_ref.shape[0])
         ],
     )
 
 
-def first_kernel(place_ref, att_ref, wide_ref, w_ref, out_ref, next_ref, sem):
-    fetch = pltpu.make_async_copy(w_ref.at[:, 1 - place_ref[1]], next_ref, sem)
-    fetch.start()
-    out_ref[...] = matmuls(att_ref, wide_ref)
-    fetch.wait()
-
-
-def second_kernel(part_ref, att_ref, wide_ref, out_ref):
-    total = part_ref[...] + matmuls(att_ref, wide_ref)
+def first_kernel(place_ref, att_ref, wide_ref, out_ref):
+    out_ref[...] = matmuls(att_ref, wide_ref, place_ref[1])
+
+
+def second_kernel(place_ref, part_ref, att_ref, wide_ref, out_ref):
+    total = part_ref[...] + matmuls(att_ref, wide_ref, 1 - place_ref[1])
     owners, draft, _ = out_ref.shape
     for s in range(owners):
         at = ((s % 2) * (owners // 2) + s // 2) * draft
         out_ref[s] = total[at : at + draft].astype(BF16)
 
 
-def project_own(place, att, wide, weight):
+def project_own(place, att, wide):
     chips, rows, deep = att.shape
-    cols = weight.shape[3]
+    cols = wide.shape[3]
     return pl.pallas_call(
         first_kernel,
-        in_specs=[SMEM_SPEC, VMEM_SPEC, VMEM_SPEC, pl.BlockSpec(memory_space=pl.ANY)],
-        out_specs=[VMEM_SPEC, VMEM_SPEC],
-        out_shape=[pltpu.VMEM((rows, cols), F32), pltpu.VMEM((chips, deep, cols), BF16)],
-        scratch_shapes=[pltpu.SemaphoreType.DMA],
+        in_specs=[SMEM_SPEC, VMEM_SPEC, VMEM_SPEC],
+        out_specs=VMEM_SPEC,
+        out_shape=pltpu.VMEM((rows, cols), F32),
         compiler_params=pltpu.CompilerParams(vmem_limit_bytes=8 << 20),
         cost_estimate=pl.CostEstimate(
-            flops=2 * rows * deep * chips * cols,
-            transcendentals=0,
-            bytes_accessed=2 * deep * chips * cols,
+            flops=2 * rows * deep * chips * cols, transcendentals=0, bytes_accessed=0
         ),
         name="project_own",
-    )(place, on_chip(att), on_chip(wide), in_hbm(weight))
-
-
-def project_twin(part, att, wide, owners):
+    )(place, on_chip(att), on_chip(wide))
+
+
+def project_twin(place, part, att, wide, owners):
     chips, rows, deep = att.shape
-    cols = wide.shape[2]
+    cols = wide.shape[3]
     return pl.pallas_call(
         second_kernel,
-        in_specs=[VMEM_SPEC, VMEM_SPEC, VMEM_SPEC],
+        in_specs=[SMEM_SPEC, VMEM_SPEC, VMEM_SPEC, VMEM_SPEC],
         out_specs=VMEM_SPEC,
         out_shape=pltpu.VMEM((owners, rows // owners, cols), BF16),
         compiler_params=pltpu.CompilerParams(vmem_limit_bytes=8 << 20),
@@ -374,7 +380,7 @@
             flops=2 * rows * deep * chips * cols, transcendentals=0, bytes_accessed=0
         ),
         name="project_twin",
-    )(on_chip(part), on_chip(att), on_chip(wide))
+    )(place, on_chip(part), on_chip(att), on_chip(wide))
 
 
 def shards(
@@ -422,7 +428,8 @@
     twin = from_partner(own, 0)
 
     span = min(4096, prefix_keys.shape[1])
-    mine, gone = prefix_part(place, own, twin, prefix_keys, prefix_values, span)
+    weight = out_weight.reshape(chips, 2, -1, out_weight.shape[1])
+    mine, gone, wide = prefix_part(place, own, twin, prefix_keys, prefix_values, weight, span)
     other = from_partner(gone, top_bit)
     for level in range(top_bit - 1, -1, -1):
         held = join(mine, other)
@@ -431,12 +438,11 @@
         mine = lax.dynamic_slice_in_dim(held, at * half, half, 0)
         other = from_partner(lax.dynamic_slice_in_dim(held, (1 - at) * half, half, 0), level)
 
-    weight = out_weight.reshape(chips, 2, -1, out_weight.shape[1])
-    copies, wide = merge_part(place, mine, other, own, twin, weight)
+    copies = merge_part(place, mine, other, own, twin, weight.shape[2])
     same = among_members(copies)
     twin = from_partner(same, 0)
-    part, wide = project_own(place, same, wide, weight)
-    pieces = project_twin(part, twin, wide, seq)
+    part = project_own(place, same, wide)
+    pieces = project_twin(place, part, twin, wide, seq)
     done = lax.all_to_all(pieces, "seq", split_axis=0, concat_axis=0, tiled=True)
     return done.transpose(1, 0, 2).reshape(own_rows, -1).astype(F32)
 

time: 77.4 us -> 74.7 us (0.965)
  Pallas kernels: 20.5 us -> 17.7 us
    pallas_call x3, Pallas kernels: 6.36 us -> 3.51 us  [the longest x1 1.38 us: project_twin(): pl.pallas_call(second_kernel, in_specs=[SMEM_SPEC, VMEM_SPEC, VMEM_SPEC,...]
  transfers between devices with their start and end apart: 3 -> 3, of which waited for: 2 -> 3; matrix products, arithmetic and copies ran while one was open for 0% -> 0% of each run, Pallas kernels for 4% -> 2%
where the time goes in v5:
time: 74.7 us; the launch traced here: 74.4 us
  blocking collectives  51.9 us (69%)
  Pallas kernels  17.7 us (24%)
  waiting for transfers between devices  3.29 us (4%)
    all_to_all x2, blocking collectives, among_members(): lax.all_to_all(array, 'seq', split_axis=0, concat_axis=0, axis_index_grou...  41.4 us
    all_to_all x1, blocking collectives, shards(): lax.all_to_all(pieces, 'seq', split_axis=0, concat_axis=0, tiled=True)  10.4 us
    pallas_call x1, Pallas kernels, prefix_part(): pl.pallas_call(prefix_kernel, grid=(keys.shape[1] // span,), in_specs=[SM...  10.1 us
    pallas_call x1, Pallas kernels, private_part(): pl.pallas_call(functools.partial(private_kernel, draft=draft, copies=copi...  4.03 us
    ppermute x3, waiting for transfers between devices, from_partner(): return lax.ppermute(array, 'seq', [(i, i ^ 1 << bit) for i in range(seq)])  3.29 us
  transfers between devices with their start and end apart: 3, of which 3 were waited for; matrix products, arithmetic and copies ran while one was open for 0% of the time, Pallas kernels for 2%

profile of v5, /device:TPU:2, one launch (start us, length us, event | category | flops | bytes accessed | tf_op | source)
XLA Modules:
  0.0 74.4 jit_solution(3202827757629872322)
XLA Ops:
  0.7 4.0 %private_part.1 = bf16[8,4,3200]{2,1,0:T(4,128)(2,1)} custom-call(s32[4]{0:T(128)} %par_ref.1, s32[1]{0:T(128)S(6)} %copy.11.len_ref, bf16[4,8192]{1,0:T(4,128)(2,1)} %q_ref.1, bf16[4,1024]{1,0:T(4,128)(2,1)} %dk_ref.1, bf16[4,1024]{1,0:T(4,128)(2,1)} %dv_ref.1, bf16[1,1024,1024]{2,1,0:T(8,128)(2,1)} %k_ref.2, bf16[1,1024,1024]{2,1,0:T(8,128)(2,1)} %v_ref.2), custom_call_target="tpu_custom_call" | custom-call | flops 134217728 | bytes 4194304 | tf_op jit(solution)/shard_map/private_part/pallas_call | solution.py:112
  4.7 13.9 %all_to_all.15.own_ref = bf16[8,4,3200]{2,1,0:T(4,128)(2,1)S(1)} all-to-all(bf16[8,4,3200]{2,1,0:T(4,128)(2,1)} %private_part.1), channel_id=1, replica_groups={{0,2,4,6,8,10,12,14},{1,3,5,7,9,11,13,15},{16,18,20,22,24,26,28,30},{17..., dimensions={0} | all-to-all | bytes 409600 | tf_op jit(solution)/shard_map/all_to_all | solution.py:412
  18.6 0.0 collective-permute-start
  18.6 0.1 pad_add_fusion.place_ref
  18.7 1.4 %collective-permute-done.twin_ref = bf16[8,4,3200]{2,1,0:T(4,128)(2,1)S(1)} collective-permute-done((bf16[8,4,3200]{2,1,0:T(4,128)(2,1)S(1)}, bf16[8,4,3200]{2,1,0:T(4,128)(2,1)S(1)}, u32[]{:S(2)}, u32[]{:S(2)}) %collective-permute-start) | collective-permute-done | bytes 204832 | tf_op jit(solution)/shard_map/ppermute | solution.py:409
  20.0 10.1 %prefix_part.1 = (f32[256,256]{1,0:T(8,128)S(1)}, f32[256,256]{1,0:T(8,128)S(1)}, bf16[8,2,512,512]{3,2,1,0:T(8,128)(2,1)S(1)}) custom-call(s32[3]{0:T(128)S(1)} %pad_add_fusion.place_ref, bf16[8,4,3200]{2,1,0:T(4,128)(2,1)S(1)} %all_to_all.15.own_ref, bf16[8,4,3200]{2,1,0:T(4,128)(2,1)S(1)} %collective-permute-done.twin_ref, bf16[1,16384,128]{2,1,0:T(8,128)(2,1)} %k_ref.3, ...), custom_call_target="tpu_custom_call" | custom-call | flops 4294967296 | bytes 8388608 | tf_op jit(solution)/shard_map/prefix_part/pallas_call | solution.py:231
  30.2 0.2 collective-permute-start.1
  30.4 1.4 %collective-permute-done.1.other_ref = f32[256,256]{1,0:T(8,128)S(1)} collective-permute-done((f32[256,256]{1,0:T(8,128)S(1)}, f32[256,256]{1,0:T(8,128)S(1)}, u32[]{:S(2)}, u32[]{:S(2)}) %collective-permute-start.1) | collective-permute-done | bytes 262176 | tf_op jit(solution)/shard_map/ppermute | solution.py:409
  31.8 0.8 %merge_part.1 = bf16[8,64,512]{2,1,0:T(8,128)(2,1)S(1)} custom-call(s32[3]{0:T(128)S(1)} %pad_add_fusion.place_ref, f32[256,256]{1,0:T(8,128)S(1)} %get-tuple-element.8.mine_ref, f32[256,256]{1,0:T(8,128)S(1)} %collective-permute-done.1.other_ref, bf16[8,4,3200]{2,1,0:T(4,128)(2,1)S(1)} %all_to_all.15.own_ref, ...), custom_call_target="tpu_custom_call" | custom-call | flops 524288 | tf_op jit(solution)/shard_map/merge_part/pallas_call | solution.py:315
  32.5 27.5 %all_to_all.16.att_ref = bf16[8,64,512]{2,1,0:T(8,128)(2,1)S(1)} all-to-all(bf16[8,64,512]{2,1,0:T(8,128)(2,1)S(1)} %merge_part.1), channel_id=1, replica_groups={{0,2,4,6,8,10,12,14},{1,3,5,7,9,11,13,15},{16,18,20,22,24,26,28,30},{17..., dimensions={0} | all-to-all | bytes 1048576 | tf_op jit(solution)/shard_map/all_to_all | solution.py:412
  60.0 0.0 collective-permute-start.2
  60.0 1.4 %project_own.1.part_ref = f32[64,512]{1,0:T(8,128)S(1)} custom-call(s32[3]{0:T(128)S(1)} %pad_add_fusion.place_ref, bf16[8,64,512]{2,1,0:T(8,128)(2,1)S(1)} %all_to_all.16.att_ref, bf16[8,2,512,512]{3,2,1,0:T(8,128)(2,1)S(1)} %get-tuple-element.10.wide_ref), custom_call_target="tpu_custom_call" | custom-call | flops 268435456 | tf_op jit(solution)/shard_map/project_own/pallas_call | solution.py:357
  61.4 0.5 collective-permute-done.2.att_ref
  61.9 1.4 %project_twin.1 = bf16[16,4,512]{2,1,0:T(4,128)(2,1)S(1)} custom-call(s32[3]{0:T(128)S(1)} %pad_add_fusion.place_ref, f32[64,512]{1,0:T(8,128)S(1)} %project_own.1.part_ref, bf16[8,64,512]{2,1,0:T(8,128)(2,1)S(1)} %collective-permute-done.2.att_ref, bf16[8,2,512,512]{3,2,1,0:T(8,128)(2,1)S(1)} %get-tuple-element.10.wide_ref), custom_call_target="tpu_custom_call" | custom-call | flops 268435456 | tf_op jit(solution)/shard_map/project_twin/pallas_call | solution.py:373
  63.3 10.4 %all_to_all.17 = bf16[16,4,512]{2,1,0:T(4,128)(2,1)S(1)} all-to-all(bf16[16,4,512]{2,1,0:T(4,128)(2,1)S(1)} %project_twin.1), channel_id=1, replica_groups=mesh['groups'=2,'seq'=16] {'seq'}, dimensions={0} | all-to-all | bytes 131072 | tf_op jit(solution)/shard_map/all_to_all | solution.py:446
  73.8 0.7 convert_element_type.13
Async XLA Ops:
  18.6 1.5 %collective-permute-start = (bf16[8,4,3200]{2,1,0:T(4,128)(2,1)S(1)}, bf16[8,4,3200]{2,1,0:T(4,128)(2,1)S(1)}, u32[]{:S(2)}, u32[]{:S(2)}) collective-permute-start(bf16[8,4,3200]{2,1,0:T(4,128)(2,1)S(1)} %all_to_all.15.own_ref), channel_id=1, source_target_pairs={{0,1},{1,0},{2,3},{3,2},{4,5},{5,4},{6,7},{7,6},{8,9},{9,8},{10,11... | collective-permute-start | bytes 614408 | tf_op jit(solution)/shard_map/ppermute | solution.py:409
  30.2 1.6 %collective-permute-start.1 = (f32[256,256]{1,0:T(8,128)S(1)}, f32[256,256]{1,0:T(8,128)S(1)}, u32[]{:S(2)}, u32[]{:S(2)}) collective-permute-start(f32[256,256]{1,0:T(8,128)S(1)} %get-tuple-element.9), channel_id=1, source_target_pairs={{0,1},{1,0},{2,3},{3,2},{4,5},{5,4},{6,7},{7,6},{8,9},{9,8},{10,11... | collective-permute-start | bytes 786440 | tf_op jit(solution)/shard_map/ppermute | solution.py:409
  60.0 1.9 %collective-permute-start.2 = (bf16[8,64,512]{2,1,0:T(8,128)(2,1)S(1)}, bf16[8,64,512]{2,1,0:T(8,128)(2,1)S(1)}, u32[]{:S(2)}, u32[]{:S(2)}) collective-permute-start(bf16[8,64,512]{2,1,0:T(8,128)(2,1)S(1)} %all_to_all.16.att_ref), channel_id=1, source_target_pairs={{0,1},{1,0},{2,3},{3,2},{4,5},{5,4},{6,7},{7,6},{8,9},{9,8},{10,11... | collective-permute-start | bytes 1572872 | tf_op jit(solution)/shard_map/ppermute | solution.py:409

commit v6 on v5

--- a/solution.py
+++ b/solution.py
@@ -6,7 +6,6 @@
 from jax.experimental import pallas as pl
 from jax.experimental.pallas import tpu as pltpu
 from jax.sharding import PartitionSpec as P
-
 
 HEADS = 64
 KVH = 8
@@ -277,7 +276,7 @@
 ):
     chips, draft, _ = own_ref.shape
     half = chips * draft
-    wide = att_ref.shape[2]
+    wide = att_ref.shape[1]
     heads = wide // HD
     first_head = place_ref[2] * heads
     col = pl.multiple_of(first_head * HD, wide)
@@ -305,8 +304,7 @@
             scale_p = jnp.exp(lse_p - top)
             mixed = scale_a * mine_ref[part, :HD] + scale_b * other_ref[part, :HD] + scale_p * out_p
             mixed = (mixed / (scale_a + scale_b + scale_p)).astype(BF16)
-            for copy in range(att_ref.shape[0]):
-                att_ref[copy, p * half : (p + 1) * half, h * HD : (h + 1) * HD] = mixed
+            att_ref[p * half : (p + 1) * half, h * HD : (h + 1) * HD] = mixed
 
 
 def merge_part(place, mine, other, own, twin, deep):
@@ -316,7 +314,7 @@
         merge_kernel,
         in_specs=[SMEM_SPEC] + [VMEM_SPEC] * 4,
         out_specs=VMEM_SPEC,
-        out_shape=pltpu.VMEM((chips, 2 * half, deep), BF16),
+        out_shape=pltpu.VMEM((2 * half, deep), BF16),
         scratch_shapes=[
             pltpu.VMEM((half, deep + LANES), F32),
             pltpu.VMEM((half, deep + LANES), F32),
@@ -329,58 +327,44 @@
     )(place, on_chip(mine), on_chip(other), on_chip(own), on_chip(twin))
 
 
-def matmuls(att_ref, wide_ref, parity):
-    return functools.reduce(
+def project_kernel(place_ref, *refs, masks, first):
+    part_ref, refs = (None, refs) if first else (refs[0], refs[1:])
+    wide_ref, out_ref = refs[len(masks) :]
+    total = functools.reduce(
         jnp.add,
         [
-            jnp.dot(att_ref[i], wide_ref[i, parity], preferred_element_type=F32)
-            for i in range(att_ref.shape[0])
+            jnp.dot(ref[...], wide_ref[place_ref[3] ^ mask], preferred_element_type=F32)
+            for ref, mask in zip(refs, masks)
         ],
     )
-
-
-def first_kernel(place_ref, att_ref, wide_ref, out_ref):
-    out_ref[...] = matmuls(att_ref, wide_ref, place_ref[1])
-
-
-def second_kernel(place_ref, part_ref, att_ref, wide_ref, out_ref):
-    total = part_ref[...] + matmuls(att_ref, wide_ref, 1 - place_ref[1])
+    if first:
+        out_ref[...] = total
+        return
+    total = total + part_ref[...]
     owners, draft, _ = out_ref.shape
     for s in range(owners):
         at = ((s % 2) * (owners // 2) + s // 2) * draft
         out_ref[s] = total[at : at + draft].astype(BF16)
 
 
-def project_own(place, att, wide):
-    chips, rows, deep = att.shape
-    cols = wide.shape[3]
+def project(place, part, chunks, wide):
+    masks = tuple(chunks)
+    rows, deep = chunks[masks[0]].shape
+    owners, _, cols = wide.shape
+    first = part is None
+    arrays = ([] if first else [part]) + [chunks[mask] for mask in masks] + [wide]
+    shape = (rows, cols) if first else (owners, rows // owners, cols)
     return pl.pallas_call(
-        first_kernel,
-        in_specs=[SMEM_SPEC, VMEM_SPEC, VMEM_SPEC],
+        functools.partial(project_kernel, masks=masks, first=first),
+        in_specs=[SMEM_SPEC] + [VMEM_SPEC] * len(arrays),
         out_specs=VMEM_SPEC,
-        out_shape=pltpu.VMEM((rows, cols), F32),
+        out_shape=pltpu.VMEM(shape, F32 if first else BF16),
         compiler_params=pltpu.CompilerParams(vmem_limit_bytes=8 << 20),
         cost_estimate=pl.CostEstimate(
-            flops=2 * rows * deep * chips * cols, transcendentals=0, bytes_accessed=0
+            flops=2 * rows * deep * len(masks) * cols, transcendentals=0, bytes_accessed=0
         ),
-        name="project_own",
-    )(place, on_chip(att), on_chip(wide))
-
-
-def project_twin(place, part, att, wide, owners):
-    chips, rows, deep = att.shape
-    cols = wide.shape[3]
-    return pl.pallas_call(
-        second_kernel,
-        in_specs=[SMEM_SPEC, VMEM_SPEC, VMEM_SPEC, VMEM_SPEC],
-        out_specs=VMEM_SPEC,
-        out_shape=pltpu.VMEM((owners, rows // owners, cols), BF16),
-        compiler_params=pltpu.CompilerParams(vmem_limit_bytes=8 << 20),
-        cost_estimate=pl.CostEstimate(
-            flops=2 * rows * deep * chips * cols, transcendentals=0, bytes_accessed=0
-        ),
-        name="project_twin",
-    )(place, on_chip(part), on_chip(att), on_chip(wide))
+        name="project_first" if first else "project_last",
+    )(place, *[on_chip(array) for array in arrays])
 
 
 def shards(
@@ -402,7 +386,7 @@
     device = lax.axis_index("seq")
     rank = device % blocks
     top_bit = blocks.bit_length() - 2
-    place = jnp.stack([(rank >> top_bit) & 1, device % 2, rank]).astype(jnp.int32)
+    place = jnp.stack([(rank >> top_bit) & 1, device % 2, rank, device]).astype(jnp.int32)
     members = [list(range(c, seq, 2)) for c in range(2)]
 
     def from_partner(array, bit):
@@ -428,7 +412,7 @@
     twin = from_partner(own, 0)
 
     span = min(4096, prefix_keys.shape[1])
-    weight = out_weight.reshape(chips, 2, -1, out_weight.shape[1])
+    weight = out_weight.reshape(seq, -1, out_weight.shape[1])
     mine, gone, wide = prefix_part(place, own, twin, prefix_keys, prefix_values, weight, span)
     other = from_partner(gone, top_bit)
     for level in range(top_bit - 1, -1, -1):
@@ -438,11 +422,23 @@
         mine = lax.dynamic_slice_in_dim(held, at * half, half, 0)
         other = from_partner(lax.dynamic_slice_in_dim(held, (1 - at) * half, half, 0), level)
 
-    copies = merge_part(place, mine, other, own, twin, weight.shape[2])
-    same = among_members(copies)
-    twin = from_partner(same, 0)
-    part = project_own(place, same, wide)
-    pieces = project_twin(place, part, twin, wide, seq)
+    chunks = {0: merge_part(place, mine, other, own, twin, weight.shape[1])}
+
+    def move(mask, source):
+        chunks[mask] = lax.ppermute(
+            chunks[source], "seq", [(i, i ^ mask ^ source) for i in range(seq)]
+        )
+
+    far = [4 * k for k in range(1, chips // 2)]
+    for mask in [2] + far:
+        move(mask, 0)
+    for mask in far:
+        move(mask + 2, mask)
+    for mask in list(chunks):
+        move(mask + 1, mask)
+    late = (far[-1] + 2, far[-1] + 3)
+    part = project(place, None, {m: chunks[m] for m in chunks if m not in late}, wide)
+    pieces = project(place, part, {m: chunks[m] for m in late}, wide)
     done = lax.all_to_all(pieces, "seq", split_axis=0, concat_axis=0, tiled=True)
     return done.transpose(1, 0, 2).reshape(own_rows, -1).astype(F32)
 

time: 74.7 us -> 71.3 us (0.954)
  blocking collectives: 51.9 us -> 25.7 us
  starting transfers between devices: 0.22 us -> 15.5 us
  waiting for transfers between devices: 3.29 us -> 10.7 us
    all_to_all x2 -> x1, blocking collectives: 41.4 us -> 13.9 us  [among_members(): lax.all_to_all(array, 'seq', split_axis=0, concat_axis=0, axis_index_grou...]
    ppermute x0 -> x15, starting transfers between devices: none -> 15.3 us  [move(): lax.ppermute(chunks[source], 'seq', [(i, i ^ mask ^ source) for i in rang...]
    ppermute x0 -> x15, waiting for transfers between devices: none -> 7.88 us  [move(): lax.ppermute(chunks[source], 'seq', [(i, i ^ mask ^ source) for i in rang...]
    all_to_all x1, blocking collectives: 10.4 us -> 11.8 us  [shards(): lax.all_to_all(pieces, 'seq', split_axis=0, concat_axis=0, tiled=True)]
    ppermute x3 -> x2, waiting for transfers between devices: 3.29 us -> 2.78 us  [from_partner(): return lax.ppermute(array, 'seq', [(i, i ^ 1 << bit) for i in range(seq)])]
  transfers between devices with their start and end apart: 3 -> 17, of which waited for: 3 -> 8; matrix products, arithmetic and copies ran while one was open for 0% -> 0% of each run, Pallas kernels for 2% -> 3%
where the time goes in v6:
time: 71.3 us; the launch traced here: 71 us
  blocking collectives  25.7 us (36%)
  Pallas kernels  17.6 us (25%)
  starting transfers between devices  15.5 us (22%)
  waiting for transfers between devices  10.7 us (15%)
  other arithmetic  0.74 us (1%)
    ppermute x15, starting transfers between devices, move(): lax.ppermute(chunks[source], 'seq', [(i, i ^ mask ^ source) for i in rang...  15.3 us
    all_to_all x1, blocking collectives, among_members(): lax.all_to_all(array, 'seq', split_axis=0, concat_axis=0, axis_index_grou...  13.9 us
    all_to_all x1, blocking collectives, shards(): lax.all_to_all(pieces, 'seq', split_axis=0, concat_axis=0, tiled=True)  11.8 us
    pallas_call x1, Pallas kernels, prefix_part(): pl.pallas_call(prefix_kernel, grid=(keys.shape[1] // span,), in_specs=[SM...  10.1 us
    ppermute x15, waiting for transfers between devices, move(): lax.ppermute(chunks[source], 'seq', [(i, i ^ mask ^ source) for i in rang...  7.88 us
    pallas_call x1, Pallas kernels, private_part(): pl.pallas_call(functools.partial(private_kernel, draft=draft, copies=copi...  4.02 us
    ppermute x2, waiting for transfers between devices, from_partner(): return lax.ppermute(array, 'seq', [(i, i ^ 1 << bit) for i in range(seq)])  2.78 us
    pallas_call x2, Pallas kernels, project(): pl.pallas_call(functools.partial(project_kernel, masks=masks, first=first...  2.76 us
  transfers between devices with their start and end apart: 17, of which 8 were waited for; matrix products, arithmetic and copies ran while one was open for 0% of the time, Pallas kernels for 3%

profile of v6, /device:TPU:2, one launch (start us, length us, event | category | flops | bytes accessed | tf_op | source)
XLA Modules:
  0.0 71.0 jit_solution(371639894336496285)
XLA Ops:
  0.7 4.0 %private_part.1 = bf16[8,4,3200]{2,1,0:T(4,128)(2,1)} custom-call(s32[4]{0:T(128)} %par_ref.1, s32[1]{0:T(128)S(6)} %copy.11.len_ref, bf16[4,8192]{1,0:T(4,128)(2,1)} %q_ref.1, bf16[4,1024]{1,0:T(4,128)(2,1)} %dk_ref.1, bf16[4,1024]{1,0:T(4,128)(2,1)} %dv_ref.1, bf16[1,1024,1024]{2,1,0:T(8,128)(2,1)} %k_ref.2, bf16[1,1024,1024]{2,1,0:T(8,128)(2,1)} %v_ref.2), custom_call_target="tpu_custom_call" | custom-call | flops 134217728 | bytes 4194304 | tf_op jit(solution)/shard_map/private_part/pallas_call | solution.py:111
  4.7 13.9 %all_to_all.10.own_ref = bf16[8,4,3200]{2,1,0:T(4,128)(2,1)S(1)} all-to-all(bf16[8,4,3200]{2,1,0:T(4,128)(2,1)} %private_part.1), channel_id=1, replica_groups={{0,2,4,6,8,10,12,14},{1,3,5,7,9,11,13,15},{16,18,20,22,24,26,28,30},{17..., dimensions={0} | all-to-all | bytes 409600 | tf_op jit(solution)/shard_map/all_to_all | solution.py:396
  18.6 0.0 collective-permute-start
  18.6 0.1 pad_add_fusion.place_ref
  18.7 1.4 %collective-permute-done.twin_ref = bf16[8,4,3200]{2,1,0:T(4,128)(2,1)S(1)} collective-permute-done((bf16[8,4,3200]{2,1,0:T(4,128)(2,1)S(1)}, bf16[8,4,3200]{2,1,0:T(4,128)(2,1)S(1)}, u32[]{:S(2)}, u32[]{:S(2)}) %collective-permute-start) | collective-permute-done | bytes 204832 | tf_op jit(solution)/shard_map/ppermute | solution.py:393
  20.0 10.1 %prefix_part.1 = (f32[256,256]{1,0:T(8,128)S(1)}, f32[256,256]{1,0:T(8,128)S(1)}, bf16[16,512,512]{2,1,0:T(8,128)(2,1)S(1)}) custom-call(s32[4]{0:T(128)S(1)} %pad_add_fusion.place_ref, bf16[8,4,3200]{2,1,0:T(4,128)(2,1)S(1)} %all_to_all.10.own_ref, bf16[8,4,3200]{2,1,0:T(4,128)(2,1)S(1)} %collective-permute-done.twin_ref, bf16[1,16384,128]{2,1,0:T(8,128)(2,1)} %k_ref.3, ...), custom_call_target="tpu_custom_call" | custom-call | flops 4294967296 | bytes 8388608 | tf_op jit(solution)/shard_map/prefix_part/pallas_call | solution.py:230
  30.2 0.2 collective-permute-start.1
  30.4 1.4 %collective-permute-done.1.other_ref = f32[256,256]{1,0:T(8,128)S(1)} collective-permute-done((f32[256,256]{1,0:T(8,128)S(1)}, f32[256,256]{1,0:T(8,128)S(1)}, u32[]{:S(2)}, u32[]{:S(2)}) %collective-permute-start.1) | collective-permute-done | bytes 262176 | tf_op jit(solution)/shard_map/ppermute | solution.py:393
  31.8 0.7 %merge_part.1.refs_0_ = bf16[64,512]{1,0:T(8,128)(2,1)S(1)} custom-call(s32[4]{0:T(128)S(1)} %pad_add_fusion.place_ref, f32[256,256]{1,0:T(8,128)S(1)} %get-tuple-element.8.mine_ref, f32[256,256]{1,0:T(8,128)S(1)} %collective-permute-done.1.other_ref, bf16[8,4,3200]{2,1,0:T(4,128)(2,1)S(1)} %all_to_all.10.own_ref, ...), custom_call_target="tpu_custom_call" | custom-call | flops 524288 | tf_op jit(solution)/shard_map/merge_part/pallas_call | solution.py:313
  32.5 11.5 %collective-permute-start.5 = (bf16[64,512]{1,0:T(8,128)(2,1)S(1)}, bf16[64,512]{1,0:T(8,128)(2,1)S(1)}, u32[]{:S(2)}, u32[]{:S(2)}) collective-permute-start(bf16[64,512]{1,0:T(8,128)(2,1)S(1)} %merge_part.1.refs_0_), channel_id=1, source_target_pairs={{0,12},{1,13},{2,14},{3,15},{4,8},{5,9},{6,10},{7,11},{8,4},{9,5},... | collective-permute-start | bytes 196616 | tf_op jit(solution)/shard_map/ppermute | solution.py:428
  44.0 0.1 collective-permute-start.8
  44.1 0.0 collective-permute-start.4
  44.1 0.9 %collective-permute-start.3 = (bf16[64,512]{1,0:T(8,128)(2,1)S(1)}, bf16[64,512]{1,0:T(8,128)(2,1)S(1)}, u32[]{:S(2)}, u32[]{:S(2)}) collective-permute-start(bf16[64,512]{1,0:T(8,128)(2,1)S(1)} %merge_part.1.refs_0_), channel_id=1, source_target_pairs={{0,4},{1,5},{2,6},{3,7},{4,0},{5,1},{6,2},{7,3},{8,12},{9,13},{10,... | collective-permute-start | bytes 196616 | tf_op jit(solution)/shard_map/ppermute | solution.py:428
  45.0 0.0 collective-permute-start.2
  45.0 1.9 %collective-permute-done.5.refs_4_ = bf16[64,512]{1,0:T(8,128)(2,1)S(1)} collective-permute-done((bf16[64,512]{1,0:T(8,128)(2,1)S(1)}, bf16[64,512]{1,0:T(8,128)(2,1)S(1)}, u32[]{:S(2)}, u32[]{:S(2)}) %collective-permute-start.5) | collective-permute-done | bytes 65568 | tf_op jit(solution)/shard_map/ppermute | solution.py:428
  46.9 0.1 collective-permute-start.15
  47.0 0.0 collective-permute-done.8.refs_7_
  47.0 0.0 collective-permute-start.12
  47.0 2.5 %collective-permute-done.4.refs_3_ = bf16[64,512]{1,0:T(8,128)(2,1)S(1)} collective-permute-done((bf16[64,512]{1,0:T(8,128)(2,1)S(1)}, bf16[64,512]{1,0:T(8,128)(2,1)S(1)}, u32[]{:S(2)}, u32[]{:S(2)}) %collective-permute-start.4) | collective-permute-done | bytes 65568 | tf_op jit(solution)/shard_map/ppermute | solution.py:428
  49.5 0.0 collective-permute-start.7
  49.5 0.4 collective-permute-done.3.refs_2_
  49.9 1.7 %collective-permute-start.6 = (bf16[64,512]{1,0:T(8,128)(2,1)S(1)}, bf16[64,512]{1,0:T(8,128)(2,1)S(1)}, u32[]{:S(2)}, u32[]{:S(2)}) collective-permute-start(bf16[64,512]{1,0:T(8,128)(2,1)S(1)} %collective-permute-done.3.refs_2_), channel_id=1, source_target_pairs={{0,2},{1,3},{2,0},{3,1},{4,6},{5,7},{6,4},{7,5},{8,10},{9,11},{10,... | collective-permute-start | bytes 196616 | tf_op jit(solution)/shard_map/ppermute | solution.py:428
  51.6 0.0 collective-permute-done.2.refs_1_
  51.6 0.0 collective-permute-start.11
  51.6 0.0 collective-permute-done.15.refs_1_
  51.6 0.5 collective-permute-start.10
  52.1 0.0 collective-permute-done.12.refs_11_
  52.1 0.1 collective-permute-start.9
  52.1 1.6 %collective-permute-done.7.refs_6_ = bf16[64,512]{1,0:T(8,128)(2,1)S(1)} collective-permute-done((bf16[64,512]{1,0:T(8,128)(2,1)S(1)}, bf16[64,512]{1,0:T(8,128)(2,1)S(1)}, u32[]{:S(2)}, u32[]{:S(2)}) %collective-permute-start.7) | collective-permute-done | bytes 65568 | tf_op jit(solution)/shard_map/ppermute | solution.py:428
  53.8 0.0 collective-permute-start.14
  53.8 0.7 collective-permute-done.6.refs_5_
  54.5 0.0 collective-permute-start.13
  54.5 0.0 collective-permute-done.11.refs_10_
  54.5 0.5 collective-permute-start.16
  55.0 0.0 collective-permute-done.10.refs_9_
  55.0 0.0 collective-permute-done.9.refs_8_
  55.0 0.0 collective-permute-done.14.refs_13_
  55.0 0.7 collective-permute-done.13.refs_12_
  55.7 1.9 %project_first.1.refs_0_ = f32[64,512]{1,0:T(8,128)S(1)} custom-call(s32[4]{0:T(128)S(1)} %pad_add_fusion.place_ref, bf16[64,512]{1,0:T(8,128)(2,1)S(1)} %merge_part.1.refs_0_, bf16[64,512]{1,0:T(8,128)(2,1)S(1)} %collective-permute-done.2.refs_1_, bf16[64,512]{1,0:T(8,128)(2,1)S(1)} %collective-permute-done.3.refs_2_, ...), custom_call_target="tpu_custom_call" | custom-call | flops 469762048 | tf_op jit(solution)/shard_map/project_first/pallas_call | solution.py:357
  57.7 0.0 collective-permute-done.16.refs_2_
  57.7 0.8 %project_last.1 = bf16[16,4,512]{2,1,0:T(4,128)(2,1)S(1)} custom-call(s32[4]{0:T(128)S(1)} %pad_add_fusion.place_ref, f32[64,512]{1,0:T(8,128)S(1)} %project_first.1.refs_0_, bf16[64,512]{1,0:T(8,128)(2,1)S(1)} %collective-permute-done.15.refs_1_, bf16[64,512]{1,0:T(8,128)(2,1)S(1)} %collective-permute-done.16.refs_2_, ...), custom_call_target="tpu_custom_call" | custom-call | flops 67108864 | tf_op jit(solution)/shard_map/project_last/pallas_call | solution.py:357
  58.5 11.8 %all_to_all.11 = bf16[16,4,512]{2,1,0:T(4,128)(2,1)S(1)} all-to-all(bf16[16,4,512]{2,1,0:T(4,128)(2,1)S(1)} %project_last.1), channel_id=1, replica_groups=mesh['groups'=2,'seq'=16] {'seq'}, dimensions={0} | all-to-all | bytes 131072 | tf_op jit(solution)/shard_map/all_to_all | solution.py:442
  70.3 0.7 convert_element_type.13
Async XLA Ops:
  18.6 1.5 %collective-permute-start = (bf16[8,4,3200]{2,1,0:T(4,128)(2,1)S(1)}, bf16[8,4,3200]{2,1,0:T(4,128)(2,1)S(1)}, u32[]{:S(2)}, u32[]{:S(2)}) collective-permute-start(bf16[8,4,3200]{2,1,0:T(4,128)(2,1)S(1)} %all_to_all.10.own_ref), channel_id=1, source_target_pairs={{0,1},{1,0},{2,3},{3,2},{4,5},{5,4},{6,7},{7,6},{8,9},{9,8},{10,11... | collective-permute-start | bytes 614408 | tf_op jit(solution)/shard_map/ppermute | solution.py:393
  30.2 1.6 %collective-permute-start.1 = (f32[256,256]{1,0:T(8,128)S(1)}, f32[256,256]{1,0:T(8,128)S(1)}, u32[]{:S(2)}, u32[]{:S(2)}) collective-permute-start(f32[256,256]{1,0:T(8,128)S(1)} %get-tuple-element.9), channel_id=1, source_target_pairs={{0,1},{1,0},{2,3},{3,2},{4,5},{5,4},{6,7},{7,6},{8,9},{9,8},{10,11... | collective-permute-start | bytes 786440 | tf_op jit(solution)/shard_map/ppermute | solution.py:393
  32.5 14.4 %collective-permute-start.5 = (bf16[64,512]{1,0:T(8,128)(2,1)S(1)}, bf16[64,512]{1,0:T(8,128)(2,1)S(1)}, u32[]{:S(2)}, u32[]{:S(2)}) collective-permute-start(bf16[64,512]{1,0:T(8,128)(2,1)S(1)} %merge_part.1.refs_0_), channel_id=1, source_target_pairs={{0,12},{1,13},{2,14},{3,15},{4,8},{5,9},{6,10},{7,11},{8,4},{9,5},... | collective-permute-start | bytes 196616 | tf_op jit(solution)/shard_map/ppermute | solution.py:428
  44.0 3.1 %collective-permute-start.8 = (bf16[64,512]{1,0:T(8,128)(2,1)S(1)}, bf16[64,512]{1,0:T(8,128)(2,1)S(1)}, u32[]{:S(2)}, u32[]{:S(2)}) collective-permute-start(bf16[64,512]{1,0:T(8,128)(2,1)S(1)} %merge_part.1.refs_0_), channel_id=1, source_target_pairs={{0,1},{1,0},{2,3},{3,2},{4,5},{5,4},{6,7},{7,6},{8,9},{9,8},{10,11... | collective-permute-start | bytes 196616 | tf_op jit(solution)/shard_map/ppermute | solution.py:428
  44.1 5.4 %collective-permute-start.4 = (bf16[64,512]{1,0:T(8,128)(2,1)S(1)}, bf16[64,512]{1,0:T(8,128)(2,1)S(1)}, u32[]{:S(2)}, u32[]{:S(2)}) collective-permute-start(bf16[64,512]{1,0:T(8,128)(2,1)S(1)} %merge_part.1.refs_0_), channel_id=1, source_target_pairs={{0,8},{1,9},{2,10},{3,11},{4,12},{5,13},{6,14},{7,15},{8,0},{9,1},... | collective-permute-start | bytes 196616 | tf_op jit(solution)/shard_map/ppermute | solution.py:428
  44.1 5.8 %collective-permute-start.3 = (bf16[64,512]{1,0:T(8,128)(2,1)S(1)}, bf16[64,512]{1,0:T(8,128)(2,1)S(1)}, u32[]{:S(2)}, u32[]{:S(2)}) collective-permute-start(bf16[64,512]{1,0:T(8,128)(2,1)S(1)} %merge_part.1.refs_0_), channel_id=1, source_target_pairs={{0,4},{1,5},{2,6},{3,7},{4,0},{5,1},{6,2},{7,3},{8,12},{9,13},{10,... | collective-permute-start | bytes 196616 | tf_op jit(solution)/shard_map/ppermute | solution.py:428
  45.0 6.6 %collective-permute-start.2 = (bf16[64,512]{1,0:T(8,128)(2,1)S(1)}, bf16[64,512]{1,0:T(8,128)(2,1)S(1)}, u32[]{:S(2)}, u32[]{:S(2)}) collective-permute-start(bf16[64,512]{1,0:T(8,128)(2,1)S(1)} %merge_part.1.refs_0_), channel_id=1, source_target_pairs={{0,2},{1,3},{2,0},{3,1},{4,6},{5,7},{6,4},{7,5},{8,10},{9,11},{10,... | collective-permute-start | bytes 196616 | tf_op jit(solution)/shard_map/ppermute | solution.py:428
  46.9 4.6 %collective-permute-start.15 = (bf16[64,512]{1,0:T(8,128)(2,1)S(1)}, bf16[64,512]{1,0:T(8,128)(2,1)S(1)}, u32[]{:S(2)}, u32[]{:S(2)}) collective-permute-start(bf16[64,512]{1,0:T(8,128)(2,1)S(1)} %collective-permute-done.5.refs_4_), channel_id=1, source_target_pairs={{0,2},{1,3},{2,0},{3,1},{4,6},{5,7},{6,4},{7,5},{8,10},{9,11},{10,... | collective-permute-start | bytes 196616 | tf_op jit(solution)/shard_map/ppermute | solution.py:428
  47.0 5.0 %collective-permute-start.12 = (bf16[64,512]{1,0:T(8,128)(2,1)S(1)}, bf16[64,512]{1,0:T(8,128)(2,1)S(1)}, u32[]{:S(2)}, u32[]{:S(2)}) collective-permute-start(bf16[64,512]{1,0:T(8,128)(2,1)S(1)} %collective-permute-done.5.refs_4_), channel_id=1, source_target_pairs={{0,1},{1,0},{2,3},{3,2},{4,5},{5,4},{6,7},{7,6},{8,9},{9,8},{10,11... | collective-permute-start | bytes 196616 | tf_op jit(solution)/shard_map/ppermute | solution.py:428
  49.5 4.3 %collective-permute-start.7 = (bf16[64,512]{1,0:T(8,128)(2,1)S(1)}, bf16[64,512]{1,0:T(8,128)(2,1)S(1)}, u32[]{:S(2)}, u32[]{:S(2)}) collective-permute-start(bf16[64,512]{1,0:T(8,128)(2,1)S(1)} %collective-permute-done.4.refs_3_), channel_id=1, source_target_pairs={{0,2},{1,3},{2,0},{3,1},{4,6},{5,7},{6,4},{7,5},{8,10},{9,11},{10,... | collective-permute-start | bytes 196616 | tf_op jit(solution)/shard_map/ppermute | solution.py:428
  49.9 4.6 %collective-permute-start.6 = (bf16[64,512]{1,0:T(8,128)(2,1)S(1)}, bf16[64,512]{1,0:T(8,128)(2,1)S(1)}, u32[]{:S(2)}, u32[]{:S(2)}) collective-permute-start(bf16[64,512]{1,0:T(8,128)(2,1)S(1)} %collective-permute-done.3.refs_2_), channel_id=1, source_target_pairs={{0,2},{1,3},{2,0},{3,1},{4,6},{5,7},{6,4},{7,5},{8,10},{9,11},{10,... | collective-permute-start | bytes 196616 | tf_op jit(solution)/shard_map/ppermute | solution.py:428
  51.6 2.9 %collective-permute-start.11 = (bf16[64,512]{1,0:T(8,128)(2,1)S(1)}, bf16[64,512]{1,0:T(8,128)(2,1)S(1)}, u32[]{:S(2)}, u32[]{:S(2)}) collective-permute-start(bf16[64,512]{1,0:T(8,128)(2,1)S(1)} %collective-permute-done.4.refs_3_), channel_id=1, source_target_pairs={{0,1},{1,0},{2,3},{3,2},{4,5},{5,4},{6,7},{7,6},{8,9},{9,8},{10,11... | collective-permute-start | bytes 196616 | tf_op jit(solution)/shard_map/ppermute | solution.py:428
  51.6 3.4 %collective-permute-start.10 = (bf16[64,512]{1,0:T(8,128)(2,1)S(1)}, bf16[64,512]{1,0:T(8,128)(2,1)S(1)}, u32[]{:S(2)}, u32[]{:S(2)}) collective-permute-start(bf16[64,512]{1,0:T(8,128)(2,1)S(1)} %collective-permute-done.3.refs_2_), channel_id=1, source_target_pairs={{0,1},{1,0},{2,3},{3,2},{4,5},{5,4},{6,7},{7,6},{8,9},{9,8},{10,11... | collective-permute-start | bytes 196616 | tf_op jit(solution)/shard_map/ppermute | solution.py:428
  52.1 2.9 %collective-permute-start.9 = (bf16[64,512]{1,0:T(8,128)(2,1)S(1)}, bf16[64,512]{1,0:T(8,128)(2,1)S(1)}, u32[]{:S(2)}, u32[]{:S(2)}) collective-permute-start(bf16[64,512]{1,0:T(8,128)(2,1)S(1)} %collective-permute-done.2.refs_1_), channel_id=1, source_target_pairs={{0,1},{1,0},{2,3},{3,2},{4,5},{5,4},{6,7},{7,6},{8,9},{9,8},{10,11... | collective-permute-start | bytes 196616 | tf_op jit(solution)/shard_map/ppermute | solution.py:428
  53.8 1.3 %collective-permute-start.14 = (bf16[64,512]{1,0:T(8,128)(2,1)S(1)}, bf16[64,512]{1,0:T(8,128)(2,1)S(1)}, u32[]{:S(2)}, u32[]{:S(2)}) collective-permute-start(bf16[64,512]{1,0:T(8,128)(2,1)S(1)} %collective-permute-done.7.refs_6_), channel_id=1, source_target_pairs={{0,1},{1,0},{2,3},{3,2},{4,5},{5,4},{6,7},{7,6},{8,9},{9,8},{10,11... | collective-permute-start | bytes 196616 | tf_op jit(solution)/shard_map/ppermute | solution.py:428
  54.5 1.3 %collective-permute-start.13 = (bf16[64,512]{1,0:T(8,128)(2,1)S(1)}, bf16[64,512]{1,0:T(8,128)(2,1)S(1)}, u32[]{:S(2)}, u32[]{:S(2)}) collective-permute-start(bf16[64,512]{1,0:T(8,128)(2,1)S(1)} %collective-permute-done.6.refs_5_), channel_id=1, source_target_pairs={{0,1},{1,0},{2,3},{3,2},{4,5},{5,4},{6,7},{7,6},{8,9},{9,8},{10,11... | collective-permute-start | bytes 196616 | tf_op jit(solution)/shard_map/ppermute | solution.py:428
  54.5 3.2 %collective-permute-start.16 = (bf16[64,512]{1,0:T(8,128)(2,1)S(1)}, bf16[64,512]{1,0:T(8,128)(2,1)S(1)}, u32[]{:S(2)}, u32[]{:S(2)}) collective-permute-start(bf16[64,512]{1,0:T(8,128)(2,1)S(1)} %collective-permute-done.15.refs_1_), channel_id=1, source_target_pairs={{0,1},{1,0},{2,3},{3,2},{4,5},{5,4},{6,7},{7,6},{8,9},{9,8},{10,11... | collective-permute-start | bytes 196616 | tf_op jit(solution)/shard_map/ppermute | solution.py:428

commit v7 on v6

v7 whole, which is shorter than its diff:
```python
import functools

import jax
import jax.numpy as jnp
from jax import lax
from jax.experimental import pallas as pl
from jax.experimental.pallas import tpu as pltpu
from jax.sharding import PartitionSpec as P


HEADS = 64
KVH = 8
HD = 128
GROUP = HEADS // KVH
SCALE = HD ** (-0.5)
LOG2E = 1.4426950408889634
LANES = 128
NEG = -1e30
LIMIT = 2.0**100
WIDE = GROUP * HD
MESSAGE = 3 * WIDE + LANES
NT = (((1,), (1,)), ((), ()))
TN = (((0,), (0,)), ((), ()))
F32 = jnp.float32
BF16 = jnp.bfloat16


def in_hbm(array):
    return pltpu.with_memory_space_constraint(array, pltpu.HBM)


def on_chip(array):
    return pltpu.with_memory_space_constraint(array, pltpu.VMEM)


VMEM_SPEC = pl.BlockSpec(memory_space=pltpu.VMEM)
SMEM_SPEC = pl.BlockSpec(memory_space=pltpu.SMEM)


def private_kernel(
    place_ref, par_ref, len_ref, q_ref, dk_ref, dv_ref, k_ref, v_ref, out_ref, *, draft, copies, batch
):
    rows = GROUP * draft
    slots = k_ref.shape[1]
    seen = []
    for i in range(draft):
        bits = jnp.int32(1 << i)
        for j in range(i):
            bits = bits | jnp.where(par_ref[i] == j, seen[j], 0)
        seen.append(bits)
    row = lax.broadcasted_iota(jnp.int32, (rows, LANES), 0) % draft
    lane = lax.broadcasted_iota(jnp.int32, (rows, LANES), 1)
    mask = jnp.zeros((rows, LANES), jnp.int32)
    for i in range(draft):
        mask = jnp.where(row == i, seen[i], mask)
    shown = (lane < draft) & ((lax.shift_right_logical(mask, jnp.minimum(lane, 31)) & 1) == 1)
    live = lax.broadcasted_iota(jnp.int32, (rows, slots), 1) < len_ref[0]
    fill = jnp.zeros((LANES - draft, HD), F32)
    stat_lane = lax.broadcasted_iota(jnp.int32, (draft, LANES), 1)
    groups = range(batch)
    queries = []
    for g in groups:
        q = q_ref[:, g * WIDE : (g + 1) * WIDE]
        for copy in range(copies):
            out_ref[g * copies + copy, :, :WIDE] = q
        q32 = q.astype(F32)
        queries.append(
            jnp.concatenate([q32[:, h * HD : (h + 1) * HD] for h in range(GROUP)], axis=0).astype(BF16)
        )
    cols = [slice(g * HD, (g + 1) * HD) for g in groups]
    scores = [
        lax.dot_general(queries[g], k_ref[0, :, cols[g]], NT, preferred_element_type=F32) for g in groups
    ]
    trees = []
    for g in groups:
        dkey = jnp.concatenate([dk_ref[:, cols[g]].astype(F32), fill], axis=0).astype(BF16)
        trees.append(lax.dot_general(queries[g], dkey, NT, preferred_element_type=F32))
    for g in groups:
        score = jnp.where(live, scores[g] * SCALE, NEG)
        tree = jnp.where(shown, trees[g] * SCALE, NEG)
        tiles = [score[:, j : j + LANES] for j in range(0, slots, LANES)] + [tree]
        peak = jnp.max(functools.reduce(jnp.maximum, tiles), axis=1, keepdims=True)
        tiles = [jnp.exp(tile - peak) for tile in tiles]
        denom = jnp.sum(functools.reduce(jnp.add, tiles), axis=1, keepdims=True)
        weights = jnp.concatenate([tile.astype(BF16) for tile in tiles[:-1]], axis=1)
        dval = jnp.concatenate([dv_ref[:, cols[g]].astype(F32), fill], axis=0).astype(BF16)
        mixture = jnp.dot(weights, v_ref[0, :, cols[g]], preferred_element_type=F32)
        mixture = mixture + jnp.dot(tiles[-1].astype(BF16), dval, preferred_element_type=F32)
        mixture = mixture / denom
        coarse = mixture.astype(BF16).astype(F32)
        fine = mixture - coarse
        lse = peak + jnp.log(denom)
        first = lse.astype(BF16).astype(F32)
        second = (lse - first).astype(BF16).astype(F32)
        third = lse - first - second
        stats = jnp.zeros((draft, LANES), F32)
        for copy in range(copies):
            at = g * copies + copy
            for h in range(GROUP):
                part = slice(h * draft, (h + 1) * draft)
                out_ref[at, :, WIDE + h * HD : WIDE + (h + 1) * HD] = coarse[part].astype(BF16)
                out_ref[at, :, 2 * WIDE + h * HD : 2 * WIDE + (h + 1) * HD] = fine[part].astype(BF16)
                if copy == 0:
                    for t, term in enumerate((first, second, third)):
                        stats = jnp.where(stat_lane == 3 * h + t, term[part], stats)
            out_ref[at, :, 3 * WIDE :] = stats.astype(BF16)


def private_part(place, parents, lengths, queries, dkeys, dvals, pkeys, pvals, copies, batch):
    draft = queries.shape[0]
    slots = pkeys.shape[1]
    return pl.pallas_call(
        functools.partial(private_kernel, draft=draft, copies=copies, batch=batch),
        grid=(KVH // batch,),
        in_specs=[
            SMEM_SPEC,
            SMEM_SPEC,
            SMEM_SPEC,
            pl.BlockSpec((draft, batch * WIDE), lambda g: (0, g)),
            pl.BlockSpec((draft, batch * HD), lambda g: (0, g)),
            pl.BlockSpec((draft, batch * HD), lambda g: (0, g)),
            pl.BlockSpec((1, slots, batch * HD), lambda g: (0, 0, g)),
            pl.BlockSpec((1, slots, batch * HD), lambda g: (0, 0, g)),
        ],
        out_specs=pl.BlockSpec((batch * copies, draft, MESSAGE), lambda g: (g, 0, 0)),
        out_shape=jax.ShapeDtypeStruct((KVH * copies, draft, MESSAGE), BF16),
        compiler_params=pltpu.CompilerParams(vmem_limit_bytes=20 << 20),
        cost_estimate=pl.CostEstimate(
            flops=4 * draft * HEADS * slots * HD,
            transcendentals=draft * HEADS * slots,
            bytes_accessed=4 * slots * KVH * HD,
        ),
        name="private_part",
    )(place, parents, lengths, queries, dkeys, dvals, pkeys, pvals)


def prefix_kernel(
    place_ref,
    told_ref,
    k_ref,
    v_ref,
    twin_k_ref,
    twin_v_ref,
    w_ref,
    out_ref,
    wide_ref,
    told32,
    qs,
    peak,
    denom,
    acc,
    sem,
):
    step = pl.program_id(0)
    chips, draft, _ = told_ref.shape
    owned = chips * draft
    rows = owned * GROUP
    span = k_ref.shape[1]
    fetch = pltpu.make_async_copy(w_ref, wide_ref, sem)

    @pl.when(step == 2)
    def _():
        fetch.start()

    @pl.when(step == 0)
    def _():
        for j in range(chips):
            told32[j * draft : (j + 1) * draft, :] = told_ref[j, :, :WIDE].astype(F32)
        for h in range(GROUP):
            qs[h * owned : (h + 1) * owned, :] = told32[:, h * HD : (h + 1) * HD].astype(BF16)
        head = lax.dot_general(k_ref[0, :HD, :], qs[...], NT, preferred_element_type=F32)
        peak[...] = jnp.max(head, axis=0, keepdims=True) * (SCALE * LOG2E)
        denom[...] = jnp.zeros(denom.shape, F32)
        acc[...] = jnp.zeros(acc.shape, F32)

    keys = (k_ref[0], twin_k_ref[0])
    values = (v_ref[0], twin_v_ref[0])
    scores = [lax.dot_general(key, qs[...], NT, preferred_element_type=F32) for key in keys]
    weights = [jnp.exp2(score * (SCALE * LOG2E) - peak[...]) for score in scores]
    sums = [jnp.sum(weight.reshape(span // 8, 8, rows), axis=0) for weight in weights]
    mixes = [
        lax.dot_general(value, weight.astype(BF16), TN, preferred_element_type=F32)
        for value, weight in zip(values, weights)
    ]
    sums = [denom[i] + sums[i] for i in range(2)]
    mixes = [acc[i] + mixes[i] for i in range(2)]
    fits = jnp.max(jnp.maximum(sums[0], sums[1])) < LIMIT

    @pl.when(fits)
    def _():
        for i in range(2):
            denom[i] = sums[i]
            acc[i] = mixes[i]

    @pl.when(jnp.logical_not(fits))
    def _():
        part = 4 * HD

        def careful(i, keys, values):
            scores = lax.dot_general(keys, qs[...], NT, preferred_element_type=F32)
            scores = scores * (SCALE * LOG2E)
            old = peak[...]
            new = jnp.maximum(old, jnp.max(scores, axis=0, keepdims=True))
            fade = jnp.exp2(old - new)
            weights = jnp.exp2(scores - new)
            peak[...] = new
            sums = jnp.sum(weights.reshape(part // 8, 8, rows), axis=0)
            mixes = lax.dot_general(values, weights.astype(BF16), TN, preferred_element_type=F32)
            denom[i] = denom[i] * fade + sums
            acc[i] = acc[i] * fade + mixes
            denom[1 - i] = denom[1 - i] * fade
            acc[1 - i] = acc[1 - i] * fade

        @pl.loop(0, span // part)
        def _(b):
            block = pl.ds(pl.multiple_of(b * part, part), part)
            careful(0, k_ref[0, block, :], v_ref[0, block, :])
            careful(1, twin_k_ref[0, block, :], twin_v_ref[0, block, :])

    @pl.when(step == pl.num_programs(0) - 1)
    def _():
        total = jnp.sum(denom[0] + denom[1], axis=0, keepdims=True)
        lse = peak[...] * (1.0 / LOG2E) + jnp.log(total)
        out_ref[:, :HD] = ((acc[0] + acc[1]) / total).T
        out_ref[:, HD:] = jnp.broadcast_to(lse, (LANES, rows)).T
        fetch.wait()


def prefix_part(place, told, keys, values, twin_keys, twin_values, weight, span):
    chips, draft, _ = told.shape
    owned = chips * draft
    rows = owned * GROUP
    return pl.pallas_call(
        prefix_kernel,
        grid=(keys.shape[1] // span,),
        in_specs=[
            SMEM_SPEC,
            pl.BlockSpec(told.shape, lambda i: (0, 0, 0)),
            pl.BlockSpec((1, span, HD), lambda i: (0, i, 0)),
            pl.BlockSpec((1, span, HD), lambda i: (0, i, 0)),
            pl.BlockSpec((1, span, HD), lambda i: (0, i, 0)),
            pl.BlockSpec((1, span, HD), lambda i: (0, i, 0)),
            pl.BlockSpec(memory_space=pl.ANY),
        ],
        out_specs=[pl.BlockSpec((rows, HD + LANES), lambda i: (0, 0)), VMEM_SPEC],
        out_shape=[
            jax.ShapeDtypeStruct((rows, HD + LANES), F32),
            pltpu.VMEM(weight.shape, BF16),
        ],
        scratch_shapes=[
            pltpu.VMEM((owned, WIDE), F32),
            pltpu.VMEM((rows, HD), BF16),
            pltpu.VMEM((1, rows), F32),
            pltpu.VMEM((2, 8, rows), F32),
            pltpu.VMEM((2, HD, rows), F32),
            pltpu.SemaphoreType.DMA,
        ],
        compiler_params=pltpu.CompilerParams(vmem_limit_bytes=40 << 20),
        cost_estimate=pl.CostEstimate(
            flops=8 * rows * keys.shape[1] * HD,
            transcendentals=2 * rows * keys.shape[1],
            bytes_accessed=4 * keys.shape[1] * HD,
        ),
        name="prefix_part",
    )(
        place,
        on_chip(told),
        in_hbm(keys),
        in_hbm(values),
        in_hbm(twin_keys),
        in_hbm(twin_values),
        in_hbm(weight),
    )


def join(first, second):
    out_a, lse_a = first[:, :HD], first[:, HD:]
    out_b, lse_b = second[:, :HD], second[:, HD:]
    top = jnp.maximum(lse_a, lse_b)
    scale_a = jnp.exp(lse_a - top)
    scale_b = jnp.exp(lse_b - top)
    both = scale_a + scale_b
    return jnp.concatenate(
        [(scale_a * out_a + scale_b * out_b) / both, top + jnp.log(both)], axis=1
    )


def merge_kernel(place_ref, mine_ref, told_ref, att_ref, told32):
    chips, draft, _ = told_ref.shape
    owned = chips * draft
    wide = att_ref.shape[1]
    heads = wide // HD
    first_head = place_ref[2] * heads
    col = pl.multiple_of(first_head * HD, wide)
    for j in range(chips):
        part = slice(j * draft, (j + 1) * draft)
        told32[part, :wide] = told_ref[j, :, pl.ds(WIDE + col, wide)].astype(F32) + told_ref[
            j, :, pl.ds(2 * WIDE + col, wide)
        ].astype(F32)
        told32[part, wide:] = told_ref[j, :, 3 * WIDE :].astype(F32)
    stats = told32[:, wide:]
    lane = lax.broadcasted_iota(jnp.int32, (owned, LANES), 1)
    for h in range(heads):
        at = 3 * (first_head + h)
        mark = (lane >= at) & (lane < at + 3)
        lse_p = jnp.sum(jnp.where(mark, stats, 0.0), axis=1, keepdims=True)
        part = slice(h * owned, (h + 1) * owned)
        lse_a = mine_ref[part, HD:]
        top = jnp.maximum(lse_a, lse_p)
        scale_a = jnp.exp(lse_a - top)
        scale_p = jnp.exp(lse_p - top)
        mixed = scale_a * mine_ref[part, :HD] + scale_p * told32[:, h * HD : (h + 1) * HD]
        att_ref[:, h * HD : (h + 1) * HD] = (mixed / (scale_a + scale_p)).astype(BF16)


def merge_part(place, mine, told):
    chips, draft, _ = told.shape
    owned = chips * draft
    wide = mine.shape[0] // owned * HD
    return pl.pallas_call(
        merge_kernel,
        in_specs=[SMEM_SPEC, VMEM_SPEC, VMEM_SPEC],
        out_specs=VMEM_SPEC,
        out_shape=pltpu.VMEM((owned, wide), BF16),
        scratch_shapes=[pltpu.VMEM((owned, wide + LANES), F32)],
        compiler_params=pltpu.CompilerParams(vmem_limit_bytes=8 << 20),
        cost_estimate=pl.CostEstimate(
            flops=8 * mine.size, transcendentals=mine.size, bytes_accessed=0
        ),
        name="merge_part",
    )(place, on_chip(mine), on_chip(told))


def project_kernel(place_ref, *refs, masks, first):
    part_ref, refs = (None, refs) if first else (refs[0], refs[1:])
    wide_ref, out_ref = refs[2 * len(masks) :]
    chip = place_ref[0]
    total = functools.reduce(
        jnp.add,
        [
            jnp.dot(
                jnp.concatenate([refs[2 * i][...], refs[2 * i + 1][...]], axis=0),
                wide_ref[chip ^ mask],
                preferred_element_type=F32,
            )
            for i, mask in enumerate(masks)
        ],
    )
    if first:
        out_ref[...] = total
        return
    total = total + part_ref[...]
    owners, draft, _ = out_ref.shape
    half = owners // 2 * draft
    own, twin = total[:half], total[half:]
    even = place_ref[1] == 0
    halves = (jnp.where(even, own, twin), jnp.where(even, twin, own))
    for s in range(owners):
        at = s // 2 * draft
        out_ref[s] = halves[s % 2][at : at + draft].astype(BF16)


def project(place, part, chunks, wide, owners):
    masks = tuple(chunks)
    rows, deep = chunks[masks[0]][0].shape
    cols = wide.shape[2]
    first = part is None
    arrays = [] if first else [part]
    for mask in masks:
        arrays.extend(chunks[mask])
    arrays.append(wide)
    shape = (2 * rows, cols) if first else (owners, 2 * rows // owners, cols)
    return pl.pallas_call(
        functools.partial(project_kernel, masks=masks, first=first),
        in_specs=[SMEM_SPEC] + [VMEM_SPEC] * len(arrays),
        out_specs=VMEM_SPEC,
        out_shape=pltpu.VMEM(shape, F32 if first else BF16),
        compiler_params=pltpu.CompilerParams(vmem_limit_bytes=8 << 20),
        cost_estimate=pl.CostEstimate(
            flops=4 * rows * deep * len(masks) * cols, transcendentals=0, bytes_accessed=0
        ),
        name="project_first" if first else "project_last",
    )(place, *[on_chip(array) for array in arrays])


def shards(
    queries,
    draft_keys,
    draft_values,
    parents,
    private_keys,
    private_values,
    priv_lengths,
    prefix_keys,
    prefix_values,
    out_weight,
):
    own_rows = queries.shape[0]
    seq = lax.axis_size("seq")
    chips = seq // 2
    blocks = seq // KVH
    device = lax.axis_index("seq")
    chip = device // 2
    sharers = blocks // 2
    rank = chip % sharers
    place = jnp.stack([chip, device % 2, rank]).astype(jnp.int32)
    members = [list(range(c, seq, 2)) for c in range(2)]

    def from_partner(array, mask):
        return lax.ppermute(array, "seq", [(i, i ^ mask) for i in range(seq)])

    twin_keys = from_partner(prefix_keys, 1)
    twin_values = from_partner(prefix_values, 1)
    message = private_part(
        place,
        in_hbm(parents),
        priv_lengths,
        in_hbm(queries),
        in_hbm(draft_keys),
        in_hbm(draft_values),
        in_hbm(private_keys),
        in_hbm(private_values),
        sharers,
        KVH // 2,
    )
    told = lax.all_to_all(
        message, "seq", split_axis=0, concat_axis=0, axis_index_groups=members, tiled=True
    )

    span = min(4096, prefix_keys.shape[1])
    weight = out_weight.reshape(chips, -1, out_weight.shape[1])
    mine, wide = prefix_part(
        place, told, prefix_keys, prefix_values, twin_keys, twin_values, weight, span
    )
    for level in range(sharers.bit_length() - 2, -1, -1):
        half = mine.shape[0] // 2
        at = (rank >> level) & 1
        kept = lax.dynamic_slice_in_dim(mine, at * half, half, 0)
        gone = lax.dynamic_slice_in_dim(mine, (1 - at) * half, half, 0)
        mine = join(kept, from_partner(gone, 2 << level))

    own = {0: merge_part(place, mine, told)}
    twin = {}
    far = [2 * k for k in range(1, chips // 2)]
    for mask in [1] + far:
        own[mask] = from_partner(own[0], 2 * mask)
    for mask in far:
        own[mask + 1] = from_partner(own[mask], 2)
    for mask in own:
        twin[mask] = from_partner(own[mask], 1)
    both = {mask: (own[mask], twin[mask]) for mask in own}
    last = far[-1] + 1
    early = {mask: both[mask] for mask in both if mask != last}
    part = project(place, None, early, wide, seq)
    pieces = project(place, part, {last: both[last]}, wide, seq)
    done = lax.all_to_all(pieces, "seq", split_axis=0, concat_axis=0, tiled=True)
    return done.transpose(1, 0, 2).reshape(own_rows, -1).astype(F32)


def solution(mesh):
    in_specs = (
        P(("groups", "seq"), None),
        P(("groups", "seq"), None),
        P(("groups", "seq"), None),
        P(("groups", "seq")),
        P(("groups", "seq"), None, None),
        P(("groups", "seq"), None, None),
        P(("groups", "seq")),
        P(("groups", "seq"), None, None),
        P(("groups", "seq"), None, None),
        P(None, "seq"),
    )
    out_specs = P(("groups", "seq"), None)

    return jax.shard_map(shards, mesh=mesh, in_specs=in_specs, out_specs=out_specs, check_vma=False)
```

time: 71.3 us -> 72.5 us (1.017)
  starting transfers between devices: 15.5 us -> 20.1 us
  waiting for transfers between devices: 10.7 us -> 8.38 us
  blocking collectives: 25.7 us -> 24.3 us
    ppermute x17, starting transfers between devices: 15.5 us -> 20.1 us  [from_partner(): return lax.ppermute(array, 'seq', [(i, i ^ mask) for i in range(seq)])]
    ppermute x17, waiting for transfers between devices: 10.7 us -> 8.38 us  [from_partner(): return lax.ppermute(array, 'seq', [(i, i ^ mask) for i in range(seq)])]
    all_to_all x1, blocking collectives: 11.8 us -> 10.5 us  [shards(): lax.all_to_all(pieces, 'seq', split_axis=0, concat_axis=0, tiled=True)]
    pallas_call x1, Pallas kernels: 10.1 us -> 11.2 us  [prefix_part(): pl.pallas_call(prefix_kernel, grid=(keys.shape[1] // span,), in_specs=[SM...]
  transfers between devices with their start and end apart: 17 -> 17, of which waited for: 8 -> 6; matrix products, arithmetic and copies ran while one was open for 0% -> 0% of each run, Pallas kernels for 3% -> 7%
where the time goes in v7:
time: 72.5 us; the launch traced here: 72.3 us
  blocking collectives  24.3 us (34%)
  starting transfers between devices  20.1 us (28%)
  Pallas kernels  18 us (25%)
  waiting for transfers between devices  8.38 us (12%)
  other arithmetic  0.74 us (1%)
  between operations  0.73 us (1%)
    ppermute x17, starting transfers between devices, from_partner(): return lax.ppermute(array, 'seq', [(i, i ^ mask) for i in range(seq)])  20.1 us
    all_to_all x1, blocking collectives, shards(): lax.all_to_all(message, 'seq', split_axis=0, concat_axis=0, axis_index_gr...  13.9 us
    pallas_call x1, Pallas kernels, prefix_part(): pl.pallas_call(prefix_kernel, grid=(keys.shape[1] // span,), in_specs=[SM...  11.2 us
    all_to_all x1, blocking collectives, shards(): lax.all_to_all(pieces, 'seq', split_axis=0, concat_axis=0, tiled=True)  10.5 us
    ppermute x17, waiting for transfers between devices, from_partner(): return lax.ppermute(array, 'seq', [(i, i ^ mask) for i in range(seq)])  8.38 us
    pallas_call x1, Pallas kernels, private_part(): pl.pallas_call(functools.partial(private_kernel, draft=draft, copies=copi...  3.4 us
    pallas_call x2, Pallas kernels, project(): pl.pallas_call(functools.partial(project_kernel, masks=masks, first=first...  2.75 us
  transfers between devices with their start and end apart: 17, of which 6 were waited for; matrix products, arithmetic and copies ran while one was open for 0% of the time, Pallas kernels for 7%

profile of v7, /device:TPU:2, one launch (start us, length us, event | category | flops | bytes accessed | tf_op | source)
XLA Modules:
  0.0 72.3 jit_solution(9499558150443682013)
XLA Ops:
  0.0 0.0 collective-permute-start
  0.0 0.5 collective-permute-start.1
  1.2 0.1 pad_add_fusion.place_ref
  1.2 3.4 %private_part.1 = bf16[8,4,3200]{2,1,0:T(4,128)(2,1)S(1)} custom-call(s32[3]{0:T(128)S(1)} %pad_add_fusion.place_ref, s32[4]{0:T(128)} %par_ref.1, s32[1]{0:T(128)S(6)} %copy.11.len_ref, bf16[4,8192]{1,0:T(4,128)(2,1)} %q_ref.1, bf16[4,1024]{1,0:T(4,128)(2,1)} %dk_ref.1, bf16[4,1024]{1,0:T(4,128)(2,1)} %dv_ref.1, bf16[1,1024,1024]{2,1,0:T(8,128)(2,1)} %k_ref.2, ...), custom_call_target="tpu_custom_call" | custom-call | flops 134217728 | bytes 4194304 | tf_op jit(solution)/shard_map/private_part/pallas_call | solution.py:112
  4.7 13.9 %all_to_all.10.told_ref = bf16[8,4,3200]{2,1,0:T(4,128)(2,1)S(1)} all-to-all(bf16[8,4,3200]{2,1,0:T(4,128)(2,1)S(1)} %private_part.1), channel_id=1, replica_groups={{0,2,4,6,8,10,12,14},{1,3,5,7,9,11,13,15},{16,18,20,22,24,26,28,30},{17..., dimensions={0} | all-to-all | bytes 409600 | tf_op jit(solution)/shard_map/all_to_all | solution.py:426
  18.5 0.0 collective-permute-done.twin_k_ref
  18.5 0.0 collective-permute-done.1.twin_v_ref
  18.5 11.2 %prefix_part.1 = (f32[256,256]{1,0:T(8,128)S(1)}, bf16[8,1024,512]{2,1,0:T(8,128)(2,1)S(1)}) custom-call(s32[3]{0:T(128)S(1)} %pad_add_fusion.place_ref, bf16[8,4,3200]{2,1,0:T(4,128)(2,1)S(1)} %all_to_all.10.told_ref, bf16[1,16384,128]{2,1,0:T(8,128)(2,1)} %k_ref.3, bf16[1,16384,128]{2,1,0:T(8,128)(2,1)} %v_ref.3, ...), custom_call_target="tpu_custom_call" | custom-call | flops 4294967296 | bytes 8388608 | tf_op jit(solution)/shard_map/prefix_part/pallas_call | solution.py:233
  29.7 0.7 merge_part.1.refs_0_
  30.4 15.6 %collective-permute-start.9 = (bf16[32,1024]{1,0:T(8,128)(2,1)S(1)}, bf16[32,1024]{1,0:T(8,128)(2,1)S(1)}, u32[]{:S(2)}, u32[]{:S(2)}) collective-permute-start(bf16[32,1024]{1,0:T(8,128)(2,1)S(1)} %merge_part.1.refs_0_), channel_id=1, source_target_pairs={{0,12},{1,13},{2,14},{3,15},{4,8},{5,9},{6,10},{7,11},{8,4},{9,5},... | collective-permute-start | bytes 196616 | tf_op jit(solution)/shard_map/ppermute | solution.py:410
  46.0 0.0 collective-permute-start.7
  46.0 0.6 collective-permute-start.5
  46.7 0.0 collective-permute-start.3
  46.7 0.0 collective-permute-start.2
  46.7 1.6 %collective-permute-done.9.refs_8_ = bf16[32,1024]{1,0:T(8,128)(2,1)S(1)} collective-permute-done((bf16[32,1024]{1,0:T(8,128)(2,1)S(1)}, bf16[32,1024]{1,0:T(8,128)(2,1)S(1)}, u32[]{:S(2)}, u32[]{:S(2)}) %collective-permute-start.9) | collective-permute-done | bytes 65568 | tf_op jit(solution)/shard_map/ppermute | solution.py:410
  48.3 0.4 collective-permute-start.15
  48.7 2.5 %collective-permute-done.7.refs_6_ = bf16[32,1024]{1,0:T(8,128)(2,1)S(1)} collective-permute-done((bf16[32,1024]{1,0:T(8,128)(2,1)S(1)}, bf16[32,1024]{1,0:T(8,128)(2,1)S(1)}, u32[]{:S(2)}, u32[]{:S(2)}) %collective-permute-start.7) | collective-permute-done | bytes 65568 | tf_op jit(solution)/shard_map/ppermute | solution.py:410
  51.2 0.0 collective-permute-start.10
  51.2 0.0 collective-permute-done.5.refs_4_
  51.2 0.0 collective-permute-start.13
  51.2 0.3 collective-permute-done.3.refs_2_
  51.5 1.8 %collective-permute-start.11 = (bf16[32,1024]{1,0:T(8,128)(2,1)S(1)}, bf16[32,1024]{1,0:T(8,128)(2,1)S(1)}, u32[]{:S(2)}, u32[]{:S(2)}) collective-permute-start(bf16[32,1024]{1,0:T(8,128)(2,1)S(1)} %collective-permute-done.5.refs_4_), channel_id=1, source_target_pairs={{0,2},{1,3},{2,0},{3,1},{4,6},{5,7},{6,4},{7,5},{8,10},{9,11},{10,... | collective-permute-start | bytes 196616 | tf_op jit(solution)/shard_map/ppermute | solution.py:410
  53.2 0.0 collective-permute-done.2.refs_1_
  53.2 0.0 collective-permute-start.8
  53.2 0.0 collective-permute-done.15.refs_1_
  53.2 0.5 collective-permute-start.6
  53.7 0.0 collective-permute-done.10.refs_9_
  53.8 0.1 collective-permute-start.4
  53.8 2.3 %collective-permute-done.13.refs_12_ = bf16[32,1024]{1,0:T(8,128)(2,1)S(1)} collective-permute-done((bf16[32,1024]{1,0:T(8,128)(2,1)S(1)}, bf16[32,1024]{1,0:T(8,128)(2,1)S(1)}, u32[]{:S(2)}, u32[]{:S(2)}) %collective-permute-start.13) | collective-permute-done | bytes 65568 | tf_op jit(solution)/shard_map/ppermute | solution.py:410
  56.2 0.0 collective-permute-start.14
  56.2 0.9 %collective-permute-done.11.refs_10_ = bf16[32,1024]{1,0:T(8,128)(2,1)S(1)} collective-permute-done((bf16[32,1024]{1,0:T(8,128)(2,1)S(1)}, bf16[32,1024]{1,0:T(8,128)(2,1)S(1)}, u32[]{:S(2)}, u32[]{:S(2)}) %collective-permute-start.11) | collective-permute-done | bytes 65568 | tf_op jit(solution)/shard_map/ppermute | solution.py:410
  57.1 0.0 collective-permute-start.12
  57.1 0.0 collective-permute-done.8.refs_7_
  57.1 0.5 collective-permute-start.16
  57.6 0.0 collective-permute-done.6.refs_5_
  57.6 0.0 collective-permute-done.4.refs_3_
  57.6 0.0 collective-permute-done.14.refs_13_
  57.6 0.7 %collective-permute-done.12.refs_11_ = bf16[32,1024]{1,0:T(8,128)(2,1)S(1)} collective-permute-done((bf16[32,1024]{1,0:T(8,128)(2,1)S(1)}, bf16[32,1024]{1,0:T(8,128)(2,1)S(1)}, u32[]{:S(2)}, u32[]{:S(2)}) %collective-permute-start.12) | collective-permute-done | bytes 65568 | tf_op jit(solution)/shard_map/ppermute | solution.py:410
  58.4 1.9 %project_first.1.refs_0_ = f32[64,512]{1,0:T(8,128)S(1)} custom-call(s32[3]{0:T(128)S(1)} %pad_add_fusion.place_ref, bf16[32,1024]{1,0:T(8,128)(2,1)S(1)} %merge_part.1.refs_0_, bf16[32,1024]{1,0:T(8,128)(2,1)S(1)} %collective-permute-done.2.refs_1_, bf16[32,1024]{1,0:T(8,128)(2,1)S(1)} %collective-permute-done.3.refs_2_, ...), custom_call_target="tpu_custom_call" | custom-call | flops 469762048 | tf_op jit(solution)/shard_map/project_first/pallas_call | solution.py:373
  60.3 0.0 collective-permute-done.16.refs_2_
  60.3 0.8 %project_last.1 = bf16[16,4,512]{2,1,0:T(4,128)(2,1)S(1)} custom-call(s32[3]{0:T(128)S(1)} %pad_add_fusion.place_ref, f32[64,512]{1,0:T(8,128)S(1)} %project_first.1.refs_0_, bf16[32,1024]{1,0:T(8,128)(2,1)S(1)} %collective-permute-done.15.refs_1_, bf16[32,1024]{1,0:T(8,128)(2,1)S(1)} %collective-permute-done.16.refs_2_, ...), custom_call_target="tpu_custom_call" | custom-call | flops 67108864 | tf_op jit(solution)/shard_map/project_last/pallas_call | solution.py:373
  61.1 10.5 %all_to_all.11 = bf16[16,4,512]{2,1,0:T(4,128)(2,1)S(1)} all-to-all(bf16[16,4,512]{2,1,0:T(4,128)(2,1)S(1)} %project_last.1), channel_id=1, replica_groups=mesh['groups'=2,'seq'=16] {'seq'}, dimensions={0} | all-to-all | bytes 131072 | tf_op jit(solution)/shard_map/all_to_all | solution.py:456
  71.6 0.7 convert_element_type.13
Async XLA Ops:
  0.0 18.5 %collective-permute-start = (bf16[1,16384,128]{2,1,0:T(8,128)(2,1)}, bf16[1,16384,128]{2,1,0:T(8,128)(2,1)}, u32[]{:S(2)}, u32[]{:S(2)}) collective-permute-start(bf16[1,16384,128]{2,1,0:T(8,128)(2,1)} %k_ref.3), channel_id=1, source_target_pairs={{0,1},{1,0},{2,3},{3,2},{4,5},{5,4},{6,7},{7,6},{8,9},{9,8},{10,11... | collective-permute-start | bytes 12582920 | tf_op jit(solution)/shard_map/ppermute | solution.py:410
  0.0 18.5 %collective-permute-start.1 = (bf16[1,16384,128]{2,1,0:T(8,128)(2,1)}, bf16[1,16384,128]{2,1,0:T(8,128)(2,1)}, u32[]{:S(2)}, u32[]{:S(2)}) collective-permute-start(bf16[1,16384,128]{2,1,0:T(8,128)(2,1)} %v_ref.3), channel_id=1, source_target_pairs={{0,1},{1,0},{2,3},{3,2},{4,5},{5,4},{6,7},{7,6},{8,9},{9,8},{10,11... | collective-permute-start | bytes 12582920 | tf_op jit(solution)/shard_map/ppermute | solution.py:410
  30.4 17.9 %collective-permute-start.9 = (bf16[32,1024]{1,0:T(8,128)(2,1)S(1)}, bf16[32,1024]{1,0:T(8,128)(2,1)S(1)}, u32[]{:S(2)}, u32[]{:S(2)}) collective-permute-start(bf16[32,1024]{1,0:T(8,128)(2,1)S(1)} %merge_part.1.refs_0_), channel_id=1, source_target_pairs={{0,12},{1,13},{2,14},{3,15},{4,8},{5,9},{6,10},{7,11},{8,4},{9,5},... | collective-permute-start | bytes 196616 | tf_op jit(solution)/shard_map/ppermute | solution.py:410
  46.0 5.2 %collective-permute-start.7 = (bf16[32,1024]{1,0:T(8,128)(2,1)S(1)}, bf16[32,1024]{1,0:T(8,128)(2,1)S(1)}, u32[]{:S(2)}, u32[]{:S(2)}) collective-permute-start(bf16[32,1024]{1,0:T(8,128)(2,1)S(1)} %merge_part.1.refs_0_), channel_id=1, source_target_pairs={{0,8},{1,9},{2,10},{3,11},{4,12},{5,13},{6,14},{7,15},{8,0},{9,1},... | collective-permute-start | bytes 196616 | tf_op jit(solution)/shard_map/ppermute | solution.py:410
  46.0 5.2 %collective-permute-start.5 = (bf16[32,1024]{1,0:T(8,128)(2,1)S(1)}, bf16[32,1024]{1,0:T(8,128)(2,1)S(1)}, u32[]{:S(2)}, u32[]{:S(2)}) collective-permute-start(bf16[32,1024]{1,0:T(8,128)(2,1)S(1)} %merge_part.1.refs_0_), channel_id=1, source_target_pairs={{0,4},{1,5},{2,6},{3,7},{4,0},{5,1},{6,2},{7,3},{8,12},{9,13},{10,... | collective-permute-start | bytes 196616 | tf_op jit(solution)/shard_map/ppermute | solution.py:410
  46.7 4.8 %collective-permute-start.3 = (bf16[32,1024]{1,0:T(8,128)(2,1)S(1)}, bf16[32,1024]{1,0:T(8,128)(2,1)S(1)}, u32[]{:S(2)}, u32[]{:S(2)}) collective-permute-start(bf16[32,1024]{1,0:T(8,128)(2,1)S(1)} %merge_part.1.refs_0_), channel_id=1, source_target_pairs={{0,2},{1,3},{2,0},{3,1},{4,6},{5,7},{6,4},{7,5},{8,10},{9,11},{10,... | collective-permute-start | bytes 196616 | tf_op jit(solution)/shard_map/ppermute | solution.py:410
  46.7 6.6 %collective-permute-start.2 = (bf16[32,1024]{1,0:T(8,128)(2,1)S(1)}, bf16[32,1024]{1,0:T(8,128)(2,1)S(1)}, u32[]{:S(2)}, u32[]{:S(2)}) collective-permute-start(bf16[32,1024]{1,0:T(8,128)(2,1)S(1)} %merge_part.1.refs_0_), channel_id=1, source_target_pairs={{0,1},{1,0},{2,3},{3,2},{4,5},{5,4},{6,7},{7,6},{8,9},{9,8},{10,11... | collective-permute-start | bytes 196616 | tf_op jit(solution)/shard_map/ppermute | solution.py:410
  48.3 5.0 %collective-permute-start.15 = (bf16[32,1024]{1,0:T(8,128)(2,1)S(1)}, bf16[32,1024]{1,0:T(8,128)(2,1)S(1)}, u32[]{:S(2)}, u32[]{:S(2)}) collective-permute-start(bf16[32,1024]{1,0:T(8,128)(2,1)S(1)} %collective-permute-done.9.refs_8_), channel_id=1, source_target_pairs={{0,2},{1,3},{2,0},{3,1},{4,6},{5,7},{6,4},{7,5},{8,10},{9,11},{10,... | collective-permute-start | bytes 196616 | tf_op jit(solution)/shard_map/ppermute | solution.py:410
  51.2 2.6 %collective-permute-start.10 = (bf16[32,1024]{1,0:T(8,128)(2,1)S(1)}, bf16[32,1024]{1,0:T(8,128)(2,1)S(1)}, u32[]{:S(2)}, u32[]{:S(2)}) collective-permute-start(bf16[32,1024]{1,0:T(8,128)(2,1)S(1)} %collective-permute-done.9.refs_8_), channel_id=1, source_target_pairs={{0,1},{1,0},{2,3},{3,2},{4,5},{5,4},{6,7},{7,6},{8,9},{9,8},{10,11... | collective-permute-start | bytes 196616 | tf_op jit(solution)/shard_map/ppermute | solution.py:410
  51.2 5.0 %collective-permute-start.13 = (bf16[32,1024]{1,0:T(8,128)(2,1)S(1)}, bf16[32,1024]{1,0:T(8,128)(2,1)S(1)}, u32[]{:S(2)}, u32[]{:S(2)}) collective-permute-start(bf16[32,1024]{1,0:T(8,128)(2,1)S(1)} %collective-permute-done.7.refs_6_), channel_id=1, source_target_pairs={{0,2},{1,3},{2,0},{3,1},{4,6},{5,7},{6,4},{7,5},{8,10},{9,11},{10,... | collective-permute-start | bytes 196616 | tf_op jit(solution)/shard_map/ppermute | solution.py:410
  51.5 5.6 %collective-permute-start.11 = (bf16[32,1024]{1,0:T(8,128)(2,1)S(1)}, bf16[32,1024]{1,0:T(8,128)(2,1)S(1)}, u32[]{:S(2)}, u32[]{:S(2)}) collective-permute-start(bf16[32,1024]{1,0:T(8,128)(2,1)S(1)} %collective-permute-done.5.refs_4_), channel_id=1, source_target_pairs={{0,2},{1,3},{2,0},{3,1},{4,6},{5,7},{6,4},{7,5},{8,10},{9,11},{10,... | collective-permute-start | bytes 196616 | tf_op jit(solution)/shard_map/ppermute | solution.py:410
  53.2 3.9 %collective-permute-start.8 = (bf16[32,1024]{1,0:T(8,128)(2,1)S(1)}, bf16[32,1024]{1,0:T(8,128)(2,1)S(1)}, u32[]{:S(2)}, u32[]{:S(2)}) collective-permute-start(bf16[32,1024]{1,0:T(8,128)(2,1)S(1)} %collective-permute-done.7.refs_6_), channel_id=1, source_target_pairs={{0,1},{1,0},{2,3},{3,2},{4,5},{5,4},{6,7},{7,6},{8,9},{9,8},{10,11... | collective-permute-start | bytes 196616 | tf_op jit(solution)/shard_map/ppermute | solution.py:410
  53.2 4.4 %collective-permute-start.6 = (bf16[32,1024]{1,0:T(8,128)(2,1)S(1)}, bf16[32,1024]{1,0:T(8,128)(2,1)S(1)}, u32[]{:S(2)}, u32[]{:S(2)}) collective-permute-start(bf16[32,1024]{1,0:T(8,128)(2,1)S(1)} %collective-permute-done.5.refs_4_), channel_id=1, source_target_pairs={{0,1},{1,0},{2,3},{3,2},{4,5},{5,4},{6,7},{7,6},{8,9},{9,8},{10,11... | collective-permute-start | bytes 196616 | tf_op jit(solution)/shard_map/ppermute | solution.py:410
  53.8 3.9 %collective-permute-start.4 = (bf16[32,1024]{1,0:T(8,128)(2,1)S(1)}, bf16[32,1024]{1,0:T(8,128)(2,1)S(1)}, u32[]{:S(2)}, u32[]{:S(2)}) collective-permute-start(bf16[32,1024]{1,0:T(8,128)(2,1)S(1)} %collective-permute-done.3.refs_2_), channel_id=1, source_target_pairs={{0,1},{1,0},{2,3},{3,2},{4,5},{5,4},{6,7},{7,6},{8,9},{9,8},{10,11... | collective-permute-start | bytes 196616 | tf_op jit(solution)/shard_map/ppermute | solution.py:410
  56.2 1.5 %collective-permute-start.14 = (bf16[32,1024]{1,0:T(8,128)(2,1)S(1)}, bf16[32,1024]{1,0:T(8,128)(2,1)S(1)}, u32[]{:S(2)}, u32[]{:S(2)}) collective-permute-start(bf16[32,1024]{1,0:T(8,128)(2,1)S(1)} %collective-permute-done.13.refs_12_), channel_id=1, source_target_pairs={{0,1},{1,0},{2,3},{3,2},{4,5},{5,4},{6,7},{7,6},{8,9},{9,8},{10,11... | collective-permute-start | bytes 196616 | tf_op jit(solution)/shard_map/ppermute | solution.py:410
  57.1 1.3 %collective-permute-start.12 = (bf16[32,1024]{1,0:T(8,128)(2,1)S(1)}, bf16[32,1024]{1,0:T(8,128)(2,1)S(1)}, u32[]{:S(2)}, u32[]{:S(2)}) collective-permute-start(bf16[32,1024]{1,0:T(8,128)(2,1)S(1)} %collective-permute-done.11.refs_10_), channel_id=1, source_target_pairs={{0,1},{1,0},{2,3},{3,2},{4,5},{5,4},{6,7},{7,6},{8,9},{9,8},{10,11... | collective-permute-start | bytes 196616 | tf_op jit(solution)/shard_map/ppermute | solution.py:410
  57.1 3.2 %collective-permute-start.16 = (bf16[32,1024]{1,0:T(8,128)(2,1)S(1)}, bf16[32,1024]{1,0:T(8,128)(2,1)S(1)}, u32[]{:S(2)}, u32[]{:S(2)}) collective-permute-start(bf16[32,1024]{1,0:T(8,128)(2,1)S(1)} %collective-permute-done.15.refs_1_), channel_id=1, source_target_pairs={{0,1},{1,0},{2,3},{3,2},{4,5},{5,4},{6,7},{7,6},{8,9},{9,8},{10,11... | collective-permute-start | bytes 196616 | tf_op jit(solution)/shard_map/ppermute | solution.py:410

commit v8 on v7

--- a/solution.py
+++ b/solution.py
@@ -331,7 +331,7 @@
     )(place, on_chip(mine), on_chip(told))
 
 
-def project_kernel(place_ref, *refs, masks, first):
+def project_kernel(place_ref, *refs, masks, first, last):
     part_ref, refs = (None, refs) if first else (refs[0], refs[1:])
     wide_ref, out_ref = refs[2 * len(masks) :]
     chip = place_ref[0]
@@ -346,10 +346,11 @@
             for i, mask in enumerate(masks)
         ],
     )
-    if first:
+    if not first:
+        total = total + part_ref[...]
+    if not last:
         out_ref[...] = total
         return
-    total = total + part_ref[...]
     owners, draft, _ = out_ref.shape
     half = owners // 2 * draft
     own, twin = total[:half], total[half:]
@@ -360,7 +361,7 @@
         out_ref[s] = halves[s % 2][at : at + draft].astype(BF16)
 
 
-def project(place, part, chunks, wide, owners):
+def project(place, part, chunks, wide, owners, last):
     masks = tuple(chunks)
     rows, deep = chunks[masks[0]][0].shape
     cols = wide.shape[2]
@@ -369,17 +370,17 @@
     for mask in masks:
         arrays.extend(chunks[mask])
     arrays.append(wide)
-    shape = (2 * rows, cols) if first else (owners, 2 * rows // owners, cols)
+    shape = (owners, 2 * rows // owners, cols) if last else (2 * rows, cols)
     return pl.pallas_call(
-        functools.partial(project_kernel, masks=masks, first=first),
+        functools.partial(project_kernel, masks=masks, first=first, last=last),
         in_specs=[SMEM_SPEC] + [VMEM_SPEC] * len(arrays),
         out_specs=VMEM_SPEC,
-        out_shape=pltpu.VMEM(shape, F32 if first else BF16),
+        out_shape=pltpu.VMEM(shape, BF16 if last else F32),
         compiler_params=pltpu.CompilerParams(vmem_limit_bytes=8 << 20),
         cost_estimate=pl.CostEstimate(
             flops=4 * rows * deep * len(masks) * cols, transcendentals=0, bytes_accessed=0
         ),
-        name="project_first" if first else "project_last",
+        name="project_last" if last else "project",
     )(place, *[on_chip(array) for array in arrays])
 
 
@@ -442,17 +443,22 @@
     own = {0: merge_part(place, mine, told)}
     twin = {}
     far = [2 * k for k in range(1, chips // 2)]
+
+    def move(target, mask, source, step):
+        target[mask] = from_partner(source, step)
+
     for mask in [1] + far:
-        own[mask] = from_partner(own[0], 2 * mask)
+        move(own, mask, own[0], 2 * mask)
     for mask in far:
-        own[mask + 1] = from_partner(own[mask], 2)
+        move(own, mask + 1, own[mask], 2)
     for mask in own:
-        twin[mask] = from_partner(own[mask], 1)
-    both = {mask: (own[mask], twin[mask]) for mask in own}
-    last = far[-1] + 1
-    early = {mask: both[mask] for mask in both if mask != last}
-    part = project(place, None, early, wide, seq)
-    pieces = project(place, part, {last: both[last]}, wide, seq)
+        move(twin, mask, own[mask], 1)
+    stages = [[0] + far[:-1], [1, far[-1]] + [m + 1 for m in far[:-1]], [far[-1] + 1]]
+    part = None
+    for number, stage in enumerate(stages):
+        chunks = {mask: (own[mask], twin[mask]) for mask in stage}
+        part = project(place, part, chunks, wide, seq, number == len(stages) - 1)
+    pieces = part
     done = lax.all_to_all(pieces, "seq", split_axis=0, concat_axis=0, tiled=True)
     return done.transpose(1, 0, 2).reshape(own_rows, -1).astype(F32)
 

time: 72.5 us -> 72.2 us (level)
  waiting for transfers between devices: 8.38 us -> 6.48 us
    ppermute x17, waiting for transfers between devices: 8.38 us -> 6.48 us  [from_partner(): return lax.ppermute(array, 'seq', [(i, i ^ mask) for i in range(seq)])]
    ppermute x17, starting transfers between devices: 20.1 us -> 20.8 us  [from_partner(): return lax.ppermute(array, 'seq', [(i, i ^ mask) for i in range(seq)])]
    pallas_call x2 -> x3, Pallas kernels: 2.75 us -> 3.42 us  [project(): pl.pallas_call(functools.partial(project_kernel, masks=masks, first=first...]
  transfers between devices with their start and end apart: 17 -> 17, of which waited for: 6 -> 4; matrix products, arithmetic and copies ran while one was open for 0% -> 0% of each run, Pallas kernels for 7% -> 8%
where the time goes in v8:
time: 72.2 us; the launch traced here: 72 us
  blocking collectives  24.5 us (34%)
  starting transfers between devices  20.8 us (29%)
  Pallas kernels  18.7 us (26%)
  waiting for transfers between devices  6.48 us (9%)
  between operations  0.77 us (1%)
  other arithmetic  0.74 us (1%)
    ppermute x17, starting transfers between devices, from_partner(): return lax.ppermute(array, 'seq', [(i, i ^ mask) for i in range(seq)])  20.8 us
    all_to_all x1, blocking collectives, shards(): lax.all_to_all(message, 'seq', split_axis=0, concat_axis=0, axis_index_gr...  13.9 us
    pallas_call x1, Pallas kernels, prefix_part(): pl.pallas_call(prefix_kernel, grid=(keys.shape[1] // span,), in_specs=[SM...  11.2 us
    all_to_all x1, blocking collectives, shards(): lax.all_to_all(pieces, 'seq', split_axis=0, concat_axis=0, tiled=True)  10.6 us
    ppermute x17, waiting for transfers between devices, from_partner(): return lax.ppermute(array, 'seq', [(i, i ^ mask) for i in range(seq)])  6.48 us
    pallas_call x3, Pallas kernels, project(): pl.pallas_call(functools.partial(project_kernel, masks=masks, first=first...  3.42 us
    pallas_call x1, Pallas kernels, private_part(): pl.pallas_call(functools.partial(private_kernel, draft=draft, copies=copi...  3.4 us
  transfers between devices with their start and end apart: 17, of which 4 were waited for; matrix products, arithmetic and copies ran while one was open for 0% of the time, Pallas kernels for 8%

profile of v8, /device:TPU:2, one launch (start us, length us, event | category | flops | bytes accessed | tf_op | source)
XLA Modules:
  0.0 72.0 jit_solution(16589558115960157134)
XLA Ops:
  0.0 0.0 collective-permute-start
  0.0 0.5 collective-permute-start.1
  1.2 0.1 pad_add_fusion.place_ref
  1.2 3.4 %private_part.1 = bf16[8,4,3200]{2,1,0:T(4,128)(2,1)S(1)} custom-call(s32[3]{0:T(128)S(1)} %pad_add_fusion.place_ref, s32[4]{0:T(128)} %par_ref.1, s32[1]{0:T(128)S(6)} %copy.11.len_ref, bf16[4,8192]{1,0:T(4,128)(2,1)} %q_ref.1, bf16[4,1024]{1,0:T(4,128)(2,1)} %dk_ref.1, bf16[4,1024]{1,0:T(4,128)(2,1)} %dv_ref.1, bf16[1,1024,1024]{2,1,0:T(8,128)(2,1)} %k_ref.2, ...), custom_call_target="tpu_custom_call" | custom-call | flops 134217728 | bytes 4194304 | tf_op jit(solution)/shard_map/private_part/pallas_call | solution.py:112
  4.7 13.9 %all_to_all.10.told_ref = bf16[8,4,3200]{2,1,0:T(4,128)(2,1)S(1)} all-to-all(bf16[8,4,3200]{2,1,0:T(4,128)(2,1)S(1)} %private_part.1), channel_id=1, replica_groups={{0,2,4,6,8,10,12,14},{1,3,5,7,9,11,13,15},{16,18,20,22,24,26,28,30},{17..., dimensions={0} | all-to-all | bytes 409600 | tf_op jit(solution)/shard_map/all_to_all | solution.py:427
  18.5 0.0 collective-permute-done.twin_k_ref
  18.5 0.0 collective-permute-done.1.twin_v_ref
  18.5 11.2 %prefix_part.1 = (f32[256,256]{1,0:T(8,128)S(1)}, bf16[8,1024,512]{2,1,0:T(8,128)(2,1)S(1)}) custom-call(s32[3]{0:T(128)S(1)} %pad_add_fusion.place_ref, bf16[8,4,3200]{2,1,0:T(4,128)(2,1)S(1)} %all_to_all.10.told_ref, bf16[1,16384,128]{2,1,0:T(8,128)(2,1)} %k_ref.3, bf16[1,16384,128]{2,1,0:T(8,128)(2,1)} %v_ref.3, ...), custom_call_target="tpu_custom_call" | custom-call | flops 4294967296 | bytes 8388608 | tf_op jit(solution)/shard_map/prefix_part/pallas_call | solution.py:233
  29.7 0.7 merge_part.1.refs_0_
  30.4 15.6 %collective-permute-start.9 = (bf16[32,1024]{1,0:T(8,128)(2,1)S(1)}, bf16[32,1024]{1,0:T(8,128)(2,1)S(1)}, u32[]{:S(2)}, u32[]{:S(2)}) collective-permute-start(bf16[32,1024]{1,0:T(8,128)(2,1)S(1)} %merge_part.1.refs_0_), channel_id=1, source_target_pairs={{0,12},{1,13},{2,14},{3,15},{4,8},{5,9},{6,10},{7,11},{8,4},{9,5},... | collective-permute-start | bytes 196616 | tf_op jit(solution)/shard_map/ppermute | solution.py:411
  46.0 0.0 collective-permute-start.5
  46.0 0.0 collective-permute-start.7
  46.0 0.6 collective-permute-start.3
  46.7 0.0 collective-permute-start.2
  46.7 1.6 %collective-permute-done.9.refs_3_ = bf16[32,1024]{1,0:T(8,128)(2,1)S(1)} collective-permute-done((bf16[32,1024]{1,0:T(8,128)(2,1)S(1)}, bf16[32,1024]{1,0:T(8,128)(2,1)S(1)}, u32[]{:S(2)}, u32[]{:S(2)}) %collective-permute-start.9) | collective-permute-done | bytes 65568 | tf_op jit(solution)/shard_map/ppermute | solution.py:411
  48.3 0.4 collective-permute-start.15
  48.7 2.5 %collective-permute-done.5.refs_4_ = bf16[32,1024]{1,0:T(8,128)(2,1)S(1)} collective-permute-done((bf16[32,1024]{1,0:T(8,128)(2,1)S(1)}, bf16[32,1024]{1,0:T(8,128)(2,1)S(1)}, u32[]{:S(2)}, u32[]{:S(2)}) %collective-permute-start.5) | collective-permute-done | bytes 65568 | tf_op jit(solution)/shard_map/ppermute | solution.py:411
  51.2 0.0 collective-permute-start.13
  51.2 0.0 collective-permute-done.7.refs_1_
  51.2 0.0 collective-permute-start.6
  51.2 0.0 collective-permute-done.3.refs_2_
  51.2 2.1 %collective-permute-start.11 = (bf16[32,1024]{1,0:T(8,128)(2,1)S(1)}, bf16[32,1024]{1,0:T(8,128)(2,1)S(1)}, u32[]{:S(2)}, u32[]{:S(2)}) collective-permute-start(bf16[32,1024]{1,0:T(8,128)(2,1)S(1)} %collective-permute-done.3.refs_2_), channel_id=1, source_target_pairs={{0,2},{1,3},{2,0},{3,1},{4,6},{5,7},{6,4},{7,5},{8,10},{9,11},{10,... | collective-permute-start | bytes 196616 | tf_op jit(solution)/shard_map/ppermute | solution.py:411
  53.3 0.0 collective-permute-done.2.refs_1_
  53.3 0.2 collective-permute-start.4
  53.5 0.0 collective-permute-done.15.refs_1_
  53.5 0.3 collective-permute-start.10
  53.8 2.2 %collective-permute-done.13.refs_7_ = bf16[32,1024]{1,0:T(8,128)(2,1)S(1)} collective-permute-done((bf16[32,1024]{1,0:T(8,128)(2,1)S(1)}, bf16[32,1024]{1,0:T(8,128)(2,1)S(1)}, u32[]{:S(2)}, u32[]{:S(2)}) %collective-permute-start.13) | collective-permute-done | bytes 65568 | tf_op jit(solution)/shard_map/ppermute | solution.py:411
  56.0 0.0 collective-permute-start.8
  56.0 0.0 collective-permute-done.6.refs_5_
  56.0 0.5 collective-permute-start.14
  56.5 0.2 collective-permute-done.11.refs_5_
  56.7 0.0 collective-permute-start.12
  56.7 0.0 collective-permute-done.4.refs_3_
  56.7 0.5 collective-permute-start.16
  57.2 1.2 %project.2.refs_0_ = f32[64,512]{1,0:T(8,128)S(1)} custom-call(s32[3]{0:T(128)S(1)} %pad_add_fusion.place_ref, bf16[32,1024]{1,0:T(8,128)(2,1)S(1)} %merge_part.1.refs_0_, bf16[32,1024]{1,0:T(8,128)(2,1)S(1)} %collective-permute-done.2.refs_1_, bf16[32,1024]{1,0:T(8,128)(2,1)S(1)} %collective-permute-done.3.refs_2_, ...), custom_call_target="tpu_custom_call" | custom-call | flops 201326592 | tf_op jit(solution)/shard_map/project/pallas_call | solution.py:374
  58.4 0.0 collective-permute-done.10.refs_4_
  58.4 0.0 collective-permute-done.8.refs_2_
  58.4 0.0 collective-permute-done.14.refs_8_
  58.4 0.0 collective-permute-done.12.refs_6_
  58.4 1.4 %project.3.refs_0_ = f32[64,512]{1,0:T(8,128)S(1)} custom-call(s32[3]{0:T(128)S(1)} %pad_add_fusion.place_ref, f32[64,512]{1,0:T(8,128)S(1)} %project.2.refs_0_, bf16[32,1024]{1,0:T(8,128)(2,1)S(1)} %collective-permute-done.7.refs_1_, bf16[32,1024]{1,0:T(8,128)(2,1)S(1)} %collective-permute-done.8.refs_2_, ...), custom_call_target="tpu_custom_call" | custom-call | flops 268435456 | tf_op jit(solution)/shard_map/project/pallas_call | solution.py:374
  59.8 0.0 collective-permute-done.16.refs_2_
  59.8 0.8 %project_last.1 = bf16[16,4,512]{2,1,0:T(4,128)(2,1)S(1)} custom-call(s32[3]{0:T(128)S(1)} %pad_add_fusion.place_ref, f32[64,512]{1,0:T(8,128)S(1)} %project.3.refs_0_, bf16[32,1024]{1,0:T(8,128)(2,1)S(1)} %collective-permute-done.15.refs_1_, bf16[32,1024]{1,0:T(8,128)(2,1)S(1)} %collective-permute-done.16.refs_2_, ...), custom_call_target="tpu_custom_call" | custom-call | flops 67108864 | tf_op jit(solution)/shard_map/project_last/pallas_call | solution.py:374
  60.7 10.6 %all_to_all.11 = bf16[16,4,512]{2,1,0:T(4,128)(2,1)S(1)} all-to-all(bf16[16,4,512]{2,1,0:T(4,128)(2,1)S(1)} %project_last.1), channel_id=1, replica_groups=mesh['groups'=2,'seq'=16] {'seq'}, dimensions={0} | all-to-all | bytes 131072 | tf_op jit(solution)/shard_map/all_to_all | solution.py:462
  71.3 0.7 convert_element_type.13
Async XLA Ops:
  0.0 18.5 %collective-permute-start = (bf16[1,16384,128]{2,1,0:T(8,128)(2,1)}, bf16[1,16384,128]{2,1,0:T(8,128)(2,1)}, u32[]{:S(2)}, u32[]{:S(2)}) collective-permute-start(bf16[1,16384,128]{2,1,0:T(8,128)(2,1)} %k_ref.3), channel_id=1, source_target_pairs={{0,1},{1,0},{2,3},{3,2},{4,5},{5,4},{6,7},{7,6},{8,9},{9,8},{10,11... | collective-permute-start | bytes 12582920 | tf_op jit(solution)/shard_map/ppermute | solution.py:411
  0.0 18.5 %collective-permute-start.1 = (bf16[1,16384,128]{2,1,0:T(8,128)(2,1)}, bf16[1,16384,128]{2,1,0:T(8,128)(2,1)}, u32[]{:S(2)}, u32[]{:S(2)}) collective-permute-start(bf16[1,16384,128]{2,1,0:T(8,128)(2,1)} %v_ref.3), channel_id=1, source_target_pairs={{0,1},{1,0},{2,3},{3,2},{4,5},{5,4},{6,7},{7,6},{8,9},{9,8},{10,11... | collective-permute-start | bytes 12582920 | tf_op jit(solution)/shard_map/ppermute | solution.py:411
  30.4 17.9 %collective-permute-start.9 = (bf16[32,1024]{1,0:T(8,128)(2,1)S(1)}, bf16[32,1024]{1,0:T(8,128)(2,1)S(1)}, u32[]{:S(2)}, u32[]{:S(2)}) collective-permute-start(bf16[32,1024]{1,0:T(8,128)(2,1)S(1)} %merge_part.1.refs_0_), channel_id=1, source_target_pairs={{0,12},{1,13},{2,14},{3,15},{4,8},{5,9},{6,10},{7,11},{8,4},{9,5},... | collective-permute-start | bytes 196616 | tf_op jit(solution)/shard_map/ppermute | solution.py:411
  46.0 5.2 %collective-permute-start.5 = (bf16[32,1024]{1,0:T(8,128)(2,1)S(1)}, bf16[32,1024]{1,0:T(8,128)(2,1)S(1)}, u32[]{:S(2)}, u32[]{:S(2)}) collective-permute-start(bf16[32,1024]{1,0:T(8,128)(2,1)S(1)} %merge_part.1.refs_0_), channel_id=1, source_target_pairs={{0,8},{1,9},{2,10},{3,11},{4,12},{5,13},{6,14},{7,15},{8,0},{9,1},... | collective-permute-start | bytes 196616 | tf_op jit(solution)/shard_map/ppermute | solution.py:411
  46.0 5.2 %collective-permute-start.7 = (bf16[32,1024]{1,0:T(8,128)(2,1)S(1)}, bf16[32,1024]{1,0:T(8,128)(2,1)S(1)}, u32[]{:S(2)}, u32[]{:S(2)}) collective-permute-start(bf16[32,1024]{1,0:T(8,128)(2,1)S(1)} %merge_part.1.refs_0_), channel_id=1, source_target_pairs={{0,2},{1,3},{2,0},{3,1},{4,6},{5,7},{6,4},{7,5},{8,10},{9,11},{10,... | collective-permute-start | bytes 196616 | tf_op jit(solution)/shard_map/ppermute | solution.py:411
  46.0 5.2 %collective-permute-start.3 = (bf16[32,1024]{1,0:T(8,128)(2,1)S(1)}, bf16[32,1024]{1,0:T(8,128)(2,1)S(1)}, u32[]{:S(2)}, u32[]{:S(2)}) collective-permute-start(bf16[32,1024]{1,0:T(8,128)(2,1)S(1)} %merge_part.1.refs_0_), channel_id=1, source_target_pairs={{0,4},{1,5},{2,6},{3,7},{4,0},{5,1},{6,2},{7,3},{8,12},{9,13},{10,... | collective-permute-start | bytes 196616 | tf_op jit(solution)/shard_map/ppermute | solution.py:411
  46.7 6.6 %collective-permute-start.2 = (bf16[32,1024]{1,0:T(8,128)(2,1)S(1)}, bf16[32,1024]{1,0:T(8,128)(2,1)S(1)}, u32[]{:S(2)}, u32[]{:S(2)}) collective-permute-start(bf16[32,1024]{1,0:T(8,128)(2,1)S(1)} %merge_part.1.refs_0_), channel_id=1, source_target_pairs={{0,1},{1,0},{2,3},{3,2},{4,5},{5,4},{6,7},{7,6},{8,9},{9,8},{10,11... | collective-permute-start | bytes 196616 | tf_op jit(solution)/shard_map/ppermute | solution.py:411
  48.3 5.2 %collective-permute-start.15 = (bf16[32,1024]{1,0:T(8,128)(2,1)S(1)}, bf16[32,1024]{1,0:T(8,128)(2,1)S(1)}, u32[]{:S(2)}, u32[]{:S(2)}) collective-permute-start(bf16[32,1024]{1,0:T(8,128)(2,1)S(1)} %collective-permute-done.9.refs_3_), channel_id=1, source_target_pairs={{0,2},{1,3},{2,0},{3,1},{4,6},{5,7},{6,4},{7,5},{8,10},{9,11},{10,... | collective-permute-start | bytes 196616 | tf_op jit(solution)/shard_map/ppermute | solution.py:411
  51.2 4.8 %collective-permute-start.13 = (bf16[32,1024]{1,0:T(8,128)(2,1)S(1)}, bf16[32,1024]{1,0:T(8,128)(2,1)S(1)}, u32[]{:S(2)}, u32[]{:S(2)}) collective-permute-start(bf16[32,1024]{1,0:T(8,128)(2,1)S(1)} %collective-permute-done.5.refs_4_), channel_id=1, source_target_pairs={{0,2},{1,3},{2,0},{3,1},{4,6},{5,7},{6,4},{7,5},{8,10},{9,11},{10,... | collective-permute-start | bytes 196616 | tf_op jit(solution)/shard_map/ppermute | solution.py:411
  51.2 4.8 %collective-permute-start.6 = (bf16[32,1024]{1,0:T(8,128)(2,1)S(1)}, bf16[32,1024]{1,0:T(8,128)(2,1)S(1)}, u32[]{:S(2)}, u32[]{:S(2)}) collective-permute-start(bf16[32,1024]{1,0:T(8,128)(2,1)S(1)} %collective-permute-done.5.refs_4_), channel_id=1, source_target_pairs={{0,1},{1,0},{2,3},{3,2},{4,5},{5,4},{6,7},{7,6},{8,9},{9,8},{10,11... | collective-permute-start | bytes 196616 | tf_op jit(solution)/shard_map/ppermute | solution.py:411
  51.2 5.5 %collective-permute-start.11 = (bf16[32,1024]{1,0:T(8,128)(2,1)S(1)}, bf16[32,1024]{1,0:T(8,128)(2,1)S(1)}, u32[]{:S(2)}, u32[]{:S(2)}) collective-permute-start(bf16[32,1024]{1,0:T(8,128)(2,1)S(1)} %collective-permute-done.3.refs_2_), channel_id=1, source_target_pairs={{0,2},{1,3},{2,0},{3,1},{4,6},{5,7},{6,4},{7,5},{8,10},{9,11},{10,... | collective-permute-start | bytes 196616 | tf_op jit(solution)/shard_map/ppermute | solution.py:411
  53.3 3.4 %collective-permute-start.4 = (bf16[32,1024]{1,0:T(8,128)(2,1)S(1)}, bf16[32,1024]{1,0:T(8,128)(2,1)S(1)}, u32[]{:S(2)}, u32[]{:S(2)}) collective-permute-start(bf16[32,1024]{1,0:T(8,128)(2,1)S(1)} %collective-permute-done.3.refs_2_), channel_id=1, source_target_pairs={{0,1},{1,0},{2,3},{3,2},{4,5},{5,4},{6,7},{7,6},{8,9},{9,8},{10,11... | collective-permute-start | bytes 196616 | tf_op jit(solution)/shard_map/ppermute | solution.py:411
  53.5 4.9 %collective-permute-start.10 = (bf16[32,1024]{1,0:T(8,128)(2,1)S(1)}, bf16[32,1024]{1,0:T(8,128)(2,1)S(1)}, u32[]{:S(2)}, u32[]{:S(2)}) collective-permute-start(bf16[32,1024]{1,0:T(8,128)(2,1)S(1)} %collective-permute-done.9.refs_3_), channel_id=1, source_target_pairs={{0,1},{1,0},{2,3},{3,2},{4,5},{5,4},{6,7},{7,6},{8,9},{9,8},{10,11... | collective-permute-start | bytes 196616 | tf_op jit(solution)/shard_map/ppermute | solution.py:411
  56.0 2.4 %collective-permute-start.8 = (bf16[32,1024]{1,0:T(8,128)(2,1)S(1)}, bf16[32,1024]{1,0:T(8,128)(2,1)S(1)}, u32[]{:S(2)}, u32[]{:S(2)}) collective-permute-start(bf16[32,1024]{1,0:T(8,128)(2,1)S(1)} %collective-permute-done.7.refs_1_), channel_id=1, source_target_pairs={{0,1},{1,0},{2,3},{3,2},{4,5},{5,4},{6,7},{7,6},{8,9},{9,8},{10,11... | collective-permute-start | bytes 196616 | tf_op jit(solution)/shard_map/ppermute | solution.py:411
  56.0 2.4 %collective-permute-start.14 = (bf16[32,1024]{1,0:T(8,128)(2,1)S(1)}, bf16[32,1024]{1,0:T(8,128)(2,1)S(1)}, u32[]{:S(2)}, u32[]{:S(2)}) collective-permute-start(bf16[32,1024]{1,0:T(8,128)(2,1)S(1)} %collective-permute-done.13.refs_7_), channel_id=1, source_target_pairs={{0,1},{1,0},{2,3},{3,2},{4,5},{5,4},{6,7},{7,6},{8,9},{9,8},{10,11... | collective-permute-start | bytes 196616 | tf_op jit(solution)/shard_map/ppermute | solution.py:411
  56.7 1.7 %collective-permute-start.12 = (bf16[32,1024]{1,0:T(8,128)(2,1)S(1)}, bf16[32,1024]{1,0:T(8,128)(2,1)S(1)}, u32[]{:S(2)}, u32[]{:S(2)}) collective-permute-start(bf16[32,1024]{1,0:T(8,128)(2,1)S(1)} %collective-permute-done.11.refs_5_), channel_id=1, source_target_pairs={{0,1},{1,0},{2,3},{3,2},{4,5},{5,4},{6,7},{7,6},{8,9},{9,8},{10,11... | collective-permute-start | bytes 196616 | tf_op jit(solution)/shard_map/ppermute | solution.py:411
  56.7 3.1 %collective-permute-start.16 = (bf16[32,1024]{1,0:T(8,128)(2,1)S(1)}, bf16[32,1024]{1,0:T(8,128)(2,1)S(1)}, u32[]{:S(2)}, u32[]{:S(2)}) collective-permute-start(bf16[32,1024]{1,0:T(8,128)(2,1)S(1)} %collective-permute-done.15.refs_1_), channel_id=1, source_target_pairs={{0,1},{1,0},{2,3},{3,2},{4,5},{5,4},{6,7},{7,6},{8,9},{9,8},{10,11... | collective-permute-start | bytes 196616 | tf_op jit(solution)/shard_map/ppermute | solution.py:411

commit v9 on v8

--- a/solution.py
+++ b/solution.py
@@ -134,6 +134,33 @@
     )(place, parents, lengths, queries, dkeys, dvals, pkeys, pvals)
 
 
+def stage_told(told_ref, told32, col, wide):
+    chips, draft, _ = told_ref.shape
+    for j in range(chips):
+        part = slice(j * draft, (j + 1) * draft)
+        told32[part, :wide] = told_ref[j, :, pl.ds(WIDE + col, wide)].astype(F32) + told_ref[
+            j, :, pl.ds(2 * WIDE + col, wide)
+        ].astype(F32)
+        told32[part, wide:] = told_ref[j, :, 3 * WIDE :].astype(F32)
+
+
+def merge_heads(out, lse, told32, att_ref, first_head):
+    owned, wide = att_ref.shape
+    stats = told32[:, wide:]
+    lane = lax.broadcasted_iota(jnp.int32, (owned, LANES), 1)
+    for h in range(wide // HD):
+        at = 3 * (first_head + h)
+        mark = (lane >= at) & (lane < at + 3)
+        lse_p = jnp.sum(jnp.where(mark, stats, 0.0), axis=1, keepdims=True)
+        part = slice(h * owned, (h + 1) * owned)
+        lse_a = lse[part]
+        top = jnp.maximum(lse_a, lse_p)
+        scale_a = jnp.exp(lse_a - top)
+        scale_p = jnp.exp(lse_p - top)
+        mixed = scale_a * out[part] + scale_p * told32[:, h * HD : (h + 1) * HD]
+        att_ref[:, h * HD : (h + 1) * HD] = (mixed / (scale_a + scale_p)).astype(BF16)
+
+
 def prefix_kernel(
     place_ref,
     told_ref,
@@ -165,7 +192,7 @@
     @pl.when(step == 0)
     def _():
         for j in range(chips):
-            told32[j * draft : (j + 1) * draft, :] = told_ref[j, :, :WIDE].astype(F32)
+            told32[j * draft : (j + 1) * draft, :WIDE] = told_ref[j, :, :WIDE].astype(F32)
         for h in range(GROUP):
             qs[h * owned : (h + 1) * owned, :] = told32[:, h * HD : (h + 1) * HD].astype(BF16)
         head = lax.dot_general(k_ref[0, :HD, :], qs[...], NT, preferred_element_type=F32)
@@ -221,15 +248,24 @@
     def _():
         total = jnp.sum(denom[0] + denom[1], axis=0, keepdims=True)
         lse = peak[...] * (1.0 / LOG2E) + jnp.log(total)
-        out_ref[:, :HD] = ((acc[0] + acc[1]) / total).T
-        out_ref[:, HD:] = jnp.broadcast_to(lse, (LANES, rows)).T
+        mixed = ((acc[0] + acc[1]) / total).T
+        lse = jnp.broadcast_to(lse, (LANES, rows)).T
+        if out_ref.dtype == BF16:
+            stage_told(told_ref, told32, 0, WIDE)
+            merge_heads(mixed, lse, told32, out_ref, 0)
+        else:
+            out_ref[:, :HD] = mixed
+            out_ref[:, HD:] = lse
         fetch.wait()
 
 
-def prefix_part(place, told, keys, values, twin_keys, twin_values, weight, span):
+def prefix_part(place, told, keys, values, twin_keys, twin_values, weight, span, merged):
     chips, draft, _ = told.shape
     owned = chips * draft
     rows = owned * GROUP
+    shape = jax.ShapeDtypeStruct((rows, HD + LANES), F32)
+    if merged:
+        shape = jax.ShapeDtypeStruct((owned, WIDE), BF16)
     return pl.pallas_call(
         prefix_kernel,
         grid=(keys.shape[1] // span,),
@@ -242,20 +278,20 @@
             pl.BlockSpec((1, span, HD), lambda i: (0, i, 0)),
             pl.BlockSpec(memory_space=pl.ANY),
         ],
-        out_specs=[pl.BlockSpec((rows, HD + LANES), lambda i: (0, 0)), VMEM_SPEC],
+        out_specs=[pl.BlockSpec(shape.shape, lambda i: (0, 0)), VMEM_SPEC],
         out_shape=[
-            jax.ShapeDtypeStruct((rows, HD + LANES), F32),
+            shape,
             pltpu.VMEM(weight.shape, BF16),
         ],
         scratch_shapes=[
-            pltpu.VMEM((owned, WIDE), F32),
+            pltpu.VMEM((owned, WIDE + LANES), F32),
             pltpu.VMEM((rows, HD), BF16),
             pltpu.VMEM((1, rows), F32),
             pltpu.VMEM((2, 8, rows), F32),
             pltpu.VMEM((2, HD, rows), F32),
             pltpu.SemaphoreType.DMA,
         ],
-        compiler_params=pltpu.CompilerParams(vmem_limit_bytes=40 << 20),
+        compiler_params=pltpu.CompilerParams(vmem_limit_bytes=24 << 20),
         cost_estimate=pl.CostEstimate(
             flops=8 * rows * keys.shape[1] * HD,
             transcendentals=2 * rows * keys.shape[1],
@@ -267,8 +303,8 @@
         on_chip(told),
         in_hbm(keys),
         in_hbm(values),
-        in_hbm(twin_keys),
-        in_hbm(twin_values),
+        on_chip(twin_keys),
+        on_chip(twin_values),
         in_hbm(weight),
     )
 
@@ -286,31 +322,10 @@
 
 
 def merge_kernel(place_ref, mine_ref, told_ref, att_ref, told32):
-    chips, draft, _ = told_ref.shape
-    owned = chips * draft
     wide = att_ref.shape[1]
-    heads = wide // HD
-    first_head = place_ref[2] * heads
-    col = pl.multiple_of(first_head * HD, wide)
-    for j in range(chips):
-        part = slice(j * draft, (j + 1) * draft)
-        told32[part, :wide] = told_ref[j, :, pl.ds(WIDE + col, wide)].astype(F32) + told_ref[
-            j, :, pl.ds(2 * WIDE + col, wide)
-        ].astype(F32)
-        told32[part, wide:] = told_ref[j, :, 3 * WIDE :].astype(F32)
-    stats = told32[:, wide:]
-    lane = lax.broadcasted_iota(jnp.int32, (owned, LANES), 1)
-    for h in range(heads):
-        at = 3 * (first_head + h)
-        mark = (lane >= at) & (lane < at + 3)
-        lse_p = jnp.sum(jnp.where(mark, stats, 0.0), axis=1, keepdims=True)
-        part = slice(h * owned, (h + 1) * owned)
-        lse_a = mine_ref[part, HD:]
-        top = jnp.maximum(lse_a, lse_p)
-        scale_a = jnp.exp(lse_a - top)
-        scale_p = jnp.exp(lse_p - top)
-        mixed = scale_a * mine_ref[part, :HD] + scale_p * told32[:, h * HD : (h + 1) * HD]
-        att_ref[:, h * HD : (h + 1) * HD] = (mixed / (scale_a + scale_p)).astype(BF16)
+    first_head = place_ref[2] * (wide // HD)
+    stage_told(told_ref, told32, pl.multiple_of(first_head * HD, wide), wide)
+    merge_heads(mine_ref[:, :HD], mine_ref[:, HD:], told32, att_ref, first_head)
 
 
 def merge_part(place, mine, told):
@@ -428,10 +443,10 @@
         message, "seq", split_axis=0, concat_axis=0, axis_index_groups=members, tiled=True
     )
 
-    span = min(4096, prefix_keys.shape[1])
+    span = min((1 << 20) // (chips * own_rows * GROUP), prefix_keys.shape[1])
     weight = out_weight.reshape(chips, -1, out_weight.shape[1])
     mine, wide = prefix_part(
-        place, told, prefix_keys, prefix_values, twin_keys, twin_values, weight, span
+        place, told, prefix_keys, prefix_values, twin_keys, twin_values, weight, span, sharers == 1
     )
     for level in range(sharers.bit_length() - 2, -1, -1):
         half = mine.shape[0] // 2
@@ -440,7 +455,7 @@
         gone = lax.dynamic_slice_in_dim(mine, (1 - at) * half, half, 0)
         mine = join(kept, from_partner(gone, 2 << level))
 
-    own = {0: merge_part(place, mine, told)}
+    own = {0: mine if sharers == 1 else merge_part(place, mine, told)}
     twin = {}
     far = [2 * k for k in range(1, chips // 2)]
 

time: 72.2 us -> 71.6 us (level)
  no operation moved by 1% of the time
where the time goes in v9:
time: 71.6 us; the launch traced here: 71.3 us
  blocking collectives  24.5 us (34%)
  starting transfers between devices  20.9 us (29%)
  Pallas kernels  18 us (25%)
  waiting for transfers between devices  6.48 us (9%)
  between operations  0.77 us (1%)
  other arithmetic  0.74 us (1%)
    ppermute x17, starting transfers between devices, from_partner(): return lax.ppermute(array, 'seq', [(i, i ^ mask) for i in range(seq)])  20.9 us
    all_to_all x1, blocking collectives, shards(): lax.all_to_all(message, 'seq', split_axis=0, concat_axis=0, axis_index_gr...  13.9 us
    pallas_call x1, Pallas kernels, prefix_part(): pl.pallas_call(prefix_kernel, grid=(keys.shape[1] // span,), in_specs=[SM...  11.2 us
    all_to_all x1, blocking collectives, shards(): lax.all_to_all(pieces, 'seq', split_axis=0, concat_axis=0, tiled=True)  10.6 us
    ppermute x17, waiting for transfers between devices, from_partner(): return lax.ppermute(array, 'seq', [(i, i ^ mask) for i in range(seq)])  6.48 us
    pallas_call x3, Pallas kernels, project(): pl.pallas_call(functools.partial(project_kernel, masks=masks, first=first...  3.42 us
    pallas_call x1, Pallas kernels, private_part(): pl.pallas_call(functools.partial(private_kernel, draft=draft, copies=copi...  3.4 us
  transfers between devices with their start and end apart: 17, of which 4 were waited for; matrix products, arithmetic and copies ran while one was open for 0% of the time, Pallas kernels for 8%

profile of v9, /device:TPU:2, one launch (start us, length us, event | category | flops | bytes accessed | tf_op | source)
XLA Modules:
  0.0 71.3 jit_solution(2949985353122126800)
XLA Ops:
  0.0 0.0 collective-permute-start
  0.0 0.5 collective-permute-start.1
  1.2 0.1 pad_add_fusion.place_ref
  1.2 3.4 %private_part.1 = bf16[8,4,3200]{2,1,0:T(4,128)(2,1)S(1)} custom-call(s32[3]{0:T(128)S(1)} %pad_add_fusion.place_ref, s32[4]{0:T(128)} %par_ref.1, s32[1]{0:T(128)S(6)} %copy.11.len_ref, bf16[4,8192]{1,0:T(4,128)(2,1)} %q_ref.1, bf16[4,1024]{1,0:T(4,128)(2,1)} %dk_ref.1, bf16[4,1024]{1,0:T(4,128)(2,1)} %dv_ref.1, bf16[1,1024,1024]{2,1,0:T(8,128)(2,1)} %k_ref.2, ...), custom_call_target="tpu_custom_call" | custom-call | flops 134217728 | bytes 4194304 | tf_op jit(solution)/shard_map/private_part/pallas_call | solution.py:112
  4.7 13.9 %all_to_all.10.told_ref = bf16[8,4,3200]{2,1,0:T(4,128)(2,1)S(1)} all-to-all(bf16[8,4,3200]{2,1,0:T(4,128)(2,1)S(1)} %private_part.1), channel_id=1, replica_groups={{0,2,4,6,8,10,12,14},{1,3,5,7,9,11,13,15},{16,18,20,22,24,26,28,30},{17..., dimensions={0} | all-to-all | bytes 409600 | tf_op jit(solution)/shard_map/all_to_all | solution.py:442
  18.5 0.0 collective-permute-done.twin_k_ref
  18.5 0.0 collective-permute-done.1.twin_v_ref
  18.5 11.2 %prefix_part.1 = (bf16[32,1024]{1,0:T(8,128)(2,1)S(1)}, bf16[8,1024,512]{2,1,0:T(8,128)(2,1)S(1)}) custom-call(s32[3]{0:T(128)S(1)} %pad_add_fusion.place_ref, bf16[8,4,3200]{2,1,0:T(4,128)(2,1)S(1)} %all_to_all.10.told_ref, bf16[1,16384,128]{2,1,0:T(8,128)(2,1)} %k_ref.3, bf16[1,16384,128]{2,1,0:T(8,128)(2,1)} %v_ref.3, ...), custom_call_target="tpu_custom_call" | custom-call | flops 4294967296 | bytes 8388608 | tf_op jit(solution)/shard_map/prefix_part/pallas_call | solution.py:269
  29.7 15.7 %collective-permute-start.9 = (bf16[32,1024]{1,0:T(8,128)(2,1)S(1)}, bf16[32,1024]{1,0:T(8,128)(2,1)S(1)}, u32[]{:S(2)}, u32[]{:S(2)}) collective-permute-start(bf16[32,1024]{1,0:T(8,128)(2,1)S(1)} %get-tuple-element.7.refs_0_), channel_id=1, source_target_pairs={{0,12},{1,13},{2,14},{3,15},{4,8},{5,9},{6,10},{7,11},{8,4},{9,5},... | collective-permute-start | bytes 196616 | tf_op jit(solution)/shard_map/ppermute | solution.py:426
  45.4 0.0 collective-permute-start.5
  45.4 0.0 collective-permute-start.7
  45.4 0.6 collective-permute-start.3
  46.1 0.0 collective-permute-start.2
  46.1 1.6 %collective-permute-done.9.refs_3_ = bf16[32,1024]{1,0:T(8,128)(2,1)S(1)} collective-permute-done((bf16[32,1024]{1,0:T(8,128)(2,1)S(1)}, bf16[32,1024]{1,0:T(8,128)(2,1)S(1)}, u32[]{:S(2)}, u32[]{:S(2)}) %collective-permute-start.9) | collective-permute-done | bytes 65568 | tf_op jit(solution)/shard_map/ppermute | solution.py:426
  47.7 0.4 collective-permute-start.15
  48.1 2.5 %collective-permute-done.5.refs_4_ = bf16[32,1024]{1,0:T(8,128)(2,1)S(1)} collective-permute-done((bf16[32,1024]{1,0:T(8,128)(2,1)S(1)}, bf16[32,1024]{1,0:T(8,128)(2,1)S(1)}, u32[]{:S(2)}, u32[]{:S(2)}) %collective-permute-start.5) | collective-permute-done | bytes 65568 | tf_op jit(solution)/shard_map/ppermute | solution.py:426
  50.6 0.0 collective-permute-start.13
  50.6 0.0 collective-permute-done.7.refs_1_
  50.6 0.0 collective-permute-start.6
  50.6 0.0 collective-permute-done.3.refs_2_
  50.6 2.1 %collective-permute-start.11 = (bf16[32,1024]{1,0:T(8,128)(2,1)S(1)}, bf16[32,1024]{1,0:T(8,128)(2,1)S(1)}, u32[]{:S(2)}, u32[]{:S(2)}) collective-permute-start(bf16[32,1024]{1,0:T(8,128)(2,1)S(1)} %collective-permute-done.3.refs_2_), channel_id=1, source_target_pairs={{0,2},{1,3},{2,0},{3,1},{4,6},{5,7},{6,4},{7,5},{8,10},{9,11},{10,... | collective-permute-start | bytes 196616 | tf_op jit(solution)/shard_map/ppermute | solution.py:426
  52.7 0.0 collective-permute-done.2.refs_1_
  52.7 0.2 collective-permute-start.4
  52.9 0.0 collective-permute-done.15.refs_1_
  52.9 0.3 collective-permute-start.10
  53.2 2.2 %collective-permute-done.13.refs_7_ = bf16[32,1024]{1,0:T(8,128)(2,1)S(1)} collective-permute-done((bf16[32,1024]{1,0:T(8,128)(2,1)S(1)}, bf16[32,1024]{1,0:T(8,128)(2,1)S(1)}, u32[]{:S(2)}, u32[]{:S(2)}) %collective-permute-start.13) | collective-permute-done | bytes 65568 | tf_op jit(solution)/shard_map/ppermute | solution.py:426
  55.4 0.0 collective-permute-start.8
  55.4 0.0 collective-permute-done.6.refs_5_
  55.4 0.5 collective-permute-start.14
  55.9 0.2 collective-permute-done.11.refs_5_
  56.1 0.0 collective-permute-start.12
  56.1 0.0 collective-permute-done.4.refs_3_
  56.1 0.5 collective-permute-start.16
  56.6 1.2 %project.2.refs_0_ = f32[64,512]{1,0:T(8,128)S(1)} custom-call(s32[3]{0:T(128)S(1)} %pad_add_fusion.place_ref, bf16[32,1024]{1,0:T(8,128)(2,1)S(1)} %get-tuple-element.7.refs_0_, bf16[32,1024]{1,0:T(8,128)(2,1)S(1)} %collective-permute-done.2.refs_1_, bf16[32,1024]{1,0:T(8,128)(2,1)S(1)} %collective-permute-done.3.refs_2_, ...), custom_call_target="tpu_custom_call" | custom-call | flops 201326592 | tf_op jit(solution)/shard_map/project/pallas_call | solution.py:389
  57.8 0.0 collective-permute-done.10.refs_4_
  57.8 0.0 collective-permute-done.8.refs_2_
  57.8 0.0 collective-permute-done.14.refs_8_
  57.8 0.0 collective-permute-done.12.refs_6_
  57.8 1.4 %project.3.refs_0_ = f32[64,512]{1,0:T(8,128)S(1)} custom-call(s32[3]{0:T(128)S(1)} %pad_add_fusion.place_ref, f32[64,512]{1,0:T(8,128)S(1)} %project.2.refs_0_, bf16[32,1024]{1,0:T(8,128)(2,1)S(1)} %collective-permute-done.7.refs_1_, bf16[32,1024]{1,0:T(8,128)(2,1)S(1)} %collective-permute-done.8.refs_2_, ...), custom_call_target="tpu_custom_call" | custom-call | flops 268435456 | tf_op jit(solution)/shard_map/project/pallas_call | solution.py:389
  59.2 0.0 collective-permute-done.16.refs_2_
  59.2 0.8 %project_last.1 = bf16[16,4,512]{2,1,0:T(4,128)(2,1)S(1)} custom-call(s32[3]{0:T(128)S(1)} %pad_add_fusion.place_ref, f32[64,512]{1,0:T(8,128)S(1)} %project.3.refs_0_, bf16[32,1024]{1,0:T(8,128)(2,1)S(1)} %collective-permute-done.15.refs_1_, bf16[32,1024]{1,0:T(8,128)(2,1)S(1)} %collective-permute-done.16.refs_2_, ...), custom_call_target="tpu_custom_call" | custom-call | flops 67108864 | tf_op jit(solution)/shard_map/project_last/pallas_call | solution.py:389
  60.1 10.6 %all_to_all.11 = bf16[16,4,512]{2,1,0:T(4,128)(2,1)S(1)} all-to-all(bf16[16,4,512]{2,1,0:T(4,128)(2,1)S(1)} %project_last.1), channel_id=1, replica_groups=mesh['groups'=2,'seq'=16] {'seq'}, dimensions={0} | all-to-all | bytes 131072 | tf_op jit(solution)/shard_map/all_to_all | solution.py:477
  70.7 0.7 convert_element_type.13
Async XLA Ops:
  0.0 18.5 %collective-permute-start = (bf16[1,16384,128]{2,1,0:T(8,128)(2,1)}, bf16[1,16384,128]{2,1,0:T(8,128)(2,1)}, u32[]{:S(2)}, u32[]{:S(2)}) collective-permute-start(bf16[1,16384,128]{2,1,0:T(8,128)(2,1)} %k_ref.3), channel_id=1, source_target_pairs={{0,1},{1,0},{2,3},{3,2},{4,5},{5,4},{6,7},{7,6},{8,9},{9,8},{10,11... | collective-permute-start | bytes 12582920 | tf_op jit(solution)/shard_map/ppermute | solution.py:426
  0.0 18.5 %collective-permute-start.1 = (bf16[1,16384,128]{2,1,0:T(8,128)(2,1)}, bf16[1,16384,128]{2,1,0:T(8,128)(2,1)}, u32[]{:S(2)}, u32[]{:S(2)}) collective-permute-start(bf16[1,16384,128]{2,1,0:T(8,128)(2,1)} %v_ref.3), channel_id=1, source_target_pairs={{0,1},{1,0},{2,3},{3,2},{4,5},{5,4},{6,7},{7,6},{8,9},{9,8},{10,11... | collective-permute-start | bytes 12582920 | tf_op jit(solution)/shard_map/ppermute | solution.py:426
  29.7 17.9 %collective-permute-start.9 = (bf16[32,1024]{1,0:T(8,128)(2,1)S(1)}, bf16[32,1024]{1,0:T(8,128)(2,1)S(1)}, u32[]{:S(2)}, u32[]{:S(2)}) collective-permute-start(bf16[32,1024]{1,0:T(8,128)(2,1)S(1)} %get-tuple-element.7.refs_0_), channel_id=1, source_target_pairs={{0,12},{1,13},{2,14},{3,15},{4,8},{5,9},{6,10},{7,11},{8,4},{9,5},... | collective-permute-start | bytes 196616 | tf_op jit(solution)/shard_map/ppermute | solution.py:426
  45.4 5.2 %collective-permute-start.5 = (bf16[32,1024]{1,0:T(8,128)(2,1)S(1)}, bf16[32,1024]{1,0:T(8,128)(2,1)S(1)}, u32[]{:S(2)}, u32[]{:S(2)}) collective-permute-start(bf16[32,1024]{1,0:T(8,128)(2,1)S(1)} %get-tuple-element.7.refs_0_), channel_id=1, source_target_pairs={{0,8},{1,9},{2,10},{3,11},{4,12},{5,13},{6,14},{7,15},{8,0},{9,1},... | collective-permute-start | bytes 196616 | tf_op jit(solution)/shard_map/ppermute | solution.py:426
  45.4 5.2 %collective-permute-start.7 = (bf16[32,1024]{1,0:T(8,128)(2,1)S(1)}, bf16[32,1024]{1,0:T(8,128)(2,1)S(1)}, u32[]{:S(2)}, u32[]{:S(2)}) collective-permute-start(bf16[32,1024]{1,0:T(8,128)(2,1)S(1)} %get-tuple-element.7.refs_0_), channel_id=1, source_target_pairs={{0,2},{1,3},{2,0},{3,1},{4,6},{5,7},{6,4},{7,5},{8,10},{9,11},{10,... | collective-permute-start | bytes 196616 | tf_op jit(solution)/shard_map/ppermute | solution.py:426
  45.4 5.2 %collective-permute-start.3 = (bf16[32,1024]{1,0:T(8,128)(2,1)S(1)}, bf16[32,1024]{1,0:T(8,128)(2,1)S(1)}, u32[]{:S(2)}, u32[]{:S(2)}) collective-permute-start(bf16[32,1024]{1,0:T(8,128)(2,1)S(1)} %get-tuple-element.7.refs_0_), channel_id=1, source_target_pairs={{0,4},{1,5},{2,6},{3,7},{4,0},{5,1},{6,2},{7,3},{8,12},{9,13},{10,... | collective-permute-start | bytes 196616 | tf_op jit(solution)/shard_map/ppermute | solution.py:426
  46.1 6.6 %collective-permute-start.2 = (bf16[32,1024]{1,0:T(8,128)(2,1)S(1)}, bf16[32,1024]{1,0:T(8,128)(2,1)S(1)}, u32[]{:S(2)}, u32[]{:S(2)}) collective-permute-start(bf16[32,1024]{1,0:T(8,128)(2,1)S(1)} %get-tuple-element.7.refs_0_), channel_id=1, source_target_pairs={{0,1},{1,0},{2,3},{3,2},{4,5},{5,4},{6,7},{7,6},{8,9},{9,8},{10,11... | collective-permute-start | bytes 196616 | tf_op jit(solution)/shard_map/ppermute | solution.py:426
  47.7 5.2 %collective-permute-start.15 = (bf16[32,1024]{1,0:T(8,128)(2,1)S(1)}, bf16[32,1024]{1,0:T(8,128)(2,1)S(1)}, u32[]{:S(2)}, u32[]{:S(2)}) collective-permute-start(bf16[32,1024]{1,0:T(8,128)(2,1)S(1)} %collective-permute-done.9.refs_3_), channel_id=1, source_target_pairs={{0,2},{1,3},{2,0},{3,1},{4,6},{5,7},{6,4},{7,5},{8,10},{9,11},{10,... | collective-permute-start | bytes 196616 | tf_op jit(solution)/shard_map/ppermute | solution.py:426
  50.6 4.8 %collective-permute-start.13 = (bf16[32,1024]{1,0:T(8,128)(2,1)S(1)}, bf16[32,1024]{1,0:T(8,128)(2,1)S(1)}, u32[]{:S(2)}, u32[]{:S(2)}) collective-permute-start(bf16[32,1024]{1,0:T(8,128)(2,1)S(1)} %collective-permute-done.5.refs_4_), channel_id=1, source_target_pairs={{0,2},{1,3},{2,0},{3,1},{4,6},{5,7},{6,4},{7,5},{8,10},{9,11},{10,... | collective-permute-start | bytes 196616 | tf_op jit(solution)/shard_map/ppermute | solution.py:426
  50.6 4.8 %collective-permute-start.6 = (bf16[32,1024]{1,0:T(8,128)(2,1)S(1)}, bf16[32,1024]{1,0:T(8,128)(2,1)S(1)}, u32[]{:S(2)}, u32[]{:S(2)}) collective-permute-start(bf16[32,1024]{1,0:T(8,128)(2,1)S(1)} %collective-permute-done.5.refs_4_), channel_id=1, source_target_pairs={{0,1},{1,0},{2,3},{3,2},{4,5},{5,4},{6,7},{7,6},{8,9},{9,8},{10,11... | collective-permute-start | bytes 196616 | tf_op jit(solution)/shard_map/ppermute | solution.py:426
  50.6 5.5 %collective-permute-start.11 = (bf16[32,1024]{1,0:T(8,128)(2,1)S(1)}, bf16[32,1024]{1,0:T(8,128)(2,1)S(1)}, u32[]{:S(2)}, u32[]{:S(2)}) collective-permute-start(bf16[32,1024]{1,0:T(8,128)(2,1)S(1)} %collective-permute-done.3.refs_2_), channel_id=1, source_target_pairs={{0,2},{1,3},{2,0},{3,1},{4,6},{5,7},{6,4},{7,5},{8,10},{9,11},{10,... | collective-permute-start | bytes 196616 | tf_op jit(solution)/shard_map/ppermute | solution.py:426
  52.7 3.4 %collective-permute-start.4 = (bf16[32,1024]{1,0:T(8,128)(2,1)S(1)}, bf16[32,1024]{1,0:T(8,128)(2,1)S(1)}, u32[]{:S(2)}, u32[]{:S(2)}) collective-permute-start(bf16[32,1024]{1,0:T(8,128)(2,1)S(1)} %collective-permute-done.3.refs_2_), channel_id=1, source_target_pairs={{0,1},{1,0},{2,3},{3,2},{4,5},{5,4},{6,7},{7,6},{8,9},{9,8},{10,11... | collective-permute-start | bytes 196616 | tf_op jit(solution)/shard_map/ppermute | solution.py:426
  52.9 4.9 %collective-permute-start.10 = (bf16[32,1024]{1,0:T(8,128)(2,1)S(1)}, bf16[32,1024]{1,0:T(8,128)(2,1)S(1)}, u32[]{:S(2)}, u32[]{:S(2)}) collective-permute-start(bf16[32,1024]{1,0:T(8,128)(2,1)S(1)} %collective-permute-done.9.refs_3_), channel_id=1, source_target_pairs={{0,1},{1,0},{2,3},{3,2},{4,5},{5,4},{6,7},{7,6},{8,9},{9,8},{10,11... | collective-permute-start | bytes 196616 | tf_op jit(solution)/shard_map/ppermute | solution.py:426
  55.4 2.4 %collective-permute-start.8 = (bf16[32,1024]{1,0:T(8,128)(2,1)S(1)}, bf16[32,1024]{1,0:T(8,128)(2,1)S(1)}, u32[]{:S(2)}, u32[]{:S(2)}) collective-permute-start(bf16[32,1024]{1,0:T(8,128)(2,1)S(1)} %collective-permute-done.7.refs_1_), channel_id=1, source_target_pairs={{0,1},{1,0},{2,3},{3,2},{4,5},{5,4},{6,7},{7,6},{8,9},{9,8},{10,11... | collective-permute-start | bytes 196616 | tf_op jit(solution)/shard_map/ppermute | solution.py:426
  55.4 2.4 %collective-permute-start.14 = (bf16[32,1024]{1,0:T(8,128)(2,1)S(1)}, bf16[32,1024]{1,0:T(8,128)(2,1)S(1)}, u32[]{:S(2)}, u32[]{:S(2)}) collective-permute-start(bf16[32,1024]{1,0:T(8,128)(2,1)S(1)} %collective-permute-done.13.refs_7_), channel_id=1, source_target_pairs={{0,1},{1,0},{2,3},{3,2},{4,5},{5,4},{6,7},{7,6},{8,9},{9,8},{10,11... | collective-permute-start | bytes 196616 | tf_op jit(solution)/shard_map/ppermute | solution.py:426
  56.1 1.7 %collective-permute-start.12 = (bf16[32,1024]{1,0:T(8,128)(2,1)S(1)}, bf16[32,1024]{1,0:T(8,128)(2,1)S(1)}, u32[]{:S(2)}, u32[]{:S(2)}) collective-permute-start(bf16[32,1024]{1,0:T(8,128)(2,1)S(1)} %collective-permute-done.11.refs_5_), channel_id=1, source_target_pairs={{0,1},{1,0},{2,3},{3,2},{4,5},{5,4},{6,7},{7,6},{8,9},{9,8},{10,11... | collective-permute-start | bytes 196616 | tf_op jit(solution)/shard_map/ppermute | solution.py:426
  56.1 3.1 %collective-permute-start.16 = (bf16[32,1024]{1,0:T(8,128)(2,1)S(1)}, bf16[32,1024]{1,0:T(8,128)(2,1)S(1)}, u32[]{:S(2)}, u32[]{:S(2)}) collective-permute-start(bf16[32,1024]{1,0:T(8,128)(2,1)S(1)} %collective-permute-done.15.refs_1_), channel_id=1, source_target_pairs={{0,1},{1,0},{2,3},{3,2},{4,5},{5,4},{6,7},{7,6},{8,9},{9,8},{10,11... | collective-permute-start | bytes 196616 | tf_op jit(solution)/shard_map/ppermute | solution.py:426
